TPU v7x, 128 devices: a whole 4x4x4 slice. The times are simulated.
128 devices in a mesh: ad: 32 (over z, y, core), tp: 4 (over x).
Axes of the slice: x: 4, y: 4, z: 4, core: 2. Of those that a mesh axis runs over, the one named last changes fastest.
Arguments:
- hidden: bfloat16 [1024, 8192], P('ad', 'tp'), may hold values from -6 to 6
- queries: bfloat16 [1024, 64, 128], P('ad', 'tp'), may hold values from -170 to 170
- key_cache_rows: bfloat16 [1024, 8, 128, 128], P('ad', 'tp'), may hold values from -6 to 6
- value_cache_rows: bfloat16 [1024, 8, 128, 128], P('ad', 'tp'), may hold values from -6 to 6
- cache_fill_length: int32 [1024], P('ad'), may hold values from 1 to 128, as said below
- adapter_choice_index: int32 [1024], P('ad'), may hold values from 0 to 2047, as said below
- key_value_weight: bfloat16 [8192, 2, 1024], P(None, None, 'tp'), may hold values from -0.0625 to 0.0625
- adapter_down_weight: bfloat16 [2048, 16, 8192], P('ad', None, 'tp'), may hold values from -0.0625 to 0.0625
- adapter_up_weight: bfloat16 [2048, 16, 2, 1024], P('ad', None, None, 'tp'), may hold values from -1.5 to 1.5
Outputs:
- appended_entries: bfloat16 [1024, 2, 8, 128], P('ad', None, 'tp')
- context: bfloat16 [1024, 64, 128], P('ad', 'tp')
Inputs may be any that keep to these rules, and one draw needn't show every extreme that they name: `adapter_choice_index`: adapter a is held by index a // 64 of ad. Among the 32 sequences of one index of ad, at most 4 name adapters of one holder; in every draw one holder receives exactly 4 from every index of ad. `cache_fill_length`: in every block of 32 sequences one has 128.
All inputs are finite; a program needn't handle non-finite values.
Results may differ from a plain program's by a relative error of at most 0.0053.
Values may be sent and summed in bfloat16 or wider, within the bound.
No kernel may reach another device: no remote copies, remote signals or barrier semaphores. Data moves between devices by JAX's collectives and lax.ppermute only.
A program may use at most 128 MiB of HBM per device.

v0:
```python
import jax
import jax.numpy as jnp
from jax import lax
from jax.sharding import PartitionSpec as P

MODEL_WIDTH = 8192
CAP = 4


adapter_scale = 0.5
epsilon = 1e-05


def copy_for_each(array, axis):
    devices = lax.axis_size(axis)
    return lax.all_to_all(
        jnp.broadcast_to(array[None], (devices, *array.shape)), axis, 0, 0, tiled=True
    )


def over_copies(array, axis):
    everything = copy_for_each(array, axis)
    return jnp.sum(everything, axis=0)


def joined_along(parts, dim):
    dims = list(parts.shape[1:])
    dims[dim] *= parts.shape[0]
    return jnp.moveaxis(parts, 0, dim).reshape(dims)


def collect(array, axis, dim):
    return joined_along(copy_for_each(array, axis), dim)


def low_rank(inputs, down_rows, up_rows):
    partial_value = jnp.einsum("sd,srd->sr", inputs, down_rows, preferred_element_type=jnp.float32)
    summed = over_copies(partial_value, "tp")
    latent_state = summed.astype(jnp.bfloat16)
    return adapter_scale * jnp.einsum(
        "tb,tbl->tl", latent_state, up_rows, preferred_element_type=jnp.float32
    )


def on_device(
    hidden,
    queries,
    key_cache_rows,
    value_cache_rows,
    cache_fill_length,
    adapter_choice_index,
    key_value_weight,
    adapter_down_weight,
    adapter_up_weight,
):
    seq_rows = hidden.shape[0]
    slab_width = hidden.shape[1]
    owners = lax.axis_size("ad")
    adapters_local = adapter_down_weight.shape[0]
    rank_columns = adapter_down_weight.shape[1]
    key_value_columns = adapter_up_weight.shape[2] * adapter_up_weight.shape[3]
    cache_slot_count = owners * CAP
    widened = hidden.astype(jnp.float32)
    squares = over_copies(jnp.sum(widened * widened, axis=1, keepdims=True), "tp")
    inverse = lax.rsqrt(squares / MODEL_WIDTH + epsilon)
    normed_slab = (widened * inverse).astype(jnp.bfloat16)
    flat_w = key_value_weight.reshape(key_value_weight.shape[0], key_value_columns)
    plain_projection_rows = jnp.dot(
        collect(normed_slab, "tp", 1), flat_w, preferred_element_type=jnp.float32
    )
    owner_index = adapter_choice_index // adapters_local
    local_index = adapter_choice_index % adapters_local
    same_owner = owner_index[:, None] == owner_index[None, :]
    earlier = jnp.arange(seq_rows)[None, :] < jnp.arange(seq_rows)[:, None]
    slot_place = jnp.sum((same_owner & earlier).astype(jnp.int32), axis=1)
    slot_target = owner_index * CAP + slot_place
    one_hot = jnp.arange(cache_slot_count)[:, None] == slot_target[None, :]
    one_hot_int = one_hot.astype(jnp.int32)
    slot_ids = jnp.sum(one_hot_int * local_index[None, :], axis=1) + adapters_local * (
        1 - jnp.sum(one_hot_int, axis=1)
    )
    slot_rows = jnp.dot(
        one_hot.astype(jnp.bfloat16), normed_slab, preferred_element_type=jnp.float32
    ).astype(jnp.bfloat16)
    rows_in = lax.all_to_all(
        slot_rows.reshape(owners, CAP, slab_width), "ad", split_axis=0, concat_axis=0, tiled=True
    )
    incoming_index = lax.all_to_all(
        slot_ids.reshape(owners, CAP), "ad", split_axis=0, concat_axis=0, tiled=True
    )
    slot_count = rows_in.shape[0] * rows_in.shape[1]
    selected_index = jnp.minimum(incoming_index.reshape(slot_count), adapters_local - 1)
    adapter_correction = low_rank(
        rows_in.reshape(slot_count, slab_width),
        adapter_down_weight[selected_index],
        adapter_up_weight[selected_index].reshape(slot_count, rank_columns, key_value_columns),
    )
    returned_rows = lax.all_to_all(
        adapter_correction.reshape(rows_in.shape[0], rows_in.shape[1], key_value_columns),
        "ad",
        split_axis=0,
        concat_axis=0,
        tiled=True,
    )
    slot_delta = returned_rows.reshape(cache_slot_count, key_value_columns)
    rows_delta = jnp.einsum(
        "ts,te->se", one_hot.astype(jnp.float32), slot_delta, precision=lax.Precision.HIGHEST
    )
    fresh_rows = (plain_projection_rows + rows_delta).astype(jnp.bfloat16)
    head_dim = queries.shape[2]
    kv_here = key_cache_rows.shape[1]
    group_size = queries.shape[1] // kv_here
    newest_view = fresh_rows.reshape(seq_rows, 2, kv_here, head_dim)
    grouped_heads = queries.reshape(seq_rows, kv_here, group_size, head_dim)
    inverse_square_root = head_dim ** (-0.5)
    scores = (
        jnp.einsum(
            "bkgd,bkcd->bkgc", grouped_heads, key_cache_rows, preferred_element_type=jnp.float32
        )
        * inverse_square_root
    )
    self_score = (
        jnp.einsum(
            "rxlw,rxw->rxl", grouped_heads, newest_view[:, 0], preferred_element_type=jnp.float32
        )
        * inverse_square_root
    )
    in_cache = jnp.arange(key_cache_rows.shape[2])[None, :] < cache_fill_length[:, None]
    scores = jnp.where(in_cache[:, None, None, :], scores, jnp.float32(-1e30))
    row_max = jnp.maximum(jnp.max(scores, axis=3), self_score)
    exp_terms = jnp.exp(scores - row_max[..., None])
    own_exp = jnp.exp(self_score - row_max)
    denominator = jnp.sum(exp_terms, axis=3) + own_exp
    weights = (exp_terms / denominator[..., None]).astype(jnp.bfloat16)
    own_weight = (own_exp / denominator).astype(jnp.bfloat16)
    context = jnp.einsum(
        "bkgc,bkcd->bkgd", weights, value_cache_rows, preferred_element_type=jnp.float32
    )
    context = (
        context
        + own_weight.astype(jnp.float32)[..., None]
        * newest_view[:, 1].astype(jnp.float32)[:, :, None, :]
    )
    return (
        newest_view,
        context.astype(jnp.bfloat16).reshape(seq_rows, kv_here * group_size, head_dim),
    )


def solution(mesh):
    placed = (
        P("ad", "tp"),
        P("ad", "tp", None),
        P("ad", "tp", None, None),
        P("ad", "tp", None, None),
        P("ad"),
        P("ad"),
        P(None, None, "tp"),
        P("ad", None, "tp"),
        P("ad", None, None, "tp"),
    )
    return jax.shard_map(
        on_device,
        mesh=mesh,
        in_specs=placed,
        out_specs=(P("ad", None, "tp", None), P("ad", "tp", None)),
        check_vma=False,
    )
```

profile of v0, /device:TPU:1, one launch (start us, length us, event | category | flops | bytes accessed | tf_op | source)
XLA Modules:
  0.0 106.8 jit_solution(11548135359402166512)
XLA Ops:
  0.7 1.2 %fusion.4 = f32[32]{0:T(128)S(1)} fusion(bf16[32,2048]{1,0:T(8,128)(2,1)} %param.9), kind=kLoop, calls=%fused_computation.12 | loop fusion | flops 196576 | bytes 131200 | tf_op jit(solution)/shard_map/reduce_sum | solution.py:64
  1.8 0.6 broadcast_in_dim.14
  2.4 4.8 %all-to-all-start = ((f32[4,32,1]{1,2,0:T(1,128)}), f32[4,32,1]{1,2,0:T(1,128)S(1)}, u32[]{:S(2)}, u32[]{:S(2)}) async-start(f32[4,32,1]{1,2,0:T(1,128)} %broadcast_in_dim.14), calls=%async_computation | async-start | bytes 4096 | tf_op jit(solution)/shard_map/all_to_all | solution.py:16
  7.3 0.7 and_select_fusion
  8.2 0.7 add.60
  9.0 2.4 %all-to-all-done = f32[4,32,1]{1,2,0:T(1,128)S(1)} async-done(((f32[4,32,1]{1,2,0:T(1,128)}), f32[4,32,1]{1,2,0:T(1,128)S(1)}, u32[]{:S(2)}, u32[]{:S(2)}) %all-to-all-start) | async-done | bytes 544 | tf_op jit(solution)/shard_map/all_to_all | solution.py:16
  11.3 10.2 %all-to-all-start.3 = ((s32[32,1,4]{2,1,0:T(1,128)}), s32[32,1,4]{2,1,0:T(1,128)S(1)}, u32[]{:S(2)}, u32[]{:S(2)}) async-start(s32[32,1,4]{2,1,0:T(1,128)} %bitcast.1), calls=%async_computation.3 | async-start | bytes 32768 | tf_op jit(solution)/shard_map/all_to_all | solution.py:88
  21.6 1.0 fusion.5
  22.6 0.4 convolution_convert_fusion
  23.0 1.0 reshape.137
  24.0 4.4 %all-to-all-done.3 = s32[32,1,4]{2,1,0:T(1,128)S(1)} async-done(((s32[32,1,4]{2,1,0:T(1,128)}), s32[32,1,4]{2,1,0:T(1,128)S(1)}, u32[]{:S(2)}, u32[]{:S(2)}) %all-to-all-start.3) | async-done | bytes 544 | tf_op jit(solution)/shard_map/all_to_all | solution.py:88
  28.4 4.2 %all-to-all-start.2 = ((bf16[32,4,2048]{2,1,0:T(4,128)(2,1)}), bf16[32,4,2048]{2,1,0:T(4,128)(2,1)S(1)}, u32[]{:S(2)}, u32[]{:S(2)}) async-start(bf16[32,4,2048]{2,1,0:T(4,128)(2,1)} %reshape.137), calls=%async_computation.2 | async-start | bytes 1048576 | tf_op jit(solution)/shard_map/all_to_all | solution.py:85
  32.9 8.4 %gather_fusion = bf16[128,16,2048]{2,1,0:T(8,128)(2,1)} fusion(bf16[64,16,2048]{2,1,0:T(8,128)(2,1)} %param.16, s32[1024]{0:T(1024)S(1)} %pad_clamp_fusion), kind=kCustom, calls=%fused_computation | custom fusion | bytes 16777728 | tf_op jit(solution)/shard_map/gather | solution.py:95
  41.3 3.0 %all-to-all-done.2 = bf16[32,4,2048]{2,1,0:T(4,128)(2,1)S(1)} async-done(((bf16[32,4,2048]{2,1,0:T(4,128)(2,1)}), bf16[32,4,2048]{2,1,0:T(4,128)(2,1)S(1)}, u32[]{:S(2)}, u32[]{:S(2)}) %all-to-all-start.2) | async-done | bytes 524320 | tf_op jit(solution)/shard_map/all_to_all | solution.py:85
  44.2 0.8 broadcast_in_dim.15
  45.1 3.5 %all-to-all-start.1 = ((bf16[4,32,2048]{2,1,0:T(8,128)(2,1)}), bf16[4,32,2048]{2,1,0:T(8,128)(2,1)S(1)}, u32[]{:S(2)}, u32[]{:S(2)}) async-start(bf16[4,32,2048]{2,1,0:T(8,128)(2,1)} %broadcast_in_dim.15), calls=%async_computation.1 | async-start | bytes 1048576 | tf_op jit(solution)/shard_map/all_to_all | solution.py:16
  48.6 2.0 %reshape.169 = bf16[128,2048,1]{1,2,0:T(2,128)(2,1)} reshape(bf16[32,4,2048]{2,1,0:T(4,128)(2,1)S(1)} %all-to-all-done.2) | data formatting | bytes 1048576 | tf_op jit(solution)/shard_map/reshape | solution.py:94
  50.6 6.7 %fusion.23 = f32[128,1,16]{2,1,0:T(1,128)S(1)} fusion(bf16[128,2048,1]{1,2,0:T(2,128)(2,1)} %reshape.169, bf16[128,16,2048]{2,1,0:T(8,128)(2,1)} %gather_fusion), kind=kOutput, calls=%fused_computation.57 | convolution fusion | flops 8388608 | bytes 8921088 | tf_op jit(solution)/shard_map/sd,srd->sr/dot_general | solution.py:37
  57.4 0.3 all-to-all-done.1
  57.7 0.7 broadcast_in_dim.16
  58.3 3.9 %all-to-all-start.4 = ((f32[4,128,16]{1,2,0:T(8,128)}), f32[4,128,16]{1,2,0:T(8,128)S(1)}, u32[]{:S(2)}, u32[]{:S(2)}) async-start(f32[4,128,16]{1,2,0:T(8,128)} %broadcast_in_dim.16), calls=%async_computation.4 | async-start | bytes 65536 | tf_op jit(solution)/shard_map/all_to_all | solution.py:16
  62.3 1.3 %fusion.21 = (f32[32,2,8]{2,1,0:T(2,128)S(1)}, f32[32,2,8,128]{3,2,1,0:T(8,128)S(1)}) fusion(bf16[32,2,128,128]{3,2,1,0:T(8,128)(2,1)S(1)} %copy-done, bf16[32,16,128]{2,1,0:T(8,128)(2,1)S(1)} %copy-done.4, pred[32,128]{1,0:T(8,128)(4,1)S(1)} %iota_compare_fusion), kind=kOutput, calls=%fused_computation.55 | convolution fusion | flops 16973312 | bytes 2496512 | tf_op jit(solution)/shard_map/bkgd,bkcd->bkgc/dot_general | solution.py:117
  63.6 8.1 %copy.36 = bf16[1024,8,2,256]{3,1,2,0:T(8,128)(2,1)} copy(bf16[1024,8,2,256]{3,2,1,0:T(2,128)(2,1)} %bitcast.58) | data formatting | bytes 16777216
  71.8 7.8 %gather_fusion.1 = bf16[128,16,2,256]{3,2,1,0:T(2,128)(2,1)} fusion(bf16[64,16,2,256]{3,2,1,0:T(2,128)(2,1)S(1)} %copy-done.1, s32[1024]{0:T(1024)S(1)} %pad_clamp_fusion), kind=kCustom, calls=%fused_computation.1 | custom fusion | bytes 4194816 | tf_op jit(solution)/shard_map/gather | solution.py:96
  79.6 4.5 %reshape.139 = bf16[128,16,512]{2,1,0:T(8,128)(2,1)} reshape(bf16[128,16,2,256]{3,2,1,0:T(2,128)(2,1)} %gather_fusion.1) | data formatting | bytes 4194304 | tf_op jit(solution)/shard_map/reshape | solution.py:96
  84.3 2.0 %fusion.24 = f32[128,1,512]{2,1,0:T(1,128)S(1)} fusion(bf16[128,16,1]{1,2,0:T(2,128)(2,1)S(1)} %copy.31, bf16[128,16,512]{2,1,0:T(8,128)(2,1)} %reshape.139), kind=kOutput, calls=%fused_computation.58 | convolution fusion | flops 2097152 | bytes 2363392 | tf_op jit(solution)/shard_map/tb,tbl->tl/dot_general | solution.py:40
  86.3 0.8 reshape.140
  87.1 5.6 %all-to-all-start.5 = ((f32[32,4,512]{2,1,0:T(4,128)}), f32[32,4,512]{2,1,0:T(4,128)S(1)}, u32[]{:S(2)}, u32[]{:S(2)}) async-start(f32[32,4,512]{2,1,0:T(4,128)} %reshape.140), calls=%async_computation.5 | async-start | bytes 524288 | tf_op jit(solution)/shard_map/all_to_all | solution.py:98
  92.7 4.9 %fusion.22 = f32[32,512]{1,0:T(8,128)S(1)} fusion(bf16[32,8192]{1,0:T(8,128)(2,1)S(1)} %bitcast.59, bf16[8192,512]{1,0:T(8,128)(2,1)} %bitcast.57), kind=kOutput, calls=%fused_computation.56 | convolution fusion | flops 268435456 | bytes 8978432 | tf_op jit(solution)/shard_map/dot_general | solution.py:68
  97.6 4.0 %all-to-all-done.5 = f32[32,4,512]{2,1,0:T(4,128)S(1)} async-done(((f32[32,4,512]{2,1,0:T(4,128)}), f32[32,4,512]{2,1,0:T(4,128)S(1)}, u32[]{:S(2)}, u32[]{:S(2)}) %all-to-all-start.5) | async-done | bytes 262176 | tf_op jit(solution)/shard_map/all_to_all | solution.py:98
  102.0 1.1 %fusion.7 = f32[32,2,1,8]{3,2,1,0:T(1,128)S(1)} fusion(bf16[32,16,128]{2,1,0:T(8,128)(2,1)} %param.10, bf16[32,2,128,1]{2,1,0,3:T(2,128)(2,1)S(1)} %get-tuple-element.4), kind=kOutput, calls=%fused_computation.18 | convolution fusion | flops 131072 | bytes 149504 | tf_op jit(solution)/shard_map/rxlw,rxw->rxl/dot_general | solution.py:123
  103.8 3.0 %fusion.2 = bf16[32,16,128]{2,1,0:T(8,128)(2,1)} fusion(bf16[32,2,128,128]{3,2,1,0:T(8,128)(2,1)} %param.12, f32[32,2,8,128]{3,2,1,0:T(8,128)S(1)} %get-tuple-element.11, f32[32,2,128]{2,1,0:T(2,128)S(1)} %get-tuple-element.5, f32[32,2,8]{2,1,0:T(2,128)S(1)} %copy.28, f32[32,2,8]{2,1,0:T(2,128)S(1)} %copy.27, f32[32,2,8]{2,1,0:T(2,128)S(1)} %copy.25), kind=kOutput, calls=%fused_computation.7 | convolution fusion | flops 17170432 | bytes 2529280 | tf_op jit(solution)/shard_map/bkgc,bkcd->bkgd/dot_general | solution.py:136
  (44 shorter events, 2.0 us)
Async XLA Ops:
  0.6 61.6 %copy-start = (bf16[32,2,128,128]{3,2,1,0:T(8,128)(2,1)S(1)}, bf16[32,2,128,128]{3,2,1,0:T(8,128)(2,1)}, u32[]{:S(2)}) copy-start(bf16[32,2,128,128]{3,2,1,0:T(8,128)(2,1)} %param.11) | copy-start | bytes 6291460
  0.6 31.9 %copy-start.6 = (s32[32]{0:T(128)S(1)}, s32[32]{0:T(128)}, u32[]{:S(2)}) copy-start(s32[32]{0:T(128)} %param.13) | copy-start | bytes 388
  2.4 8.9 %all-to-all-start = ((f32[4,32,1]{1,2,0:T(1,128)}), f32[4,32,1]{1,2,0:T(1,128)S(1)}, u32[]{:S(2)}, u32[]{:S(2)}) async-start(f32[4,32,1]{1,2,0:T(1,128)} %broadcast_in_dim.14), calls=%async_computation | async-start | bytes 4096 | tf_op jit(solution)/shard_map/all_to_all | solution.py:16
  11.3 17.1 %all-to-all-start.3 = ((s32[32,1,4]{2,1,0:T(1,128)}), s32[32,1,4]{2,1,0:T(1,128)S(1)}, u32[]{:S(2)}, u32[]{:S(2)}) async-start(s32[32,1,4]{2,1,0:T(1,128)} %bitcast.1), calls=%async_computation.3 | async-start | bytes 32768 | tf_op jit(solution)/shard_map/all_to_all | solution.py:88
  28.4 15.9 %all-to-all-start.2 = ((bf16[32,4,2048]{2,1,0:T(4,128)(2,1)}), bf16[32,4,2048]{2,1,0:T(4,128)(2,1)S(1)}, u32[]{:S(2)}, u32[]{:S(2)}) async-start(bf16[32,4,2048]{2,1,0:T(4,128)(2,1)} %reshape.137), calls=%async_computation.2 | async-start | bytes 1048576 | tf_op jit(solution)/shard_map/all_to_all | solution.py:85
  45.1 12.6 %all-to-all-start.1 = ((bf16[4,32,2048]{2,1,0:T(8,128)(2,1)}), bf16[4,32,2048]{2,1,0:T(8,128)(2,1)S(1)}, u32[]{:S(2)}, u32[]{:S(2)}) async-start(bf16[4,32,2048]{2,1,0:T(8,128)(2,1)} %broadcast_in_dim.15), calls=%async_computation.1 | async-start | bytes 1048576 | tf_op jit(solution)/shard_map/all_to_all | solution.py:16
  50.6 11.7 %copy-start.4 = (bf16[32,16,128]{2,1,0:T(8,128)(2,1)S(1)}, bf16[32,16,128]{2,1,0:T(8,128)(2,1)}, u32[]{:S(2)}) copy-start(bf16[32,16,128]{2,1,0:T(8,128)(2,1)} %param.10) | copy-start | bytes 393220
  57.7 5.9 %copy-start.2 = (bf16[4,32,2048]{2,1,0:T(8,128)(2,1)}, bf16[4,32,2048]{2,1,0:T(8,128)(2,1)S(1)}, u32[]{:S(2)}) copy-start(bf16[4,32,2048]{2,1,0:T(8,128)(2,1)S(1)} %all-to-all-done.1) | copy-start | bytes 1572868
  58.3 25.8 %all-to-all-start.4 = ((f32[4,128,16]{1,2,0:T(8,128)}), f32[4,128,16]{1,2,0:T(8,128)S(1)}, u32[]{:S(2)}, u32[]{:S(2)}) async-start(f32[4,128,16]{1,2,0:T(8,128)} %broadcast_in_dim.16), calls=%async_computation.4 | async-start | bytes 65536 | tf_op jit(solution)/shard_map/all_to_all | solution.py:16
  63.6 8.2 %copy-start.1 = (bf16[64,16,2,256]{3,2,1,0:T(2,128)(2,1)S(1)}, bf16[64,16,2,256]{3,2,1,0:T(2,128)(2,1)}, u32[]{:S(2)}) copy-start(bf16[64,16,2,256]{3,2,1,0:T(2,128)(2,1)} %param.17) | copy-start | bytes 3145732
  79.6 4.5 %copy-start.3 = (bf16[4,32,2048]{2,1,0:T(8,128)(2,1)S(1)}, bf16[4,32,2048]{2,1,0:T(8,128)(2,1)}, u32[]{:S(2)}) copy-start(bf16[4,32,2048]{2,1,0:T(8,128)(2,1)} %copy-done.2) | copy-start | bytes 1572868
  87.1 14.5 %all-to-all-start.5 = ((f32[32,4,512]{2,1,0:T(4,128)}), f32[32,4,512]{2,1,0:T(4,128)S(1)}, u32[]{:S(2)}, u32[]{:S(2)}) async-start(f32[32,4,512]{2,1,0:T(4,128)} %reshape.140), calls=%async_computation.5 | async-start | bytes 524288 | tf_op jit(solution)/shard_map/all_to_all | solution.py:98
  101.9 4.9 %copy-start.5 = (bf16[32,2,2,128]{3,2,1,0:T(2,128)(2,1)}, bf16[32,2,2,128]{3,2,1,0:T(2,128)(2,1)S(1)}, u32[]{:S(2)}) copy-start(bf16[32,2,2,128]{3,2,1,0:T(2,128)(2,1)S(1)} %reshape.142) | copy-start | bytes 98308
where the time goes:
time: 107 us
  local copies, waits for them, and re-layouts  36.4 us (34%)
  starting transfers between devices  32.2 us (30%)
  matrix products  19.7 us (18%)
  waiting for transfers between devices  14 us (13%)
  other arithmetic  3.67 us (3%)
    all_to_all x3, starting transfers between devices, copy_for_each(): lax.all_to_all(jnp.broadcast_to(array[None], (devices, *array.shape)), ax...  12.2 us
    all_to_all x1, starting transfers between devices, on_device(): lax.all_to_all(slot_ids.reshape(owners, CAP), 'ad', split_axis=0, concat_...  10.2 us
    gather x1, local copies, waits for them, and re-layouts, on_device(): adapter_down_weight[selected_index]  8.42 us
    unnamed x15, local copies, waits for them, and re-layouts  8.15 us
    gather x1, local copies, waits for them, and re-layouts, on_device(): adapter_up_weight[selected_index]  7.84 us
    dot_general x1, matrix products, low_rank(): jnp.einsum('sd,srd->sr', inputs, down_rows, preferred_element_type=jnp.fl...  6.74 us
    all_to_all x1, starting transfers between devices, on_device(): lax.all_to_all(adapter_correction.reshape(rows_in.shape[0], rows_in.shape...  5.57 us
    dot_general x1, matrix products, on_device(): jnp.dot(collect(normed_slab, 'tp', 1), flat_w, preferred_element_type=jnp...  4.9 us
  transfers between devices with their start and end apart: 6, of which 5 were waited for; matrix products, arithmetic and copies ran while one was open for 45% of the time, Pallas kernels for 0%

commit v1 on v0

v1 whole, which is shorter than its diff:
```python
import jax
import jax.numpy as jnp
from jax import lax
from jax.experimental import pallas as pl
from jax.experimental.pallas import tpu as pltpu
from jax.sharding import PartitionSpec as P

F32 = jnp.float32
BF16 = jnp.bfloat16
I32 = jnp.int32

MODEL_WIDTH = 8192
SEQ = 32
OWNERS = 32
ADAPTERS = 64
RANK = 16
SLAB = 2048
HALF = SLAB // 2
SLOT_ROWS = OWNERS * 8
KV = 2
GROUP = 8
HEAD = 128
CTX = 128
QROWS = SEQ * KV * GROUP
adapter_scale = 0.5
epsilon = 1e-05
NEG = -1e30

VMEM = pl.BlockSpec(memory_space=pltpu.VMEM)
SMEM = pl.BlockSpec(memory_space=pltpu.SMEM)
HBM = pl.BlockSpec(memory_space=pl.ANY)
NT = (((1,), (1,)), ((), ()))


def iota(shape, dim):
    return lax.broadcasted_iota(I32, shape, dim)


def ones_where(cond):
    return jnp.where(cond, 1.0, 0.0).astype(BF16)


def spread_ids(idx_ref, shape, dim):
    place = iota(shape, dim) & (SEQ - 1)
    out = jnp.zeros(shape, I32)
    for t in range(SEQ):
        out = jnp.where(place == t, idx_ref[t], out)
    return out


def call(kernel, out_shape, in_specs, scratch=(), out_specs=None, limit=48, cost=None):
    return pl.pallas_call(
        kernel,
        out_shape=out_shape,
        in_specs=in_specs,
        out_specs=out_specs if out_specs is not None else jax.tree.map(lambda _: VMEM, out_shape),
        scratch_shapes=list(scratch),
        compiler_params=pltpu.CompilerParams(vmem_limit_bytes=limit << 20),
        cost_estimate=cost,
    )


def slots_kernel(idx_ref, h_ref, out_ref):
    shape = (SEQ, 2 * SEQ)
    along = spread_ids(idx_ref, shape, 1)
    down = spread_ids(idx_ref, shape, 0)
    lane = iota(shape, 1)
    earlier = ((along >> 6) == (down >> 6)) & (iota(shape, 0) < (lane & (SEQ - 1)))
    place = jnp.sum(earlier.astype(I32), axis=0, keepdims=True)
    target = (along[0:1] >> 6) * 8 + place + 4 * (lane[0:1] >> 5)
    hot = ones_where(iota((SLOT_ROWS, 2 * SEQ), 0) == target)
    local = spread_ids(idx_ref, (2 * SEQ, 128), 0) & (ADAPTERS - 1)
    mark = ones_where(iota((2 * SEQ, 128), 1) == 2 * local + (iota((2 * SEQ, 128), 0) >> 5))
    rows = jnp.concatenate([h_ref[:, :HALF], h_ref[:, HALF:]], axis=0)
    out_ref[:, :HALF] = jnp.dot(hot, rows, preferred_element_type=F32).astype(BF16)
    out_ref[:, HALF:] = jnp.dot(hot, mark, preferred_element_type=F32).astype(BF16)


def down_kernel(r_ref, d_ref, t_ref):
    marks = r_ref[:, HALF:]
    pick = ones_where((iota((ADAPTERS, 128), 1) >> 1) == iota((ADAPTERS, 128), 0))
    chosen = lax.dot_general(pick, marks, NT, preferred_element_type=F32)
    rows = r_ref[:, :HALF]
    first = ((iota((256, SLOT_ROWS), 1) >> 2) & 1) == 0
    total = jnp.zeros((RANK, SLOT_ROWS), F32)
    for c in range(4):
        part = slice(256 * c, 256 * (c + 1))
        g0 = lax.dot_general(d_ref[part, :HALF], rows, NT, preferred_element_type=F32)
        g1 = lax.dot_general(d_ref[part, HALF:], rows, NT, preferred_element_type=F32)
        g = jnp.where(first, g0, g1).reshape(16, RANK, SLOT_ROWS)
        total += jnp.sum(g * chosen[16 * c : 16 * (c + 1)][:, None, :], axis=0)
    ahead = pltpu.roll(total, SLOT_ROWS - 4, 1)
    behind = pltpu.roll(total, 4, 1)
    t_ref[...] = total + jnp.where(first[:RANK], ahead, behind)


def mask_kernel(r_ref, m_ref):
    q = iota((128, RANK * 128), 1)
    spread = ones_where(iota((128, RANK * 128), 0) == 2 * (q >> 5) + (q & 1))
    m_ref[...] = jnp.dot(r_ref[:, HALF:], spread, preferred_element_type=F32).astype(BF16)


def up_kernel(x_ref, y_ref, m_ref, u_ref, z_ref):
    latent = (x_ref[...] + y_ref[...]).astype(BF16).astype(F32)
    turned = jnp.transpose(latent).astype(BF16)
    repeat = ones_where(((iota((RANK, 256), 1) >> 1) & (RANK - 1)) == iota((RANK, 256), 0))
    wide = jnp.dot(turned, repeat, preferred_element_type=F32).astype(BF16)
    sums = [jnp.zeros((SLOT_ROWS, HEAD), F32) for _ in range(KV)]
    for k in range(8):
        part = slice(256 * k, 256 * (k + 1))
        left = wide * m_ref[:, part]
        for c in range(KV):
            sums[c] += jnp.dot(left, u_ref[c, part, :], preferred_element_type=F32)
    for c in range(KV):
        z_ref[:, HEAD * c : HEAD * (c + 1)] = sums[c].astype(BF16)


def attend_kernel(len_ref, q_ref, k_ref, v_ref, u_ref, acc_ref, m_ref, l_ref, u2_ref, s_ref, p_ref, sem):
    copies = [
        pltpu.make_async_copy(u_ref.at[:, :, pl.ds(HEAD * c, HEAD)], u2_ref.at[c], sem.at[c])
        for c in range(KV)
    ]
    for copy in copies:
        copy.start()
    scale = HEAD**-0.5
    lane = iota((GROUP, CTX), 1)
    for b in range(SEQ):
        inside = lane < len_ref[b]
        for k in range(KV):
            row = (b * KV + k) * GROUP
            s = lax.dot_general(
                q_ref[row : row + GROUP, :], k_ref[b * KV + k], NT, preferred_element_type=F32
            )
            s_ref[row : row + GROUP, :] = jnp.where(inside, s * scale, NEG)
    for part in range(4):
        rows = slice(QROWS // 4 * part, QROWS // 4 * (part + 1))
        s = s_ref[rows, :]
        m = jnp.max(s, axis=1, keepdims=True)
        p = jnp.exp(s - m)
        m_ref[rows, :] = jnp.broadcast_to(m, p.shape)
        l_ref[rows, :] = jnp.broadcast_to(jnp.sum(p, axis=1, keepdims=True), p.shape)
        p_ref[rows, :] = p.astype(BF16)
    for pair in range(SEQ * KV):
        row = pair * GROUP
        acc_ref[row : row + GROUP, :] = jnp.dot(
            p_ref[row : row + GROUP, :], v_ref[pair], preferred_element_type=F32
        )
    for copy in copies:
        copy.wait()


def base_kernel(tp_ref, h0_ref, h1_ref, h2_ref, h3_ref, w_ref, out_ref, inv_ref, buf, sem):
    me = tp_ref[0]
    depth = 4 * SLAB
    order = (0, 1, 3, 2)
    shards = (h0_ref, h1_ref, h2_ref, h3_ref)
    copies = []
    for s in order:
        start = pl.multiple_of(((me + s) & 3) * depth, depth)
        copy = pltpu.make_async_copy(w_ref.at[pl.ds(start, depth)], buf.at[s], sem.at[s])
        copy.start()
        copies.append(copy)
    lane = iota((SEQ, 512), 1) & 3
    spread = ones_where((iota((128, 512), 1) >> 2) == iota((128, 512), 0))
    total = jnp.zeros((4 * SEQ, HEAD), F32)
    squares = jnp.zeros((SEQ, 128), F32)
    for s, copy in zip(order, copies):
        copy.wait()
        for half in range(2):
            blocks = [shards[s][:, 128 * i : 128 * (i + 1)] for i in range(8 * half, 8 * half + 8)]
            for block in blocks:
                wide = block.astype(F32)
                squares += wide * wide
            wide = jnp.dot(jnp.concatenate(blocks, axis=0), spread, preferred_element_type=F32)
            for i in range(8):
                one = wide[SEQ * i : SEQ * (i + 1)]
                left = jnp.concatenate([jnp.where(lane == n, one, 0.0) for n in range(4)], axis=0)
                start = 512 * (8 * half + i)
                total += jnp.dot(
                    left.astype(BF16), buf[s, start : start + 512, :], preferred_element_type=F32
                )
    out_ref[...] = total
    mean = jnp.sum(squares, axis=1, keepdims=True) / MODEL_WIDTH
    inv_ref[...] = jnp.broadcast_to(lax.rsqrt(mean + epsilon), (SEQ, 128))


def final_kernel(idx_ref, z_ref, base_ref, inv_ref, q_ref, acc_ref, m_ref, l_ref, kv_ref, ctx_ref):
    shape = (2 * SEQ, SEQ)
    along = spread_ids(idx_ref, shape, 1)
    down = spread_ids(idx_ref, shape, 0)
    row = iota(shape, 0)
    earlier = ((along >> 6) == (down >> 6)) & (iota(shape, 1) < (row & (SEQ - 1)))
    place = jnp.sum(earlier.astype(I32), axis=1, keepdims=True)
    target = (down[:, 0:1] >> 6) * 8 + place + 4 * (row[:, 0:1] >> 5)
    hot = ones_where(iota((2 * SEQ, SLOT_ROWS), 1) == target)
    delta = jnp.dot(hot, z_ref[...], preferred_element_type=F32)
    inverse = inv_ref[...]
    fresh = {}
    for j in range(2):
        for c in range(KV):
            plain = base_ref[SEQ * (2 * c + j) : SEQ * (2 * c + j + 1), :]
            extra = delta[SEQ * j : SEQ * (j + 1), HEAD * c : HEAD * (c + 1)]
            fresh[j, c] = ((plain + adapter_scale * extra) * inverse).astype(BF16)
            kv_ref[j, c] = fresh[j, c]
    lift_row = iota((QROWS, 2 * SEQ), 0)
    lift = ones_where(
        iota((QROWS, 2 * SEQ), 1) == ((lift_row >> 3) & 1) * SEQ + (lift_row >> 4)
    )
    new_key = jnp.dot(lift, jnp.concatenate([fresh[0, 0], fresh[0, 1]], axis=0), preferred_element_type=F32)
    new_value = jnp.dot(lift, jnp.concatenate([fresh[1, 0], fresh[1, 1]], axis=0), preferred_element_type=F32)
    own = jnp.sum(q_ref[...].astype(F32) * new_key, axis=1, keepdims=True) * (HEAD**-0.5)
    m = m_ref[...]
    top = jnp.maximum(m, own)
    keep = jnp.exp(m - top)
    own_exp = jnp.exp(own - top)
    denominator = keep * l_ref[...] + own_exp
    own_weight = (own_exp / denominator).astype(BF16).astype(F32)
    ctx_ref[...] = (acc_ref[...] * (keep / denominator) + own_weight * new_value).astype(BF16)


def on_device(
    hidden,
    queries,
    key_cache_rows,
    value_cache_rows,
    cache_fill_length,
    adapter_choice_index,
    key_value_weight,
    adapter_down_weight,
    adapter_up_weight,
):
    shape = jax.ShapeDtypeStruct
    owners = lax.axis_size("ad")
    me = lax.axis_index("tp").astype(I32).reshape(1)
    ring = lax.axis_size("tp")

    slots = call(slots_kernel, shape((SLOT_ROWS, HALF + 128), BF16), [SMEM, VMEM])(
        adapter_choice_index, hidden
    )
    arrived = lax.all_to_all(
        slots.reshape(owners, 8, HALF + 128), "ad", 0, 0, tiled=True
    ).reshape(SLOT_ROWS, HALF + 128)

    others = [
        lax.ppermute(hidden, "tp", [(i, (i - s) % ring) for i in range(ring)]) for s in (1, 2, 3)
    ]
    flat_queries = queries.reshape(QROWS, HEAD)
    partial, top, norm, up_halves = call(
        attend_kernel,
        (
            shape((QROWS, HEAD), F32),
            shape((QROWS, CTX), F32),
            shape((QROWS, CTX), F32),
            shape((KV, ADAPTERS * RANK, 2, HEAD), BF16),
        ),
        [SMEM, VMEM, VMEM, VMEM, HBM],
        scratch=[
            pltpu.VMEM((QROWS, CTX), F32),
            pltpu.VMEM((QROWS, CTX), BF16),
            pltpu.SemaphoreType.DMA((KV,)),
        ],
    )(
        cache_fill_length,
        flat_queries,
        key_cache_rows.reshape(SEQ * KV, CTX, HEAD),
        value_cache_rows.reshape(SEQ * KV, CTX, HEAD),
        adapter_up_weight.reshape(ADAPTERS * RANK, 2, KV * HEAD),
    )

    sums = call(down_kernel, shape((RANK, SLOT_ROWS), F32), [VMEM, VMEM])(
        arrived, adapter_down_weight.reshape(ADAPTERS * RANK, SLAB)
    )
    mask = call(mask_kernel, shape((SLOT_ROWS, RANK * 128), BF16), [VMEM])(arrived)
    sums = sums + lax.ppermute(sums, "tp", [(i, i ^ 1) for i in range(ring)])
    across = lax.ppermute(sums, "tp", [(i, ring - 1 - i) for i in range(ring)])
    corrections = call(up_kernel, shape((SLOT_ROWS, KV * HEAD), BF16), [VMEM] * 4)(
        sums, across, mask, up_halves.reshape(KV, RANK * 128, HEAD)
    )
    returned = lax.all_to_all(
        corrections.reshape(owners, 8, KV * HEAD), "ad", 0, 0, tiled=True
    ).reshape(SLOT_ROWS, KV * HEAD)

    weight_rows = (
        key_value_weight.reshape(MODEL_WIDTH, 2, KV, HEAD)
        .transpose(0, 2, 1, 3)
        .reshape(4 * MODEL_WIDTH, HEAD)
    )
    base, inverse = call(
        base_kernel,
        (shape((4 * SEQ, HEAD), F32), shape((SEQ, 128), F32)),
        [SMEM, VMEM, VMEM, VMEM, VMEM, HBM],
        scratch=[pltpu.VMEM((4, 4 * SLAB, HEAD), BF16), pltpu.SemaphoreType.DMA((4,))],
    )(me, hidden, *others, weight_rows)

    entries, context = call(
        final_kernel,
        (shape((2, KV, SEQ, HEAD), BF16), shape((QROWS, HEAD), BF16)),
        [SMEM] + [VMEM] * 7,
    )(adapter_choice_index, returned, base, inverse, flat_queries, partial, top, norm)
    return (
        entries.transpose(2, 0, 1, 3),
        context.reshape(SEQ, KV * GROUP, HEAD),
    )


def solution(mesh):
    placed = (
        P("ad", "tp"),
        P("ad", "tp", None),
        P("ad", "tp", None, None),
        P("ad", "tp", None, None),
        P("ad"),
        P("ad"),
        P(None, None, "tp"),
        P("ad", None, "tp"),
        P("ad", None, None, "tp"),
    )
    return jax.shard_map(
        on_device,
        mesh=mesh,
        in_specs=placed,
        out_specs=(P("ad", None, "tp", None), P("ad", "tp", None)),
        check_vma=False,
    )
```

time: 107 us -> 57.9 us (0.54)
  local copies, waits for them, and re-layouts: 36.4 us -> 4.49 us
  blocking collectives: 0 us -> 21.7 us
  starting transfers between devices: 32.2 us -> 11.5 us
  matrix products: 19.7 us -> 0 us
  Pallas kernels: 0 us -> 15.7 us
  waiting for transfers between devices: 14 us -> 3.52 us
  other arithmetic: 3.67 us -> 0.01 us
    all_to_all x6 -> x1, starting transfers between devices: 32.2 us -> 6.02 us  [on_device(): lax.all_to_all(corrections.reshape(owners, 8, KV * HEAD), 'ad', 0, 0, til...]
    all_to_all x0 -> x1, blocking collectives: none -> 21.7 us  [on_device(): lax.all_to_all(slots.reshape(owners, 8, HALF + 128), 'ad', 0, 0, tiled=True)]
    dot_general x8 -> x0, matrix products: 19.7 us -> none  [the longest x1 6.74 us: low_rank(): jnp.einsum('sd,srd->sr', inputs, down_rows, preferred_element_type=jnp.fl...]
    gather x2 -> x0, local copies, waits for them, and re-layouts: 16.3 us -> none  [the longest x1 8.42 us: on_device(): adapter_down_weight[selected_index]]
    pallas_call x0 -> x7, Pallas kernels: none -> 15.7 us  [the longest x1 5.56 us: on_device(): call(base_kernel, (shape((4 * SEQ, HEAD), F32), shape((SEQ, 128), F32)),...]
    all_to_all x6 -> x1, waiting for transfers between devices: 14 us -> 2.13 us  [on_device(): lax.all_to_all(corrections.reshape(owners, 8, KV * HEAD), 'ad', 0, 0, til...]
    reshape x7 -> x0, local copies, waits for them, and re-layouts: 8.45 us -> none  [the longest x1 4.48 us: on_device(): adapter_up_weight[selected_index]]
    ppermute x0 -> x5, starting transfers between devices: none -> 5.46 us  [the longest x1 2.48 us: on_device(): across = lax.ppermute(sums, 'tp', [(i, ring - 1 - i) for i in range(ring)])]
  transfers between devices with their start and end apart: 6 -> 6, of which waited for: 5 -> 2; matrix products, arithmetic and copies ran while one was open for 45% -> 0% of each run, Pallas kernels for 0% -> 20%
where the time goes in v1:
time: 57.9 us; the launch traced here: 57.6 us
  blocking collectives  21.7 us (37%)
  Pallas kernels  15.7 us (27%)
  starting transfers between devices  11.5 us (20%)
  local copies, waits for them, and re-layouts  4.49 us (8%)
  waiting for transfers between devices  3.52 us (6%)
  between operations  0.76 us (1%)
    all_to_all x1, blocking collectives, on_device(): lax.all_to_all(slots.reshape(owners, 8, HALF + 128), 'ad', 0, 0, tiled=True)  21.7 us
    all_to_all x1, starting transfers between devices, on_device(): lax.all_to_all(corrections.reshape(owners, 8, KV * HEAD), 'ad', 0, 0, til...  6.02 us
    pallas_call x1, Pallas kernels, on_device(): call(base_kernel, (shape((4 * SEQ, HEAD), F32), shape((SEQ, 128), F32)),...  5.56 us
    unnamed x19, local copies, waits for them, and re-layouts  4.49 us
    pallas_call x1, Pallas kernels, on_device(): call(attend_kernel, (shape((QROWS, HEAD), F32), shape((QROWS, CTX), F32),...  4.09 us
    ppermute x1, starting transfers between devices, on_device(): across = lax.ppermute(sums, 'tp', [(i, ring - 1 - i) for i in range(ring)])  2.48 us
    all_to_all x1, waiting for transfers between devices, on_device(): lax.all_to_all(corrections.reshape(owners, 8, KV * HEAD), 'ad', 0, 0, til...  2.13 us
    pallas_call x1, Pallas kernels, on_device(): call(final_kernel, (shape((2, KV, SEQ, HEAD), BF16), shape((QROWS, HEAD),...  1.79 us
  transfers between devices with their start and end apart: 6, of which 2 were waited for; matrix products, arithmetic and copies ran while one was open for 0% of the time, Pallas kernels for 20%

profile of v1, /device:TPU:1, one launch (start us, length us, event | category | flops | bytes accessed | tf_op | source)
XLA Modules:
  0.0 57.6 jit_solution(14677010117444888753)
XLA Ops:
  0.6 0.0 copy-start.2
  0.6 0.0 copy-start.3
  0.7 1.0 %copy-done.3 = bf16[32,2048]{1,0:T(8,128)(2,1)S(1)} copy-done((bf16[32,2048]{1,0:T(8,128)(2,1)S(1)}, bf16[32,2048]{1,0:T(8,128)(2,1)}, u32[]{:S(2)}) %copy-start.3) | copy-done | bytes 131096
  1.6 0.7 %copy-done.6 = s32[32]{0:T(128)S(1)} copy-done((s32[32]{0:T(128)S(1)}, s32[32]{0:T(128)}, u32[]{:S(2)}) %copy-start.6) | copy-done | bytes 152
  2.3 0.9 %shard_map.104 = bf16[256,1152]{1,0:T(8,128)(2,1)S(1)} custom-call(s32[32]{0:T(128)S(1)} %copy-done.6, bf16[32,2048]{1,0:T(8,128)(2,1)S(1)} %copy-done.3), custom_call_target="tpu_custom_call" | custom-call | tf_op jit(solution)/shard_map/pallas_call | solution.py:237
  3.2 21.7 %all_to_all.10 = bf16[32,8,1152]{2,1,0:T(8,128)(2,1)S(1)} all-to-all(bf16[32,8,1152]{2,1,0:T(8,128)(2,1)S(1)} %bitcast.21), channel_id=1, replica_groups=mesh['ad'=32,'tp'=4] {'ad'}, dimensions={0} | all-to-all | bytes 1179648 | tf_op jit(solution)/shard_map/all_to_all | solution.py:240
  24.8 2.2 %copy-done = bf16[64,16,2048]{2,1,0:T(8,128)(2,1)S(1)} copy-done((bf16[64,16,2048]{2,1,0:T(8,128)(2,1)S(1)}, bf16[64,16,2048]{2,1,0:T(8,128)(2,1)}, u32[]{:S(2)}) %copy-start) | copy-done | bytes 4194328
  27.0 1.4 %shard_map.105 = f32[16,256]{1,0:T(8,128)S(1)} custom-call(bf16[256,1152]{1,0:T(8,128)(2,1)S(1)} %bitcast.18, bf16[1024,2048]{1,0:T(8,128)(2,1)S(1)} %bitcast.20), custom_call_target="tpu_custom_call" | custom-call | tf_op jit(solution)/shard_map/pallas_call | solution.py:270
  28.4 1.2 %collective-permute-start = (f32[16,256]{1,0:T(8,128)S(1)}, f32[16,256]{1,0:T(8,128)S(1)}, u32[]{:S(2)}, u32[]{:S(2)}) collective-permute-start(f32[16,256]{1,0:T(8,128)S(1)} %shard_map.105), channel_id=1, source_target_pairs={{0,1},{1,0},{2,3},{3,2},{4,5},{5,4},{6,7},{7,6},{8,9},{9,8},{10,11... | collective-permute-start | bytes 49160 | tf_op jit(solution)/shard_map/ppermute | solution.py:274
  29.7 1.4 %collective-permute-done = f32[16,256]{1,0:T(8,128)S(1)} collective-permute-done((f32[16,256]{1,0:T(8,128)S(1)}, f32[16,256]{1,0:T(8,128)S(1)}, u32[]{:S(2)}, u32[]{:S(2)}) %collective-permute-start) | collective-permute-done | bytes 16416 | tf_op jit(solution)/shard_map/ppermute | solution.py:274
  31.0 2.5 %collective-permute-start.1 = (f32[16,256]{1,0:T(8,128)S(1)}, f32[16,256]{1,0:T(8,128)S(1)}, u32[]{:S(2)}, u32[]{:S(2)}) collective-permute-start(f32[16,256]{1,0:T(8,128)S(1)} %add.3.x_ref), channel_id=1, source_target_pairs={{0,3},{1,2},{2,1},{3,0},{4,7},{5,6},{6,5},{7,4},{8,11},{9,10},{10,... | collective-permute-start | bytes 49160 | tf_op jit(solution)/shard_map/ppermute | solution.py:275
  33.5 0.0 copy-done.4
  33.5 0.2 collective-permute-start.2
  33.7 1.5 %collective-permute-start.3 = (bf16[32,2048]{1,0:T(8,128)(2,1)S(1)}, bf16[32,2048]{1,0:T(8,128)(2,1)S(1)}, u32[]{:S(2)}, u32[]{:S(2)}) collective-permute-start(bf16[32,2048]{1,0:T(8,128)(2,1)S(1)} %copy-done.4), channel_id=1, source_target_pairs={{0,2},{1,3},{2,0},{3,1},{4,6},{5,7},{6,4},{7,5},{8,10},{9,11},{10,... | collective-permute-start | bytes 393224 | tf_op jit(solution)/shard_map/ppermute | solution.py:245
  35.3 0.0 collective-permute-start.4
  35.3 0.0 copy-done.2
  35.3 0.0 copy-done.5
  35.3 0.0 copy-done.8
  35.3 0.0 copy-done.1
  35.3 4.1 %shard_map.107 = (f32[512,128]{1,0:T(8,128)S(1)}, f32[512,128]{1,0:T(8,128)S(1)}, f32[512,128]{1,0:T(8,128)S(1)}, bf16[2,1024,2,128]{3,2,1,0:T(2,128)(2,1)S(1)}) custom-call(s32[32]{0:T(128)S(1)} %copy-done.8, bf16[512,128]{1,0:T(8,128)(2,1)S(1)} %bitcast.25, bf16[64,128,128]{2,1,0:T(8,128)(2,1)S(1)} %bitcast.22, bf16[64,128,128]{2,1,0:T(8,128)(2,1)} %bitcast.30, ...), custom_call_target="tpu_custom_call" | custom-call | tf_op jit(solution)/shard_map/pallas_call | solution.py:248
  39.4 0.4 shard_map.106.m_ref
  39.8 0.0 collective-permute-done.1.y_ref
  39.8 1.5 %shard_map.108 = bf16[256,256]{1,0:T(8,128)(2,1)} custom-call(f32[16,256]{1,0:T(8,128)S(1)} %add.3.x_ref, f32[16,256]{1,0:T(8,128)S(1)} %collective-permute-done.1.y_ref, bf16[256,2048]{1,0:T(8,128)(2,1)S(1)} %shard_map.106.m_ref, bf16[2,2048,128]{2,1,0:T(8,128)(2,1)S(1)} %bitcast.23), custom_call_target="tpu_custom_call" | custom-call | tf_op jit(solution)/shard_map/pallas_call | solution.py:276
  41.4 6.0 %all-to-all-start.1 = ((bf16[32,8,256]{2,1,0:T(8,128)(2,1)}), bf16[32,8,256]{2,1,0:T(8,128)(2,1)S(1)}, u32[]{:S(2)}, u32[]{:S(2)}) async-start(bf16[32,8,256]{2,1,0:T(8,128)(2,1)} %bitcast.8), calls=%async_computation.1 | async-start | bytes 262144 | tf_op jit(solution)/shard_map/all_to_all | solution.py:279
  47.4 0.0 collective-permute-done.2.h1_ref
  47.4 0.0 collective-permute-done.3.h2_ref
  47.4 0.0 collective-permute-done.4.h3_ref
  47.4 0.0 copy-start.7
  47.4 5.6 %shard_map.109 = (f32[128,128]{1,0:T(8,128)S(1)}, f32[32,128]{1,0:T(8,128)S(1)}) custom-call(s32[1]{0:T(128)} %bitcast.10.tp_ref, bf16[32,2048]{1,0:T(8,128)(2,1)S(1)} %copy-done.4, bf16[32,2048]{1,0:T(8,128)(2,1)S(1)} %collective-permute-done.2.h1_ref, bf16[32,2048]{1,0:T(8,128)(2,1)S(1)} %collective-permute-done.3.h2_ref, ...), custom_call_target="tpu_custom_call" | custom-call | tf_op jit(solution)/shard_map/pallas_call | solution.py:288
  53.0 2.1 %all-to-all-done.1 = bf16[32,8,256]{2,1,0:T(8,128)(2,1)S(1)} async-done(((bf16[32,8,256]{2,1,0:T(8,128)(2,1)}), bf16[32,8,256]{2,1,0:T(8,128)(2,1)S(1)}, u32[]{:S(2)}, u32[]{:S(2)}) %all-to-all-start.1) | async-done | bytes 131104 | tf_op jit(solution)/shard_map/all_to_all | solution.py:279
  55.1 1.8 %shard_map.110 = (bf16[2,2,32,128]{3,2,1,0:T(8,128)(2,1)S(1)}, bf16[512,128]{1,0:T(8,128)(2,1)}) custom-call(s32[32]{0:T(128)S(1)} %copy-done.7, bf16[256,256]{1,0:T(8,128)(2,1)S(1)} %bitcast.27, f32[128,128]{1,0:T(8,128)S(1)} %get-tuple-element.11.base_ref, f32[32,128]{1,0:T(8,128)S(1)} %get-tuple-element.12.inv_ref, bf16[512,128]{1,0:T(8,128)(2,1)S(1)} %bitcast.26, ...), custom_call_target="tpu_custom_call" | custom-call | tf_op jit(solution)/shard_map/pallas_call | solution.py:295
  56.9 0.6 %copy.12 = bf16[32,2,2,128]{3,2,1,0:T(2,128)(2,1)} copy(bf16[32,2,2,128]{3,0,2,1:T(8,128)(2,1)S(1)} %bitcast.28) | data formatting | bytes 65536
  (8 shorter events, 0.0 us)
Async XLA Ops:
  0.6 34.6 %copy-start.2 = (bf16[64,16,2,256]{3,2,1,0:T(2,128)(2,1)S(1)}, bf16[64,16,2,256]{3,2,1,0:T(2,128)(2,1)}, u32[]{:S(2)}) copy-start(bf16[64,16,2,256]{3,2,1,0:T(2,128)(2,1)} %param.17) | copy-start | bytes 3145732
  0.6 1.0 %copy-start.3 = (bf16[32,2048]{1,0:T(8,128)(2,1)S(1)}, bf16[32,2048]{1,0:T(8,128)(2,1)}, u32[]{:S(2)}) copy-start(bf16[32,2048]{1,0:T(8,128)(2,1)} %h0_ref.1) | copy-start | bytes 393220
  1.6 0.7 %copy-start.6 = (s32[32]{0:T(128)S(1)}, s32[32]{0:T(128)}, u32[]{:S(2)}) copy-start(s32[32]{0:T(128)} %idx_ref.3) | copy-start | bytes 388
  2.3 31.2 %copy-start.4 = (bf16[32,2048]{1,0:T(8,128)(2,1)S(1)}, bf16[32,2048]{1,0:T(8,128)(2,1)}, u32[]{:S(2)}) copy-start(bf16[32,2048]{1,0:T(8,128)(2,1)} %h0_ref.1) | copy-start | bytes 393220
  2.3 33.0 %copy-start.5 = (bf16[32,16,128]{2,1,0:T(8,128)(2,1)S(1)}, bf16[32,16,128]{2,1,0:T(8,128)(2,1)}, u32[]{:S(2)}) copy-start(bf16[32,16,128]{2,1,0:T(8,128)(2,1)} %param.10) | copy-start | bytes 393220
  2.3 33.0 %copy-start.8 = (s32[32]{0:T(128)S(1)}, s32[32]{0:T(128)}, u32[]{:S(2)}) copy-start(s32[32]{0:T(128)} %len_ref.1) | copy-start | bytes 388
  24.8 2.2 %copy-start = (bf16[64,16,2048]{2,1,0:T(8,128)(2,1)S(1)}, bf16[64,16,2048]{2,1,0:T(8,128)(2,1)}, u32[]{:S(2)}) copy-start(bf16[64,16,2048]{2,1,0:T(8,128)(2,1)} %param.16) | copy-start | bytes 12582916
  27.0 8.3 %copy-start.1 = (bf16[32,2,128,128]{3,2,1,0:T(8,128)(2,1)S(1)}, bf16[32,2,128,128]{3,2,1,0:T(8,128)(2,1)}, u32[]{:S(2)}) copy-start(bf16[32,2,128,128]{3,2,1,0:T(8,128)(2,1)} %param.11) | copy-start | bytes 6291460
  28.4 2.6 %collective-permute-start = (f32[16,256]{1,0:T(8,128)S(1)}, f32[16,256]{1,0:T(8,128)S(1)}, u32[]{:S(2)}, u32[]{:S(2)}) collective-permute-start(f32[16,256]{1,0:T(8,128)S(1)} %shard_map.105), channel_id=1, source_target_pairs={{0,1},{1,0},{2,3},{3,2},{4,5},{5,4},{6,7},{7,6},{8,9},{9,8},{10,11... | collective-permute-start | bytes 49160 | tf_op jit(solution)/shard_map/ppermute | solution.py:274
  31.0 8.8 %collective-permute-start.1 = (f32[16,256]{1,0:T(8,128)S(1)}, f32[16,256]{1,0:T(8,128)S(1)}, u32[]{:S(2)}, u32[]{:S(2)}) collective-permute-start(f32[16,256]{1,0:T(8,128)S(1)} %add.3.x_ref), channel_id=1, source_target_pairs={{0,3},{1,2},{2,1},{3,0},{4,7},{5,6},{6,5},{7,4},{8,11},{9,10},{10,... | collective-permute-start | bytes 49160 | tf_op jit(solution)/shard_map/ppermute | solution.py:275
  33.5 13.9 %collective-permute-start.2 = (bf16[32,2048]{1,0:T(8,128)(2,1)S(1)}, bf16[32,2048]{1,0:T(8,128)(2,1)S(1)}, u32[]{:S(2)}, u32[]{:S(2)}) collective-permute-start(bf16[32,2048]{1,0:T(8,128)(2,1)S(1)} %copy-done.4), channel_id=1, source_target_pairs={{0,3},{1,0},{2,1},{3,2},{4,7},{5,4},{6,5},{7,6},{8,11},{9,8},{10,9... | collective-permute-start | bytes 393224 | tf_op jit(solution)/shard_map/ppermute | solution.py:245
  33.7 13.7 %collective-permute-start.3 = (bf16[32,2048]{1,0:T(8,128)(2,1)S(1)}, bf16[32,2048]{1,0:T(8,128)(2,1)S(1)}, u32[]{:S(2)}, u32[]{:S(2)}) collective-permute-start(bf16[32,2048]{1,0:T(8,128)(2,1)S(1)} %copy-done.4), channel_id=1, source_target_pairs={{0,2},{1,3},{2,0},{3,1},{4,6},{5,7},{6,4},{7,5},{8,10},{9,11},{10,... | collective-permute-start | bytes 393224 | tf_op jit(solution)/shard_map/ppermute | solution.py:245
  35.3 12.2 %collective-permute-start.4 = (bf16[32,2048]{1,0:T(8,128)(2,1)S(1)}, bf16[32,2048]{1,0:T(8,128)(2,1)S(1)}, u32[]{:S(2)}, u32[]{:S(2)}) collective-permute-start(bf16[32,2048]{1,0:T(8,128)(2,1)S(1)} %copy-done.4), channel_id=1, source_target_pairs={{0,1},{1,2},{2,3},{3,0},{4,5},{5,6},{6,7},{7,4},{8,9},{9,10},{10,1... | collective-permute-start | bytes 393224 | tf_op jit(solution)/shard_map/ppermute | solution.py:245
  41.4 13.8 %all-to-all-start.1 = ((bf16[32,8,256]{2,1,0:T(8,128)(2,1)}), bf16[32,8,256]{2,1,0:T(8,128)(2,1)S(1)}, u32[]{:S(2)}, u32[]{:S(2)}) async-start(bf16[32,8,256]{2,1,0:T(8,128)(2,1)} %bitcast.8), calls=%async_computation.1 | async-start | bytes 262144 | tf_op jit(solution)/shard_map/all_to_all | solution.py:279
  47.4 7.7 %copy-start.7 = (s32[32]{0:T(128)S(1)}, s32[32]{0:T(128)}, u32[]{:S(2)}) copy-start(s32[32]{0:T(128)} %idx_ref.3) | copy-start | bytes 388

commit v2 on v1

v2 whole, which is shorter than its diff:
```python
import jax
import jax.numpy as jnp
from jax import lax
from jax.experimental import pallas as pl
from jax.experimental.pallas import tpu as pltpu
from jax.sharding import PartitionSpec as P

F32 = jnp.float32
BF16 = jnp.bfloat16
I32 = jnp.int32

MODEL_WIDTH = 8192
SEQ = 32
OWNERS = 32
ADAPTERS = 64
RANK = 16
SLAB = 2048
HALF = SLAB // 2
SLOT_ROWS = OWNERS * 8
KV = 2
GROUP = 8
HEAD = 128
CTX = 128
PAIRS = 4
QROWS = SEQ * KV * GROUP
adapter_scale = 0.5
epsilon = 1e-05
NEG = -1e30

VMEM = pl.BlockSpec(memory_space=pltpu.VMEM)
SMEM = pl.BlockSpec(memory_space=pltpu.SMEM)
HBM = pl.BlockSpec(memory_space=pltpu.MemorySpace.HBM)
NT = (((1,), (1,)), ((), ()))


def iota(shape, dim):
    return lax.broadcasted_iota(I32, shape, dim)


def ones_where(cond):
    return jnp.where(cond, 1.0, 0.0).astype(BF16)


def spread_ids(idx_ref, shape, dim):
    place = iota(shape, dim) & (SEQ - 1)
    out = jnp.zeros(shape, I32)
    for t in range(SEQ):
        out = jnp.where(place == t, idx_ref[t], out)
    return out


def call(kernel, out_shape, in_specs, scratch=(), out_specs=None, limit=16, cost=None):
    return pl.pallas_call(
        kernel,
        out_shape=out_shape,
        in_specs=in_specs,
        out_specs=out_specs if out_specs is not None else jax.tree.map(lambda _: VMEM, out_shape),
        scratch_shapes=list(scratch),
        compiler_params=pltpu.CompilerParams(vmem_limit_bytes=limit << 20),
        cost_estimate=cost,
    )


def in_hbm(*arrays):
    return [pltpu.with_memory_space_constraint(a, pltpu.MemorySpace.HBM) for a in arrays]


def slots_kernel(idx_hbm, h_hbm, out_ref, idx_ref, h_ref, sem):
    rows_copy = pltpu.make_async_copy(h_hbm, h_ref, sem.at[0])
    ids_copy = pltpu.make_async_copy(idx_hbm, idx_ref, sem.at[1])
    ids_copy.start()
    rows_copy.start()
    ids_copy.wait()
    shape = (SEQ, 2 * SEQ)
    along = spread_ids(idx_ref, shape, 1)
    down = spread_ids(idx_ref, shape, 0)
    lane = iota(shape, 1)
    earlier = ((along >> 6) == (down >> 6)) & (iota(shape, 0) < (lane & (SEQ - 1)))
    place = jnp.sum(earlier.astype(I32), axis=0, keepdims=True)
    target = (along[0:1] >> 6) * 8 + place + 4 * (lane[0:1] >> 5)
    hot = ones_where(iota((SLOT_ROWS, 2 * SEQ), 0) == target)
    local = spread_ids(idx_ref, (2 * SEQ, 128), 0) & (ADAPTERS - 1)
    mark = ones_where(iota((2 * SEQ, 128), 1) == 2 * local + (iota((2 * SEQ, 128), 0) >> 5))
    out_ref[:, HALF:] = jnp.dot(hot, mark, preferred_element_type=F32).astype(BF16)
    rows_copy.wait()
    rows = jnp.concatenate([h_ref[:, :HALF], h_ref[:, HALF:]], axis=0)
    out_ref[:, :HALF] = jnp.dot(hot, rows, preferred_element_type=F32).astype(BF16)


def down_kernel(r_ref, d0_ref, d_hbm, t_ref, d_ref, sem):
    copies = [
        pltpu.make_async_copy(d_hbm.at[pl.ds(256 * (n + 1), 256)], d_ref.at[n], sem.at[n])
        for n in range(3)
    ]
    for copy in copies:
        copy.start()
    marks = r_ref[:, HALF:]
    pick = ones_where((iota((ADAPTERS, 128), 1) >> 1) == iota((ADAPTERS, 128), 0))
    chosen = lax.dot_general(pick, marks, NT, preferred_element_type=F32)
    rows = r_ref[:, :HALF]
    first = ((iota((256, SLOT_ROWS), 1) >> 2) & 1) == 0
    total = jnp.zeros((RANK, SLOT_ROWS), F32)
    for c in range(4):
        part = d0_ref
        if c:
            copies[c - 1].wait()
            part = d_ref.at[c - 1]
        g0 = lax.dot_general(part[:, :HALF], rows, NT, preferred_element_type=F32)
        g1 = lax.dot_general(part[:, HALF:], rows, NT, preferred_element_type=F32)
        g = jnp.where(first, g0, g1).reshape(16, RANK, SLOT_ROWS)
        total += jnp.sum(g * chosen[16 * c : 16 * (c + 1)][:, None, :], axis=0)
    ahead = pltpu.roll(total, SLOT_ROWS - 4, 1)
    behind = pltpu.roll(total, 4, 1)
    t_ref[...] = total + jnp.where(first[:RANK], ahead, behind)


def mask_kernel(r_ref, m_ref):
    q = iota((128, RANK * 128), 1)
    spread = ones_where(iota((128, RANK * 128), 0) == 2 * (q >> 5) + (q & 1))
    m_ref[...] = jnp.dot(r_ref[:, HALF:], spread, preferred_element_type=F32).astype(BF16)


def up_kernel(a_ref, b_ref, c_ref, d_ref, m_ref, u_ref, z_ref):
    latent = ((a_ref[...] + b_ref[...]) + (c_ref[...] + d_ref[...])).astype(BF16).astype(F32)
    turned = jnp.transpose(latent).astype(BF16)
    repeat = ones_where(((iota((RANK, 256), 1) >> 1) & (RANK - 1)) == iota((RANK, 256), 0))
    wide = jnp.dot(turned, repeat, preferred_element_type=F32).astype(BF16)
    sums = [jnp.zeros((SLOT_ROWS, HEAD), F32) for _ in range(KV)]
    for k in range(8):
        part = slice(256 * k, 256 * (k + 1))
        left = wide * m_ref[:, part]
        for c in range(KV):
            sums[c] += jnp.dot(left, u_ref[c, part, :], preferred_element_type=F32)
    for c in range(KV):
        z_ref[:, HEAD * c : HEAD * (c + 1)] = sums[c].astype(BF16)


def attend_kernel(
    len_hbm, q_hbm, k_hbm, v_hbm, u_ref, d_ref,
    mid_ref, lse_ref, u2_ref, d0_ref,
    len_ref, q_ref, k_ref, v_ref, s_ref, sem, in_sem,
):
    inputs = [
        pltpu.make_async_copy(source, target, in_sem.at[n])
        for n, (source, target) in enumerate(
            ((len_hbm, len_ref), (q_hbm, q_ref), (k_hbm, k_ref), (v_hbm, v_ref))
        )
    ]
    for copy in inputs:
        copy.start()
    copies = [
        pltpu.make_async_copy(u_ref.at[:, :, pl.ds(HEAD * c, HEAD)], u2_ref.at[c], sem.at[c])
        for c in range(KV)
    ]
    copies.append(pltpu.make_async_copy(d_ref.at[pl.ds(0, 256)], d0_ref, sem.at[KV]))
    for copy in copies:
        copy.start()
    scale = HEAD**-0.5
    lane = iota((GROUP, CTX), 1)
    for copy in inputs[:3]:
        copy.wait()
    for g in range(SEQ * KV // PAIRS):
        rows = slice(GROUP * PAIRS * g, GROUP * PAIRS * (g + 1))
        keys = k_ref[PAIRS * g : PAIRS * (g + 1)].reshape(PAIRS * CTX, HEAD)
        s = lax.dot_general(q_ref[rows, :], keys, NT, preferred_element_type=F32) * scale
        for n in range(PAIRS):
            pair = PAIRS * g + n
            own = s[GROUP * n : GROUP * (n + 1), CTX * n : CTX * (n + 1)]
            s_ref[GROUP * pair : GROUP * (pair + 1), :] = jnp.where(
                lane < len_ref[pair // KV], own, NEG
            )
    for part in range(4):
        rows = slice(QROWS // 4 * part, QROWS // 4 * (part + 1))
        s = s_ref[rows, :]
        m = jnp.max(s, axis=1, keepdims=True)
        p = jnp.exp(s - m)
        norm = jnp.broadcast_to(jnp.sum(p, axis=1, keepdims=True), p.shape)
        lse_ref[rows, :] = m + jnp.log(norm)
        s_ref[rows, :] = p / norm
    inputs[3].wait()
    for g in range(SEQ * KV // PAIRS):
        blocks = []
        for n in range(PAIRS):
            pair = PAIRS * g + n
            p = s_ref[GROUP * pair : GROUP * (pair + 1), :]
            zero = jnp.zeros_like(p)
            blocks.append(
                jnp.concatenate([p if k == n else zero for k in range(PAIRS)], axis=1)
            )
        values = v_ref[PAIRS * g : PAIRS * (g + 1)].reshape(PAIRS * CTX, HEAD)
        mid_ref[GROUP * PAIRS * g : GROUP * PAIRS * (g + 1), :] = jnp.dot(
            jnp.concatenate(blocks, axis=0).astype(BF16), values, preferred_element_type=F32
        )
    for copy in copies:
        copy.wait()


def inverse_rms(shards):
    squares = jnp.zeros((SEQ, 128), F32)
    for shard in shards:
        for i in range(SLAB // 128):
            wide = shard[:, 128 * i : 128 * (i + 1)].astype(F32)
            squares += wide * wide
    mean = jnp.sum(squares, axis=1, keepdims=True) / MODEL_WIDTH
    return jnp.broadcast_to(lax.rsqrt(mean + epsilon), (SEQ, 128))


def base_half(steps, tp_ref, shards, inverse, w_ref, buf, left_ref, sem):
    me = tp_ref[0]
    depth = 4 * SLAB
    copies = []
    for n, s in enumerate(steps):
        start = pl.multiple_of(((me + s) & 3) * depth, depth)
        copies.append(pltpu.make_async_copy(w_ref.at[pl.ds(start, depth)], buf.at[n], sem.at[n]))
        copies[n].start()
    inverse = inverse()
    place = iota((SEQ, 512), 1) & 3
    spread = ones_where((iota((128, 512), 1) >> 2) == iota((128, 512), 0))
    total = jnp.zeros((4 * SEQ, HEAD), F32)
    for n, shard in enumerate(shards):
        blocks = [
            (shard[:, 128 * i : 128 * (i + 1)].astype(F32) * inverse).astype(BF16)
            for i in range(SLAB // 128)
        ]
        wide = jnp.dot(jnp.concatenate(blocks, axis=0), spread, preferred_element_type=F32)
        for i in range(SLAB // 128):
            one = wide[SEQ * i : SEQ * (i + 1)]
            for k in range(4):
                left_ref[SEQ * k : SEQ * (k + 1), 512 * i : 512 * (i + 1)] = jnp.where(
                    place == k, one, 0.0
                ).astype(BF16)
        copies[n].wait()
        total += jnp.dot(left_ref[...], buf[n], preferred_element_type=F32)
    return total


def base_first_kernel(tp_ref, h0_ref, h1_ref, h2_ref, h3_ref, w_ref, out_ref, inv_ref, *scratch):
    def inverse():
        inv_ref[...] = inverse_rms((h0_ref, h1_ref, h2_ref, h3_ref))
        return inv_ref[...]

    out_ref[...] = base_half((0, 1), tp_ref, (h0_ref, h1_ref), inverse, w_ref, *scratch)


def base_last_kernel(tp_ref, h2_ref, h3_ref, inv_ref, before_ref, w_ref, out_ref, *scratch):
    out_ref[...] = before_ref[...] + base_half(
        (2, 3), tp_ref, (h2_ref, h3_ref), lambda: inv_ref[...], w_ref, *scratch
    )


def final_kernel(idx_ref, z_ref, base_ref, inv_ref, q_ref, mid_ref, lse_ref, kv_ref, ctx_ref):
    shape = (2 * SEQ, SEQ)
    along = spread_ids(idx_ref, shape, 1)
    down = spread_ids(idx_ref, shape, 0)
    row = iota(shape, 0)
    earlier = ((along >> 6) == (down >> 6)) & (iota(shape, 1) < (row & (SEQ - 1)))
    place = jnp.sum(earlier.astype(I32), axis=1, keepdims=True)
    target = (down[:, 0:1] >> 6) * 8 + place + 4 * (row[:, 0:1] >> 5)
    hot = ones_where(iota((2 * SEQ, SLOT_ROWS), 1) == target)
    delta = jnp.dot(hot, z_ref[...], preferred_element_type=F32)
    inverse = inv_ref[...]
    fresh = {}
    for j in range(2):
        for c in range(KV):
            plain = base_ref[SEQ * (2 * c + j) : SEQ * (2 * c + j + 1), :]
            extra = delta[SEQ * j : SEQ * (j + 1), HEAD * c : HEAD * (c + 1)]
            fresh[j, c] = (plain + adapter_scale * inverse * extra).astype(BF16)
            kv_ref[:, j, c, :] = fresh[j, c]
    lift_row = iota((QROWS, 2 * SEQ), 0)
    lift = ones_where(
        iota((QROWS, 2 * SEQ), 1) == ((lift_row >> 3) & 1) * SEQ + (lift_row >> 4)
    )
    new_key = jnp.dot(lift, jnp.concatenate([fresh[0, 0], fresh[0, 1]], axis=0), preferred_element_type=F32)
    new_value = jnp.dot(lift, jnp.concatenate([fresh[1, 0], fresh[1, 1]], axis=0), preferred_element_type=F32)
    own = jnp.sum(q_ref[...].astype(F32) * new_key, axis=1, keepdims=True) * (HEAD**-0.5)
    gap = own - lse_ref[...]
    small = jnp.exp(-jnp.abs(gap))
    share = jnp.where(gap > 0, 1.0, small) / (1.0 + small)
    own_weight = share.astype(BF16).astype(F32)
    ctx_ref[...] = (mid_ref[...] * (1.0 - share) + own_weight * new_value).astype(BF16)


def on_device(
    hidden,
    queries,
    key_cache_rows,
    value_cache_rows,
    cache_fill_length,
    adapter_choice_index,
    key_value_weight,
    adapter_down_weight,
    adapter_up_weight,
):
    shape = jax.ShapeDtypeStruct
    owners = lax.axis_size("ad")
    ring = lax.axis_size("tp")

    slots = call(
        slots_kernel,
        shape((SLOT_ROWS, HALF + 128), BF16),
        [HBM, HBM],
        scratch=[
            pltpu.SMEM((SEQ,), I32),
            pltpu.VMEM((SEQ, SLAB), BF16),
            pltpu.SemaphoreType.DMA((2,)),
        ],
    )(*in_hbm(adapter_choice_index, hidden))
    slots, rows_here, fill = lax.optimization_barrier((slots, hidden, cache_fill_length))
    arrived = lax.all_to_all(
        slots.reshape(owners, 8, HALF + 128), "ad", 0, 0, tiled=True
    ).reshape(SLOT_ROWS, HALF + 128)

    others = [
        lax.ppermute(rows_here, "tp", [(i, (i - s) % ring) for i in range(ring)]) for s in (1, 2, 3)
    ]
    flat_queries = queries.reshape(QROWS, HEAD)
    middle, level, up_halves, down = call(
        attend_kernel,
        (
            shape((QROWS, HEAD), F32),
            shape((QROWS, CTX), F32),
            pltpu.VMEM((KV, ADAPTERS * RANK, 2, HEAD), BF16),
            pltpu.VMEM((256, SLAB), BF16),
        ),
        [HBM] * 6,
        scratch=[
            pltpu.SMEM((SEQ,), I32),
            pltpu.VMEM((QROWS, HEAD), BF16),
            pltpu.VMEM((SEQ * KV, CTX, HEAD), BF16),
            pltpu.VMEM((SEQ * KV, CTX, HEAD), BF16),
            pltpu.VMEM((QROWS, CTX), F32),
            pltpu.SemaphoreType.DMA((KV + 1,)),
            pltpu.SemaphoreType.DMA((4,)),
        ],
        cost=pl.CostEstimate(flops=1 << 30, transcendentals=1 << 16, bytes_accessed=12 << 20),
    )(
        *in_hbm(
            fill,
            flat_queries,
            key_cache_rows.reshape(SEQ * KV, CTX, HEAD),
            value_cache_rows.reshape(SEQ * KV, CTX, HEAD),
            adapter_up_weight.reshape(ADAPTERS * RANK, 2, KV * HEAD),
            adapter_down_weight.reshape(ADAPTERS * RANK, SLAB),
        )
    )
    arrived, middle, rows_here = lax.optimization_barrier((arrived, middle, rows_here))
    sums = call(
        down_kernel,
        shape((RANK, SLOT_ROWS), F32),
        [VMEM, VMEM, HBM],
        scratch=[pltpu.VMEM((3, 256, SLAB), BF16), pltpu.SemaphoreType.DMA((3,))],
    )(arrived, down, *in_hbm(adapter_down_weight.reshape(ADAPTERS * RANK, SLAB)))
    mask = call(mask_kernel, shape((SLOT_ROWS, RANK * 128), BF16), [VMEM])(arrived)
    shares = [
        lax.ppermute(sums, "tp", [(i, (i + s) % ring) for i in range(ring)]) for s in (1, 3, 2)
    ]
    me = lax.axis_index("tp").astype(I32).reshape(1)
    weight_rows = (
        key_value_weight.reshape(MODEL_WIDTH, 2, KV, HEAD)
        .transpose(0, 2, 1, 3)
        .reshape(4 * MODEL_WIDTH, HEAD)
    )
    half_scratch = [
        pltpu.VMEM((2, 4 * SLAB, HEAD), BF16),
        pltpu.VMEM((4 * SEQ, 4 * SLAB), BF16),
        pltpu.SemaphoreType.DMA((2,)),
    ]
    base, inverse = call(
        base_first_kernel,
        (shape((4 * SEQ, HEAD), F32), shape((SEQ, 128), F32)),
        [SMEM, VMEM, VMEM, VMEM, VMEM, HBM],
        scratch=half_scratch,
    )(me, hidden, *others, *in_hbm(weight_rows))
    shares, base = lax.optimization_barrier((shares, base))
    corrections = call(up_kernel, shape((SLOT_ROWS, KV * HEAD), BF16), [VMEM] * 6)(
        sums, *shares, mask, up_halves.reshape(KV, RANK * 128, HEAD)
    )
    returned = lax.all_to_all(
        corrections.reshape(owners, 8, KV * HEAD), "ad", 0, 0, tiled=True
    ).reshape(SLOT_ROWS, KV * HEAD)

    base = call(
        base_last_kernel,
        shape((4 * SEQ, HEAD), F32),
        [SMEM, VMEM, VMEM, VMEM, VMEM, HBM],
        scratch=half_scratch,
    )(me, *others[1:], inverse, base, *in_hbm(weight_rows))

    entries, context = call(
        final_kernel,
        (shape((SEQ, 2, KV, HEAD), BF16), shape((QROWS, HEAD), BF16)),
        [SMEM] + [VMEM] * 6,
    )(adapter_choice_index, returned, base, inverse, flat_queries, middle, level)
    return (
        entries,
        context.reshape(SEQ, KV * GROUP, HEAD),
    )


def solution(mesh):
    placed = (
        P("ad", "tp"),
        P("ad", "tp", None),
        P("ad", "tp", None, None),
        P("ad", "tp", None, None),
        P("ad"),
        P("ad"),
        P(None, None, "tp"),
        P("ad", None, "tp"),
        P("ad", None, None, "tp"),
    )
    return jax.shard_map(
        on_device,
        mesh=mesh,
        in_specs=placed,
        out_specs=(P("ad", None, "tp", None), P("ad", "tp", None)),
        check_vma=False,
    )
```

time: 57.9 us -> 51.9 us (0.90)
  blocking collectives: 21.7 us -> 0 us
  starting transfers between devices: 11.5 us -> 23.7 us
  waiting for transfers between devices: 3.52 us -> 7.53 us
  local copies, waits for them, and re-layouts: 4.49 us -> 0.72 us
  Pallas kernels: 15.7 us -> 18.9 us
    all_to_all x1 -> x0, blocking collectives: 21.7 us -> none  [on_device(): lax.all_to_all(slots.reshape(owners, 8, HALF + 128), 'ad', 0, 0, tiled=True)]
    all_to_all x0 -> x1, starting transfers between devices: none -> 9.61 us  [on_device(): lax.all_to_all(slots.reshape(owners, 8, HALF + 128), 'ad', 0, 0, tiled=True)]
    pallas_call x5 -> x6, Pallas kernels: 11.1 us -> 15.2 us  [the longest x1 3.54 us: on_device(): call(base_last_kernel, shape((4 * SEQ, HEAD), F32), [SMEM, VMEM, VMEM, VM...]
    unnamed x19 -> x10, local copies, waits for them, and re-layouts: 4.49 us -> 0.72 us
    ppermute x5 -> x6, starting transfers between devices: 5.46 us -> 9.18 us  [the longest x3 4.89 us: on_device(): lax.ppermute(rows_here, 'tp', [(i, (i - s) % ring) for i in range(ring)])]
    all_to_all x0 -> x1, waiting for transfers between devices: none -> 3.35 us  [on_device(): lax.all_to_all(slots.reshape(owners, 8, HALF + 128), 'ad', 0, 0, tiled=True)]
    all_to_all x1, waiting for transfers between devices: 2.13 us -> 4.16 us  [on_device(): lax.all_to_all(corrections.reshape(owners, 8, KV * HEAD), 'ad', 0, 0, til...]
    ppermute x5 -> x6, waiting for transfers between devices: 1.39 us -> 0.02 us  [the longest x3 0.01 us: on_device(): lax.ppermute(rows_here, 'tp', [(i, (i - s) % ring) for i in range(ring)])]
  transfers between devices with their start and end apart: 6 -> 8, of which waited for: 2 -> 2; matrix products, arithmetic and copies ran while one was open for 0% -> 0% of each run, Pallas kernels for 20% -> 26%
where the time goes in v2:
time: 51.9 us; the launch traced here: 51.6 us
  starting transfers between devices  23.7 us (46%)
  Pallas kernels  18.9 us (36%)
  waiting for transfers between devices  7.53 us (15%)
  between operations  0.76 us (1%)
  local copies, waits for them, and re-layouts  0.72 us (1%)
    all_to_all x1, starting transfers between devices, on_device(): lax.all_to_all(slots.reshape(owners, 8, HALF + 128), 'ad', 0, 0, tiled=True)  9.61 us
    all_to_all x1, starting transfers between devices, on_device(): lax.all_to_all(corrections.reshape(owners, 8, KV * HEAD), 'ad', 0, 0, til...  4.95 us
    ppermute x3, starting transfers between devices, on_device(): lax.ppermute(rows_here, 'tp', [(i, (i - s) % ring) for i in range(ring)])  4.89 us
    ppermute x3, starting transfers between devices, on_device(): lax.ppermute(sums, 'tp', [(i, (i + s) % ring) for i in range(ring)])  4.29 us
    all_to_all x1, waiting for transfers between devices, on_device(): lax.all_to_all(corrections.reshape(owners, 8, KV * HEAD), 'ad', 0, 0, til...  4.16 us
    pallas_call x1, Pallas kernels, on_device(): call(base_last_kernel, shape((4 * SEQ, HEAD), F32), [SMEM, VMEM, VMEM, VM...  3.54 us
    pallas_call x1, Pallas kernels, on_device(): call(base_first_kernel, (shape((4 * SEQ, HEAD), F32), shape((SEQ, 128), F...  3.49 us
    all_to_all x1, waiting for transfers between devices, on_device(): lax.all_to_all(slots.reshape(owners, 8, HALF + 128), 'ad', 0, 0, tiled=True)  3.35 us
  transfers between devices with their start and end apart: 8, of which 2 were waited for; matrix products, arithmetic and copies ran while one was open for 0% of the time, Pallas kernels for 26%

profile of v2, /device:TPU:1, one launch (start us, length us, event | category | flops | bytes accessed | tf_op | source)
XLA Modules:
  0.0 51.6 jit_solution(2252875332426961216)
XLA Ops:
  0.6 2.0 %shard_map.104 = bf16[256,1152]{1,0:T(8,128)(2,1)} custom-call(s32[32]{0:T(128)} %idx_ref.1, bf16[32,2048]{1,0:T(8,128)(2,1)} %h0_ref.1), custom_call_target="tpu_custom_call" | custom-call | tf_op jit(solution)/shard_map/pallas_call | solution.py:298
  2.7 9.6 %all-to-all-start = ((bf16[32,8,1152]{2,1,0:T(8,128)(2,1)}), bf16[32,8,1152]{2,1,0:T(8,128)(2,1)S(1)}, u32[]{:S(2)}, u32[]{:S(2)}) async-start(bf16[32,8,1152]{2,1,0:T(8,128)(2,1)} %bitcast), calls=%async_computation | async-start | bytes 1179648 | tf_op jit(solution)/shard_map/all_to_all | solution.py:309
  12.3 1.3 %collective-permute-start.5 = (bf16[32,2048]{1,0:T(8,128)(2,1)}, bf16[32,2048]{1,0:T(8,128)(2,1)S(1)}, u32[]{:S(2)}, u32[]{:S(2)}) collective-permute-start(bf16[32,2048]{1,0:T(8,128)(2,1)} %h0_ref.1), channel_id=1, source_target_pairs={{0,1},{1,2},{2,3},{3,0},{4,5},{5,6},{6,7},{7,4},{8,9},{9,10},{10,1... | collective-permute-start | bytes 393224 | tf_op jit(solution)/shard_map/ppermute | solution.py:314
  13.6 2.4 %collective-permute-start.4 = (bf16[32,2048]{1,0:T(8,128)(2,1)}, bf16[32,2048]{1,0:T(8,128)(2,1)S(1)}, u32[]{:S(2)}, u32[]{:S(2)}) collective-permute-start(bf16[32,2048]{1,0:T(8,128)(2,1)} %h0_ref.1), channel_id=1, source_target_pairs={{0,2},{1,3},{2,0},{3,1},{4,6},{5,7},{6,4},{7,5},{8,10},{9,11},{10,... | collective-permute-start | bytes 393224 | tf_op jit(solution)/shard_map/ppermute | solution.py:314
  16.0 1.2 %collective-permute-start.3 = (bf16[32,2048]{1,0:T(8,128)(2,1)}, bf16[32,2048]{1,0:T(8,128)(2,1)S(1)}, u32[]{:S(2)}, u32[]{:S(2)}) collective-permute-start(bf16[32,2048]{1,0:T(8,128)(2,1)} %h0_ref.1), channel_id=1, source_target_pairs={{0,3},{1,0},{2,1},{3,2},{4,7},{5,4},{6,5},{7,6},{8,11},{9,8},{10,9... | collective-permute-start | bytes 393224 | tf_op jit(solution)/shard_map/ppermute | solution.py:314
  17.2 3.3 %shard_map.105 = (f32[512,128]{1,0:T(8,128)S(1)}, f32[512,128]{1,0:T(8,128)S(1)}, bf16[2,1024,2,128]{3,2,1,0:T(2,128)(2,1)S(1)}, bf16[256,2048]{1,0:T(8,128)(2,1)S(1)}) custom-call(s32[32]{0:T(128)} %len_hbm, bf16[512,128]{1,0:T(8,128)(2,1)} %bitcast.20, bf16[64,128,128]{2,1,0:T(8,128)(2,1)} %bitcast.27, bf16[64,128,128]{2,1,0:T(8,128)(2,1)} %bitcast.28, ...), custom_call_target="tpu_custom_call" | custom-call | flops 1073741824 | bytes 12582912 | tf_op jit(solution)/shard_map/pallas_call | solution.py:317
  20.5 0.0 copy-start.2
  20.5 0.7 %copy-done.2 = f32[512,128]{1,0:T(8,128)} copy-done((f32[512,128]{1,0:T(8,128)}, f32[512,128]{1,0:T(8,128)S(1)}, u32[]{:S(2)}) %copy-start.2) | copy-done | bytes 262168
  21.2 3.4 %all-to-all-done = bf16[32,8,1152]{2,1,0:T(8,128)(2,1)S(1)} async-done(((bf16[32,8,1152]{2,1,0:T(8,128)(2,1)}), bf16[32,8,1152]{2,1,0:T(8,128)(2,1)S(1)}, u32[]{:S(2)}, u32[]{:S(2)}) %all-to-all-start) | async-done | bytes 589856 | tf_op jit(solution)/shard_map/all_to_all | solution.py:309
  24.5 2.8 %shard_map.106.a_ref = f32[16,256]{1,0:T(8,128)S(1)} custom-call(bf16[256,1152]{1,0:T(8,128)(2,1)S(1)} %bitcast.17, bf16[256,2048]{1,0:T(8,128)(2,1)S(1)} %get-tuple-element.24.d0_ref, bf16[1024,2048]{1,0:T(8,128)(2,1)} %bitcast.26), custom_call_target="tpu_custom_call" | custom-call | tf_op jit(solution)/shard_map/pallas_call | solution.py:347
  27.3 2.8 %collective-permute-start.2 = (f32[16,256]{1,0:T(8,128)S(1)}, f32[16,256]{1,0:T(8,128)S(1)}, u32[]{:S(2)}, u32[]{:S(2)}) collective-permute-start(f32[16,256]{1,0:T(8,128)S(1)} %shard_map.106.a_ref), channel_id=1, source_target_pairs={{0,2},{1,3},{2,0},{3,1},{4,6},{5,7},{6,4},{7,5},{8,10},{9,11},{10,... | collective-permute-start | bytes 49160 | tf_op jit(solution)/shard_map/ppermute | solution.py:355
  30.1 0.9 %collective-permute-start.1 = (f32[16,256]{1,0:T(8,128)S(1)}, f32[16,256]{1,0:T(8,128)S(1)}, u32[]{:S(2)}, u32[]{:S(2)}) collective-permute-start(f32[16,256]{1,0:T(8,128)S(1)} %shard_map.106.a_ref), channel_id=1, source_target_pairs={{0,3},{1,0},{2,1},{3,2},{4,7},{5,4},{6,5},{7,6},{8,11},{9,8},{10,9... | collective-permute-start | bytes 49160 | tf_op jit(solution)/shard_map/ppermute | solution.py:355
  31.0 0.0 collective-permute-done.5.h3_ref
  31.0 0.6 %collective-permute-start = (f32[16,256]{1,0:T(8,128)S(1)}, f32[16,256]{1,0:T(8,128)S(1)}, u32[]{:S(2)}, u32[]{:S(2)}) collective-permute-start(f32[16,256]{1,0:T(8,128)S(1)} %shard_map.106.a_ref), channel_id=1, source_target_pairs={{0,1},{1,2},{2,3},{3,0},{4,5},{5,6},{6,7},{7,4},{8,9},{9,10},{10,1... | collective-permute-start | bytes 49160 | tf_op jit(solution)/shard_map/ppermute | solution.py:355
  31.6 0.0 collective-permute-done.4.h2_ref
  31.6 0.0 collective-permute-done.3.h1_ref
  31.6 0.0 copy-done
  31.6 3.5 %shard_map.107 = (f32[128,128]{1,0:T(8,128)S(1)}, f32[32,128]{1,0:T(8,128)S(1)}) custom-call(s32[1]{0:T(128)} %bitcast.7.tp_ref, bf16[32,2048]{1,0:T(8,128)(2,1)S(1)} %copy-done, bf16[32,2048]{1,0:T(8,128)(2,1)S(1)} %collective-permute-done.3.h1_ref, bf16[32,2048]{1,0:T(8,128)(2,1)S(1)} %collective-permute-done.4.h2_ref, ...), custom_call_target="tpu_custom_call" | custom-call | tf_op jit(solution)/shard_map/pallas_call | solution.py:368
  35.1 0.4 shard_map.108.m_ref
  35.6 0.0 collective-permute-done.2.d_ref
  35.6 0.0 collective-permute-done.1.c_ref
  35.6 0.0 collective-permute-done.b_ref
  35.6 1.5 %shard_map.109 = bf16[256,256]{1,0:T(8,128)(2,1)} custom-call(f32[16,256]{1,0:T(8,128)S(1)} %shard_map.106.a_ref, f32[16,256]{1,0:T(8,128)S(1)} %collective-permute-done.b_ref, f32[16,256]{1,0:T(8,128)S(1)} %collective-permute-done.1.c_ref, f32[16,256]{1,0:T(8,128)S(1)} %collective-permute-done.2.d_ref, bf16[256,2048]{1,0:T(8,128)(2,1)S(1)} %shard_map.108.m_ref, ...), custom_call_target="tpu_custom_call" | custom-call | tf_op jit(solution)/shard_map/pallas_call | solution.py:375
  37.1 5.0 %all-to-all-start.1 = ((bf16[32,8,256]{2,1,0:T(8,128)(2,1)}), bf16[32,8,256]{2,1,0:T(8,128)(2,1)S(1)}, u32[]{:S(2)}, u32[]{:S(2)}) async-start(bf16[32,8,256]{2,1,0:T(8,128)(2,1)} %bitcast.12), calls=%async_computation.1 | async-start | bytes 262144 | tf_op jit(solution)/shard_map/all_to_all | solution.py:378
  42.1 0.0 copy-start.1
  42.1 0.0 copy-start.3
  42.1 0.0 copy-start.4
  42.1 3.5 %shard_map.110.base_ref = f32[128,128]{1,0:T(8,128)S(1)} custom-call(s32[1]{0:T(128)} %bitcast.7.tp_ref, bf16[32,2048]{1,0:T(8,128)(2,1)S(1)} %collective-permute-done.4.h2_ref, bf16[32,2048]{1,0:T(8,128)(2,1)S(1)} %collective-permute-done.5.h3_ref, f32[32,128]{1,0:T(8,128)S(1)} %get-tuple-element.30.inv_ref, f32[128,128]{1,0:T(8,128)S(1)} %get-tuple-element.31.before_ref, ...), custom_call_target="tpu_custom_call" | custom-call | tf_op jit(solution)/shard_map/pallas_call | solution.py:382
  45.7 4.2 %all-to-all-done.1 = bf16[32,8,256]{2,1,0:T(8,128)(2,1)S(1)} async-done(((bf16[32,8,256]{2,1,0:T(8,128)(2,1)}), bf16[32,8,256]{2,1,0:T(8,128)(2,1)S(1)}, u32[]{:S(2)}, u32[]{:S(2)}) %all-to-all-start.1) | async-done | bytes 131104 | tf_op jit(solution)/shard_map/all_to_all | solution.py:378
  49.8 0.0 copy-done.1
  49.8 0.0 copy-done.4
  49.8 1.8 %shard_map.111 = (bf16[32,2,2,128]{3,2,1,0:T(2,128)(2,1)}, bf16[512,128]{1,0:T(8,128)(2,1)}) custom-call(s32[32]{0:T(128)S(1)} %copy-done.4, bf16[256,256]{1,0:T(8,128)(2,1)S(1)} %bitcast.22, f32[128,128]{1,0:T(8,128)S(1)} %shard_map.110.base_ref, f32[32,128]{1,0:T(8,128)S(1)} %get-tuple-element.30.inv_ref, bf16[512,128]{1,0:T(8,128)(2,1)S(1)} %bitcast.21, ...), custom_call_target="tpu_custom_call" | custom-call | tf_op jit(solution)/shard_map/pallas_call | solution.py:389
  (2 shorter events, 0.0 us)
Async XLA Ops:
  2.7 21.9 %all-to-all-start = ((bf16[32,8,1152]{2,1,0:T(8,128)(2,1)}), bf16[32,8,1152]{2,1,0:T(8,128)(2,1)S(1)}, u32[]{:S(2)}, u32[]{:S(2)}) async-start(bf16[32,8,1152]{2,1,0:T(8,128)(2,1)} %bitcast), calls=%async_computation | async-start | bytes 1179648 | tf_op jit(solution)/shard_map/all_to_all | solution.py:309
  12.3 18.7 %collective-permute-start.5 = (bf16[32,2048]{1,0:T(8,128)(2,1)}, bf16[32,2048]{1,0:T(8,128)(2,1)S(1)}, u32[]{:S(2)}, u32[]{:S(2)}) collective-permute-start(bf16[32,2048]{1,0:T(8,128)(2,1)} %h0_ref.1), channel_id=1, source_target_pairs={{0,1},{1,2},{2,3},{3,0},{4,5},{5,6},{6,7},{7,4},{8,9},{9,10},{10,1... | collective-permute-start | bytes 393224 | tf_op jit(solution)/shard_map/ppermute | solution.py:314
  13.6 18.0 %collective-permute-start.4 = (bf16[32,2048]{1,0:T(8,128)(2,1)}, bf16[32,2048]{1,0:T(8,128)(2,1)S(1)}, u32[]{:S(2)}, u32[]{:S(2)}) collective-permute-start(bf16[32,2048]{1,0:T(8,128)(2,1)} %h0_ref.1), channel_id=1, source_target_pairs={{0,2},{1,3},{2,0},{3,1},{4,6},{5,7},{6,4},{7,5},{8,10},{9,11},{10,... | collective-permute-start | bytes 393224 | tf_op jit(solution)/shard_map/ppermute | solution.py:314
  16.0 15.6 %collective-permute-start.3 = (bf16[32,2048]{1,0:T(8,128)(2,1)}, bf16[32,2048]{1,0:T(8,128)(2,1)S(1)}, u32[]{:S(2)}, u32[]{:S(2)}) collective-permute-start(bf16[32,2048]{1,0:T(8,128)(2,1)} %h0_ref.1), channel_id=1, source_target_pairs={{0,3},{1,0},{2,1},{3,2},{4,7},{5,4},{6,5},{7,6},{8,11},{9,8},{10,9... | collective-permute-start | bytes 393224 | tf_op jit(solution)/shard_map/ppermute | solution.py:314
  20.5 0.7 %copy-start.2 = (f32[512,128]{1,0:T(8,128)}, f32[512,128]{1,0:T(8,128)S(1)}, u32[]{:S(2)}) copy-start(f32[512,128]{1,0:T(8,128)S(1)} %get-tuple-element.33.lse_ref) | copy-start | bytes 786436
  21.2 10.4 %copy-start = (bf16[32,2048]{1,0:T(8,128)(2,1)S(1)}, bf16[32,2048]{1,0:T(8,128)(2,1)}, u32[]{:S(2)}) copy-start(bf16[32,2048]{1,0:T(8,128)(2,1)} %h0_ref.1) | copy-start | bytes 393220
  27.3 8.2 %collective-permute-start.2 = (f32[16,256]{1,0:T(8,128)S(1)}, f32[16,256]{1,0:T(8,128)S(1)}, u32[]{:S(2)}, u32[]{:S(2)}) collective-permute-start(f32[16,256]{1,0:T(8,128)S(1)} %shard_map.106.a_ref), channel_id=1, source_target_pairs={{0,2},{1,3},{2,0},{3,1},{4,6},{5,7},{6,4},{7,5},{8,10},{9,11},{10,... | collective-permute-start | bytes 49160 | tf_op jit(solution)/shard_map/ppermute | solution.py:355
  30.1 5.4 %collective-permute-start.1 = (f32[16,256]{1,0:T(8,128)S(1)}, f32[16,256]{1,0:T(8,128)S(1)}, u32[]{:S(2)}, u32[]{:S(2)}) collective-permute-start(f32[16,256]{1,0:T(8,128)S(1)} %shard_map.106.a_ref), channel_id=1, source_target_pairs={{0,3},{1,0},{2,1},{3,2},{4,7},{5,4},{6,5},{7,6},{8,11},{9,8},{10,9... | collective-permute-start | bytes 49160 | tf_op jit(solution)/shard_map/ppermute | solution.py:355
  31.0 4.6 %collective-permute-start = (f32[16,256]{1,0:T(8,128)S(1)}, f32[16,256]{1,0:T(8,128)S(1)}, u32[]{:S(2)}, u32[]{:S(2)}) collective-permute-start(f32[16,256]{1,0:T(8,128)S(1)} %shard_map.106.a_ref), channel_id=1, source_target_pairs={{0,1},{1,2},{2,3},{3,0},{4,5},{5,6},{6,7},{7,4},{8,9},{9,10},{10,1... | collective-permute-start | bytes 49160 | tf_op jit(solution)/shard_map/ppermute | solution.py:355
  37.1 12.7 %all-to-all-start.1 = ((bf16[32,8,256]{2,1,0:T(8,128)(2,1)}), bf16[32,8,256]{2,1,0:T(8,128)(2,1)S(1)}, u32[]{:S(2)}, u32[]{:S(2)}) async-start(bf16[32,8,256]{2,1,0:T(8,128)(2,1)} %bitcast.12), calls=%async_computation.1 | async-start | bytes 262144 | tf_op jit(solution)/shard_map/all_to_all | solution.py:378
  42.1 7.7 %copy-start.1 = (bf16[32,16,128]{2,1,0:T(8,128)(2,1)S(1)}, bf16[32,16,128]{2,1,0:T(8,128)(2,1)}, u32[]{:S(2)}) copy-start(bf16[32,16,128]{2,1,0:T(8,128)(2,1)} %param.10) | copy-start | bytes 393220
  42.1 7.7 %copy-start.3 = (f32[512,128]{1,0:T(8,128)S(1)}, f32[512,128]{1,0:T(8,128)}, u32[]{:S(2)}) copy-start(f32[512,128]{1,0:T(8,128)} %copy-done.2) | copy-start | bytes 786436
  42.1 7.7 %copy-start.4 = (s32[32]{0:T(128)S(1)}, s32[32]{0:T(128)}, u32[]{:S(2)}) copy-start(s32[32]{0:T(128)} %idx_ref.1) | copy-start | bytes 388

commit v3 on v2

v3 whole, which is shorter than its diff:
```python
import jax
import jax.numpy as jnp
from jax import lax
from jax.experimental import pallas as pl
from jax.experimental.pallas import tpu as pltpu
from jax.sharding import PartitionSpec as P

F32 = jnp.float32
BF16 = jnp.bfloat16
I32 = jnp.int32

MODEL_WIDTH = 8192
SEQ = 32
OWNERS = 32
ADAPTERS = 64
RANK = 16
HELD_PARTS = ((0, 256), (256, 256))
HELD = 512
PIECES = ((512, 256), (768, 256))
SLAB = 2048
HALF = SLAB // 2
DEPTH = 4 * SLAB
SLOT_ROWS = OWNERS * 8
KV = 2
GROUP = 8
HEAD = 128
CTX = 128
PAIRS = 4
QROWS = SEQ * KV * GROUP
adapter_scale = 0.5
epsilon = 1e-05
NEG = -1e30

VMEM = pl.BlockSpec(memory_space=pltpu.VMEM)
SMEM = pl.BlockSpec(memory_space=pltpu.SMEM)
HBM = pl.BlockSpec(memory_space=pltpu.MemorySpace.HBM)
NT = (((1,), (1,)), ((), ()))


def iota(shape, dim):
    return lax.broadcasted_iota(I32, shape, dim)


def ones_where(cond):
    return jnp.where(cond, 1.0, 0.0).astype(BF16)


def spread_ids(idx_ref, shape, dim):
    place = iota(shape, dim) & (SEQ - 1)
    out = jnp.zeros(shape, I32)
    for t in range(SEQ):
        out = jnp.where(place == t, idx_ref[t], out)
    return out


def call(kernel, out_shape, in_specs, scratch=(), out_specs=None, limit=16, cost=None):
    return pl.pallas_call(
        kernel,
        out_shape=out_shape,
        in_specs=in_specs,
        out_specs=out_specs if out_specs is not None else jax.tree.map(lambda _: VMEM, out_shape),
        scratch_shapes=list(scratch),
        compiler_params=pltpu.CompilerParams(vmem_limit_bytes=limit << 20),
        cost_estimate=cost,
    )


def in_hbm(*arrays):
    return [pltpu.with_memory_space_constraint(a, pltpu.MemorySpace.HBM) for a in arrays]


def slots_kernel(idx_hbm, h_hbm, out_hbm, idx_ref, h_ref, out_ref, sem, out_sem):
    rows_copy = pltpu.make_async_copy(h_hbm, h_ref, sem.at[0])
    ids_copy = pltpu.make_async_copy(idx_hbm, idx_ref, sem.at[1])
    ids_copy.start()
    rows_copy.start()
    ids_copy.wait()
    shape = (SEQ, 2 * SEQ)
    along = spread_ids(idx_ref, shape, 1)
    down = spread_ids(idx_ref, shape, 0)
    lane = iota(shape, 1)
    earlier = ((along >> 6) == (down >> 6)) & (iota(shape, 0) < (lane & (SEQ - 1)))
    place = jnp.sum(earlier.astype(I32), axis=0, keepdims=True)
    target = (along[0:1] >> 6) * 8 + place + 4 * (lane[0:1] >> 5)
    hot = ones_where(iota((SLOT_ROWS, 2 * SEQ), 0) == target)
    local = spread_ids(idx_ref, (2 * SEQ, 128), 0) & (ADAPTERS - 1)
    mark = ones_where(iota((2 * SEQ, 128), 1) == 2 * local + (iota((2 * SEQ, 128), 0) >> 5))
    out_ref[:, HALF:] = jnp.dot(hot, mark, preferred_element_type=F32).astype(BF16)
    rows_copy.wait()
    rows = jnp.concatenate([h_ref[:, :HALF], h_ref[:, HALF:]], axis=0)
    copies = []
    for n in range(4):
        part = slice(SLOT_ROWS // 4 * n, SLOT_ROWS // 4 * (n + 1))
        out_ref[part, :HALF] = jnp.dot(hot[part], rows, preferred_element_type=F32).astype(BF16)
        copies.append(pltpu.make_async_copy(out_ref.at[part], out_hbm.at[part], out_sem.at[n]))
        copies[n].start()
    for copy in copies:
        copy.wait()


def down_kernel(r_ref, held_ref, d_hbm, t_ref, d_ref, sem):
    copies = []
    for n, (start, count) in enumerate(PIECES):
        rows = pl.ds(start - HELD, count)
        copies.append(
            pltpu.make_async_copy(d_hbm.at[pl.ds(start, count)], d_ref.at[rows], sem.at[n])
        )
        copies[n].start()
    marks = r_ref[:, HALF:]
    pick = ones_where((iota((ADAPTERS, 128), 1) >> 1) == iota((ADAPTERS, 128), 0))
    chosen = lax.dot_general(pick, marks, NT, preferred_element_type=F32)
    rows = r_ref[:, :HALF]

    def product(part, start, count):
        first = ((iota((count, SLOT_ROWS), 1) >> 2) & 1) == 0
        g0 = lax.dot_general(part[:, :HALF], rows, NT, preferred_element_type=F32)
        g1 = lax.dot_general(part[:, HALF:], rows, NT, preferred_element_type=F32)
        g = jnp.where(first, g0, g1).reshape(count // RANK, RANK, SLOT_ROWS)
        mine = chosen[start // RANK : (start + count) // RANK]
        return jnp.sum(g * mine[:, None, :], axis=0)

    total = jnp.zeros((RANK, SLOT_ROWS), F32)
    for start, count in HELD_PARTS:
        total += product(held_ref.at[pl.ds(start, count)], start, count)
    for n, (start, count) in enumerate(PIECES):
        copies[n].wait()
        total += product(d_ref.at[pl.ds(start - HELD, count)], start, count)
    first = ((iota((RANK, SLOT_ROWS), 1) >> 2) & 1) == 0
    ahead = pltpu.roll(total, SLOT_ROWS - 4, 1)
    behind = pltpu.roll(total, 4, 1)
    t_ref[...] = total + jnp.where(first, ahead, behind)


def up_kernel(a_ref, b_ref, m_ref, u_ref, z_ref):
    latent = (a_ref[...] + b_ref[...]).astype(BF16).astype(F32)
    turned = jnp.transpose(latent).astype(BF16)
    repeat = ones_where(((iota((RANK, 256), 1) >> 1) & (RANK - 1)) == iota((RANK, 256), 0))
    wide = jnp.dot(turned, repeat, preferred_element_type=F32).astype(BF16)
    total = jnp.zeros((SLOT_ROWS, KV * HEAD), F32)
    for k in range(8):
        part = slice(256 * k, 256 * (k + 1))
        right = jnp.concatenate([u_ref[c, part, :] for c in range(KV)], axis=1)
        total += jnp.dot(wide * m_ref[:, part], right, preferred_element_type=F32)
    z_ref[...] = total.astype(BF16)


def returned_rows(idx_ref, hot_ref):
    shape = (2 * SEQ, SEQ)
    along = spread_ids(idx_ref, shape, 1)
    down = spread_ids(idx_ref, shape, 0)
    row = iota(shape, 0)
    earlier = ((along >> 6) == (down >> 6)) & (iota(shape, 1) < (row & (SEQ - 1)))
    place = jnp.sum(earlier.astype(I32), axis=1, keepdims=True)
    target = (down[:, 0:1] >> 6) * 8 + place + 4 * (row[:, 0:1] >> 5)
    hot_ref[...] = ones_where(iota((2 * SEQ, SLOT_ROWS), 1) == target)
def query_tokens(lift_ref):
    lift_row = iota((QROWS, 2 * SEQ), 0)
    lift_ref[...] = ones_where(
        iota((QROWS, 2 * SEQ), 1) == ((lift_row >> 3) & 1) * SEQ + (lift_row >> 4)
    )


def inverse_rms(shards):
    squares = jnp.zeros((SEQ, 128), F32)
    for shard in shards:
        for i in range(SLAB // 128):
            wide = shard[:, 128 * i : 128 * (i + 1)].astype(F32)
            squares += wide * wide
    mean = jnp.sum(squares, axis=1, keepdims=True) / MODEL_WIDTH
    return jnp.broadcast_to(lax.rsqrt(mean + epsilon), (SEQ, 128))


def start_weights(tp_ref, steps, w_ref, buf, sem):
    me = tp_ref[0]
    copies = []
    for n, s in enumerate(steps):
        for k in range(2):
            start = pl.multiple_of(((me + s) & 3) * DEPTH + k * (DEPTH // 2), DEPTH // 2)
            place = 2 * n + k
            copies.append(
                pltpu.make_async_copy(
                    w_ref.at[pl.ds(start, DEPTH // 2)], buf.at[place], sem.at[place]
                )
            )
            copies[place].start()
    return copies


def base_part(shards, inverse, copies, buf, left_ref):
    place = iota((SEQ, 512), 1) & 3
    spread = ones_where((iota((128, 512), 1) >> 2) == iota((128, 512), 0))
    total = jnp.zeros((4 * SEQ, HEAD), F32)
    for n, shard in enumerate(shards):
        blocks = [shard[:, 128 * i : 128 * (i + 1)] for i in range(SLAB // 128)]
        if inverse is not None:
            blocks = [(block.astype(F32) * inverse).astype(BF16) for block in blocks]
        wide = jnp.dot(jnp.concatenate(blocks, axis=0), spread, preferred_element_type=F32)
        for i in range(SLAB // 128):
            one = wide[SEQ * i : SEQ * (i + 1)]
            for k in range(4):
                left_ref[SEQ * k : SEQ * (k + 1), 512 * i : 512 * (i + 1)] = jnp.where(
                    place == k, one, 0.0
                ).astype(BF16)
        for k in range(2):
            copies[2 * n + k].wait()
            total += jnp.dot(
                left_ref[:, DEPTH // 2 * k : DEPTH // 2 * (k + 1)],
                buf[2 * n + k],
                preferred_element_type=F32,
            )
    return total


def attend_kernel(
    tp_ref, len_hbm, idx_hbm, q_hbm, k_hbm, v_hbm, h_hbm, d_ref, w_ref,
    mid_hbm, lse_hbm, hot_ref, d0_ref, base_ref,
    len_ref, idx_ref, q_ref, k_ref, v_ref, h_ref, s_ref, mid_ref, lse_ref, buf, left_ref,
    sem, in_sem, w_sem,
):
    inputs = [
        pltpu.make_async_copy(source, target, in_sem.at[n])
        for n, (source, target) in enumerate(
            ((len_hbm, len_ref), (idx_hbm, idx_ref), (q_hbm, q_ref), (k_hbm, k_ref), (v_hbm, v_ref), (h_hbm, h_ref))
        )
    ]
    for copy in inputs:
        copy.start()
    down_copy = pltpu.make_async_copy(d_ref.at[pl.ds(0, HELD)], d0_ref, sem.at[0])
    weights = start_weights(tp_ref, (0,), w_ref, buf, w_sem)
    down_copy.start()
    inputs[0].wait()
    inputs[1].wait()
    returned_rows(idx_ref, hot_ref)
    scale = HEAD**-0.5
    lane = iota((GROUP, CTX), 1)
    inputs[2].wait()
    inputs[3].wait()
    for g in range(SEQ * KV // PAIRS):
        rows = slice(GROUP * PAIRS * g, GROUP * PAIRS * (g + 1))
        keys = k_ref[PAIRS * g : PAIRS * (g + 1)].reshape(PAIRS * CTX, HEAD)
        s = lax.dot_general(q_ref[rows, :], keys, NT, preferred_element_type=F32) * scale
        for n in range(PAIRS):
            pair = PAIRS * g + n
            own = s[GROUP * n : GROUP * (n + 1), CTX * n : CTX * (n + 1)]
            s_ref[GROUP * pair : GROUP * (pair + 1), :] = jnp.where(
                lane < len_ref[pair // KV], own, NEG
            )
    for part in range(4):
        rows = slice(QROWS // 4 * part, QROWS // 4 * (part + 1))
        s = s_ref[rows, :]
        m = jnp.max(s, axis=1, keepdims=True)
        p = jnp.exp(s - m)
        norm = jnp.broadcast_to(jnp.sum(p, axis=1, keepdims=True), p.shape)
        lse_ref[rows, :] = m + jnp.log(norm)
        s_ref[rows, :] = p / norm
    level_copy = pltpu.make_async_copy(lse_ref, lse_hbm, sem.at[1])
    level_copy.start()
    inputs[4].wait()
    for g in range(SEQ * KV // PAIRS):
        blocks = []
        for n in range(PAIRS):
            pair = PAIRS * g + n
            p = s_ref[GROUP * pair : GROUP * (pair + 1), :]
            zero = jnp.zeros_like(p)
            blocks.append(
                jnp.concatenate([p if k == n else zero for k in range(PAIRS)], axis=1)
            )
        values = v_ref[PAIRS * g : PAIRS * (g + 1)].reshape(PAIRS * CTX, HEAD)
        mid_ref[GROUP * PAIRS * g : GROUP * PAIRS * (g + 1), :] = jnp.dot(
            jnp.concatenate(blocks, axis=0).astype(BF16), values, preferred_element_type=F32
        )
    middle_copy = pltpu.make_async_copy(mid_ref, mid_hbm, sem.at[2])
    middle_copy.start()
    inputs[5].wait()
    base_ref[...] = base_part((h_ref,), None, weights, buf, left_ref)
    for copy in (down_copy, level_copy, middle_copy):
        copy.wait()


def between_kernel(
    tp_ref, r_ref, h0_ref, h1_ref, h2_ref, h3_ref, before_ref, u_ref, w_ref,
    mask_ref, inv_ref, u2_ref, out_ref, buf, left_ref, w_sem, sem,
):
    copies = [
        pltpu.make_async_copy(u_ref.at[:, :, pl.ds(HEAD * c, HEAD)], u2_ref.at[c], sem.at[c])
        for c in range(KV)
    ]
    for copy in copies:
        copy.start()
    weights = start_weights(tp_ref, (1,), w_ref, buf, w_sem)
    q = iota((128, RANK * 128), 1)
    spread = ones_where(iota((128, RANK * 128), 0) == 2 * (q >> 5) + (q & 1))
    mask_ref[...] = jnp.dot(r_ref[:, HALF:], spread, preferred_element_type=F32).astype(BF16)
    inverse = inverse_rms((h0_ref, h1_ref, h2_ref, h3_ref))
    inv_ref[...] = inverse
    total = base_part((h1_ref,), inverse, weights, buf, left_ref)
    for k in range(4):
        rows = slice(SEQ * k, SEQ * (k + 1))
        out_ref[rows, :] = total[rows] + before_ref[rows, :] * inverse
    for copy in copies:
        copy.wait()


def base_kernel(
    tp_ref, h2_ref, h3_ref, inv_ref, before_ref, w_ref,
    out_ref, lift_ref, buf, left_ref, sem,
):
    copies = start_weights(tp_ref, (2, 3), w_ref, buf, sem)
    query_tokens(lift_ref)
    out_ref[...] = before_ref[...] + base_part(
        (h2_ref, h3_ref), inv_ref[...], copies, buf, left_ref
    )


def final_kernel(hot_ref, lift_ref, z_ref, base_ref, inv_ref, q_ref, mid_ref, lse_ref, kv_ref, ctx_ref):
    lift = lift_ref[...]
    delta = jnp.dot(hot_ref[...], z_ref[...], preferred_element_type=F32)
    inverse = inv_ref[...]
    fresh = {}
    for j in range(2):
        for c in range(KV):
            plain = base_ref[SEQ * (2 * c + j) : SEQ * (2 * c + j + 1), :]
            extra = delta[SEQ * j : SEQ * (j + 1), HEAD * c : HEAD * (c + 1)]
            fresh[j, c] = (plain + adapter_scale * inverse * extra).astype(BF16)
            kv_ref[:, j, c, :] = fresh[j, c]
    new_key = jnp.dot(lift, jnp.concatenate([fresh[0, 0], fresh[0, 1]], axis=0), preferred_element_type=F32)
    new_value = jnp.dot(lift, jnp.concatenate([fresh[1, 0], fresh[1, 1]], axis=0), preferred_element_type=F32)
    own = jnp.sum(q_ref[...].astype(F32) * new_key, axis=1, keepdims=True) * (HEAD**-0.5)
    gap = own - lse_ref[...]
    small = jnp.exp(-jnp.abs(gap))
    share = jnp.where(gap > 0, 1.0, small) / (1.0 + small)
    own_weight = share.astype(BF16).astype(F32)
    ctx_ref[...] = (mid_ref[...] * (1.0 - share) + own_weight * new_value).astype(BF16)


def on_device(
    hidden,
    queries,
    key_cache_rows,
    value_cache_rows,
    cache_fill_length,
    adapter_choice_index,
    key_value_weight,
    adapter_down_weight,
    adapter_up_weight,
):
    shape = jax.ShapeDtypeStruct
    owners = lax.axis_size("ad")
    ring = lax.axis_size("tp")

    slots = call(
        slots_kernel,
        shape((SLOT_ROWS, HALF + 128), BF16),
        [HBM, HBM],
        out_specs=HBM,
        scratch=[
            pltpu.SMEM((SEQ,), I32),
            pltpu.VMEM((SEQ, SLAB), BF16),
            pltpu.VMEM((SLOT_ROWS, HALF + 128), BF16),
            pltpu.SemaphoreType.DMA((2,)),
            pltpu.SemaphoreType.DMA((4,)),
        ],
    )(*in_hbm(adapter_choice_index, hidden))
    slots, rows_here, fill = lax.optimization_barrier((slots, hidden, cache_fill_length))
    arrived = lax.all_to_all(
        slots.reshape(owners, 8, HALF + 128), "ad", 0, 0, tiled=True
    ).reshape(SLOT_ROWS, HALF + 128)

    others = [
        lax.ppermute(rows_here, "tp", [(i, (i - s) % ring) for i in range(ring)]) for s in (1, 2, 3)
    ]
    flat_queries = queries.reshape(QROWS, HEAD)
    me = lax.axis_index("tp").astype(I32).reshape(1)
    weight_rows = (
        key_value_weight.reshape(MODEL_WIDTH, 2, KV, HEAD)
        .transpose(0, 2, 1, 3)
        .reshape(4 * MODEL_WIDTH, HEAD)
    )

    def weight_scratch(count):
        return [
            pltpu.VMEM((2 * count, DEPTH // 2, HEAD), BF16),
            pltpu.VMEM((4 * SEQ, DEPTH), BF16),
        ]

    middle, level, hot, down, base = call(
        attend_kernel,
        (
            pltpu.MemorySpace.HBM((QROWS, HEAD), F32),
            pltpu.MemorySpace.HBM((QROWS, CTX), F32),
            shape((2 * SEQ, SLOT_ROWS), BF16),
            pltpu.VMEM((HELD, SLAB), BF16),
            shape((4 * SEQ, HEAD), F32),
        ),
        [SMEM] + [HBM] * 8,
        out_specs=(HBM, HBM, VMEM, VMEM, VMEM),
        scratch=[
            pltpu.SMEM((SEQ,), I32),
            pltpu.SMEM((SEQ,), I32),
            pltpu.VMEM((QROWS, HEAD), BF16),
            pltpu.VMEM((SEQ * KV, CTX, HEAD), BF16),
            pltpu.VMEM((SEQ * KV, CTX, HEAD), BF16),
            pltpu.VMEM((SEQ, SLAB), BF16),
            pltpu.VMEM((QROWS, CTX), F32),
            pltpu.VMEM((QROWS, HEAD), F32),
            pltpu.VMEM((QROWS, CTX), F32),
            *weight_scratch(1),
            pltpu.SemaphoreType.DMA((3,)),
            pltpu.SemaphoreType.DMA((6,)),
            pltpu.SemaphoreType.DMA((2,)),
        ],
        limit=24,
        cost=pl.CostEstimate(flops=1 << 30, transcendentals=1 << 16, bytes_accessed=12 << 20),
    )(
        me,
        *in_hbm(
            fill,
            adapter_choice_index,
            flat_queries,
            key_cache_rows.reshape(SEQ * KV, CTX, HEAD),
            value_cache_rows.reshape(SEQ * KV, CTX, HEAD),
            hidden,
            adapter_down_weight.reshape(ADAPTERS * RANK, SLAB),
            weight_rows,
        ),
    )
    arrived, middle, rows_here = lax.optimization_barrier((arrived, middle, rows_here))
    sums = call(
        down_kernel,
        shape((RANK, SLOT_ROWS), F32),
        [VMEM, VMEM, HBM],
        scratch=[
            pltpu.VMEM((ADAPTERS * RANK - HELD, SLAB), BF16),
            pltpu.SemaphoreType.DMA((len(PIECES),)),
        ],
    )(arrived, down, *in_hbm(adapter_down_weight.reshape(ADAPTERS * RANK, SLAB)))
    sums = sums + lax.ppermute(sums, "tp", [(i, i ^ 1) for i in range(ring)])
    across = lax.ppermute(sums, "tp", [(i, ring - 1 - i) for i in range(ring)])
    mask, inverse, up_halves, base = call(
        between_kernel,
        (
            shape((SLOT_ROWS, RANK * 128), BF16),
            shape((SEQ, 128), F32),
            pltpu.VMEM((KV, ADAPTERS * RANK, 2, HEAD), BF16),
            shape((4 * SEQ, HEAD), F32),
        ),
        [SMEM] + [VMEM] * 6 + [HBM] * 2,
        scratch=[
            *weight_scratch(1),
            pltpu.SemaphoreType.DMA((2,)),
            pltpu.SemaphoreType.DMA((KV,)),
        ],
        limit=24,
    )(
        me,
        arrived,
        hidden,
        *others,
        base,
        *in_hbm(adapter_up_weight.reshape(ADAPTERS * RANK, 2, KV * HEAD), weight_rows),
    )
    corrections = call(up_kernel, shape((SLOT_ROWS, KV * HEAD), BF16), [VMEM] * 4)(
        sums, across, mask, up_halves.reshape(KV, RANK * 128, HEAD)
    )
    returned = lax.all_to_all(
        corrections.reshape(owners, 8, KV * HEAD), "ad", 0, 0, tiled=True
    ).reshape(SLOT_ROWS, KV * HEAD)

    base, lift = call(
        base_kernel,
        (
            shape((4 * SEQ, HEAD), F32),
            shape((QROWS, 2 * SEQ), BF16),
        ),
        [SMEM, VMEM, VMEM, VMEM, VMEM, HBM],
        scratch=[*weight_scratch(2), pltpu.SemaphoreType.DMA((4,))],
        limit=24,
    )(me, *others[1:], inverse, base, *in_hbm(weight_rows))

    entries, context = call(
        final_kernel,
        (shape((SEQ, 2, KV, HEAD), BF16), shape((QROWS, HEAD), BF16)),
        [VMEM] * 8,
    )(hot, lift, returned, base, inverse, flat_queries, middle, level)
    return (
        entries,
        context.reshape(SEQ, KV * GROUP, HEAD),
    )


def solution(mesh):
    placed = (
        P("ad", "tp"),
        P("ad", "tp", None),
        P("ad", "tp", None, None),
        P("ad", "tp", None, None),
        P("ad"),
        P("ad"),
        P(None, None, "tp"),
        P("ad", None, "tp"),
        P("ad", None, None, "tp"),
    )
    return jax.shard_map(
        on_device,
        mesh=mesh,
        in_specs=placed,
        out_specs=(P("ad", None, "tp", None), P("ad", "tp", None)),
        check_vma=False,
    )
```

time: 51.9 us -> 50.9 us (0.981)
  waiting for transfers between devices: 7.53 us -> 9.3 us
  Pallas kernels: 18.9 us -> 17.4 us
  local copies, waits for them, and re-layouts: 0.72 us -> 0.02 us
  starting transfers between devices: 23.7 us -> 23.1 us
    ppermute x3 -> x2, waiting for transfers between devices: 0.01 us -> 1.37 us  [the longest x1 1.37 us: on_device(): sums = sums + lax.ppermute(sums, 'tp', [(i, i ^ 1) for i in range(ring)])]
    unnamed x10 -> x8, local copies, waits for them, and re-layouts: 0.72 us -> 0.02 us
    pallas_call x1, Pallas kernels: 1.81 us -> 1.18 us  [on_device(): call(final_kernel, (shape((SEQ, 2, KV, HEAD), BF16), shape((QROWS, HEAD),...]
    ppermute x3, starting transfers between devices: 4.89 us -> 4.28 us  [on_device(): lax.ppermute(rows_here, 'tp', [(i, (i - s) % ring) for i in range(ring)])]
    ppermute x3 -> x2, starting transfers between devices: 4.29 us -> 3.77 us  [the longest x1 2.48 us: on_device(): across = lax.ppermute(sums, 'tp', [(i, ring - 1 - i) for i in range(ring)])]
    pallas_call x6 -> x5, Pallas kernels: 14.3 us -> 13.9 us  [the longest x1 4.3 us: on_device(): call(attend_kernel, (pltpu.MemorySpace.HBM((QROWS, HEAD), F32), pltpu.Mem...]
  transfers between devices with their start and end apart: 8 -> 7, of which waited for: 2 -> 3; matrix products, arithmetic and copies ran while one was open for 0% -> 0% of each run, Pallas kernels for 26% -> 26%
where the time goes in v3:
time: 50.9 us; the launch traced here: 50.6 us
  starting transfers between devices  23.1 us (45%)
  Pallas kernels  17.4 us (34%)
  waiting for transfers between devices  9.3 us (18%)
  between operations  0.74 us (1%)
    all_to_all x1, starting transfers between devices, on_device(): lax.all_to_all(slots.reshape(owners, 8, HALF + 128), 'ad', 0, 0, tiled=True)  9.61 us
    all_to_all x1, starting transfers between devices, on_device(): lax.all_to_all(corrections.reshape(owners, 8, KV * HEAD), 'ad', 0, 0, til...  5.46 us
    pallas_call x1, Pallas kernels, on_device(): call(attend_kernel, (pltpu.MemorySpace.HBM((QROWS, HEAD), F32), pltpu.Mem...  4.3 us
    ppermute x3, starting transfers between devices, on_device(): lax.ppermute(rows_here, 'tp', [(i, (i - s) % ring) for i in range(ring)])  4.28 us
    all_to_all x1, waiting for transfers between devices, on_device(): lax.all_to_all(corrections.reshape(owners, 8, KV * HEAD), 'ad', 0, 0, til...  4.25 us
    all_to_all x1, waiting for transfers between devices, on_device(): lax.all_to_all(slots.reshape(owners, 8, HALF + 128), 'ad', 0, 0, tiled=True)  3.67 us
    pallas_call x1, Pallas kernels, on_device(): call(base_kernel, (shape((4 * SEQ, HEAD), F32), shape((QROWS, 2 * SEQ), B...  3.45 us
    pallas_call x1, Pallas kernels, on_device(): call(between_kernel, (shape((SLOT_ROWS, RANK * 128), BF16), shape((SEQ, 1...  2.88 us
  transfers between devices with their start and end apart: 7, of which 3 were waited for; matrix products, arithmetic and copies ran while one was open for 0% of the time, Pallas kernels for 26%

profile of v3, /device:TPU:1, one launch (start us, length us, event | category | flops | bytes accessed | tf_op | source)
XLA Modules:
  0.0 50.6 jit_solution(18341673738443944668)
XLA Ops:
  0.6 2.0 %shard_map.104 = bf16[256,1152]{1,0:T(8,128)(2,1)} custom-call(s32[32]{0:T(128)} %idx_hbm.3, bf16[32,2048]{1,0:T(8,128)(2,1)} %h0_ref.1), custom_call_target="tpu_custom_call" | custom-call | tf_op jit(solution)/shard_map/pallas_call | solution.py:351
  2.6 9.6 %all-to-all-start = ((bf16[32,8,1152]{2,1,0:T(8,128)(2,1)}), bf16[32,8,1152]{2,1,0:T(8,128)(2,1)S(1)}, u32[]{:S(2)}, u32[]{:S(2)}) async-start(bf16[32,8,1152]{2,1,0:T(8,128)(2,1)} %bitcast.8), calls=%async_computation | async-start | bytes 1179648 | tf_op jit(solution)/shard_map/all_to_all | solution.py:365
  12.2 2.5 %collective-permute-start.2 = (bf16[32,2048]{1,0:T(8,128)(2,1)}, bf16[32,2048]{1,0:T(8,128)(2,1)S(1)}, u32[]{:S(2)}, u32[]{:S(2)}) collective-permute-start(bf16[32,2048]{1,0:T(8,128)(2,1)} %h0_ref.1), channel_id=1, source_target_pairs={{0,3},{1,0},{2,1},{3,2},{4,7},{5,4},{6,5},{7,6},{8,11},{9,8},{10,9... | collective-permute-start | bytes 393224 | tf_op jit(solution)/shard_map/ppermute | solution.py:370
  14.8 0.0 collective-permute-start.1
  14.8 1.7 %collective-permute-start = (bf16[32,2048]{1,0:T(8,128)(2,1)}, bf16[32,2048]{1,0:T(8,128)(2,1)S(1)}, u32[]{:S(2)}, u32[]{:S(2)}) collective-permute-start(bf16[32,2048]{1,0:T(8,128)(2,1)} %h0_ref.1), channel_id=1, source_target_pairs={{0,2},{1,3},{2,0},{3,1},{4,6},{5,7},{6,4},{7,5},{8,10},{9,11},{10,... | collective-permute-start | bytes 393224 | tf_op jit(solution)/shard_map/ppermute | solution.py:370
  16.5 4.3 %shard_map.105 = (f32[512,128]{1,0:T(8,128)}, f32[512,128]{1,0:T(8,128)}, bf16[64,256]{1,0:T(8,128)(2,1)S(1)}, bf16[512,2048]{1,0:T(8,128)(2,1)S(1)}, f32[128,128]{1,0:T(8,128)S(1)}) custom-call(s32[1]{0:T(128)} %bitcast.tp_ref, s32[32]{0:T(128)} %len_hbm, s32[32]{0:T(128)} %idx_hbm.3, bf16[512,128]{1,0:T(8,128)(2,1)} %bitcast.20, ...), custom_call_target="tpu_custom_call" | custom-call | flops 1073741824 | bytes 12582912 | tf_op jit(solution)/shard_map/pallas_call | solution.py:386
  20.8 3.7 %all-to-all-done = bf16[32,8,1152]{2,1,0:T(8,128)(2,1)S(1)} async-done(((bf16[32,8,1152]{2,1,0:T(8,128)(2,1)}), bf16[32,8,1152]{2,1,0:T(8,128)(2,1)S(1)}, u32[]{:S(2)}, u32[]{:S(2)}) %all-to-all-start) | async-done | bytes 589856 | tf_op jit(solution)/shard_map/all_to_all | solution.py:365
  24.5 0.0 copy-start
  24.5 2.3 %shard_map.108 = f32[16,256]{1,0:T(8,128)S(1)} custom-call(bf16[256,1152]{1,0:T(8,128)(2,1)S(1)} %bitcast.17, bf16[512,2048]{1,0:T(8,128)(2,1)S(1)} %get-tuple-element.30.held_ref, bf16[1024,2048]{1,0:T(8,128)(2,1)} %bitcast.27), custom_call_target="tpu_custom_call" | custom-call | tf_op jit(solution)/shard_map/pallas_call | solution.py:428
  26.8 1.3 %collective-permute-start.3 = (f32[16,256]{1,0:T(8,128)S(1)}, f32[16,256]{1,0:T(8,128)S(1)}, u32[]{:S(2)}, u32[]{:S(2)}) collective-permute-start(f32[16,256]{1,0:T(8,128)S(1)} %shard_map.108), channel_id=1, source_target_pairs={{0,1},{1,0},{2,3},{3,2},{4,5},{5,4},{6,7},{7,6},{8,9},{9,8},{10,11... | collective-permute-start | bytes 49160 | tf_op jit(solution)/shard_map/ppermute | solution.py:437
  28.1 1.4 %collective-permute-done.3 = f32[16,256]{1,0:T(8,128)S(1)} collective-permute-done((f32[16,256]{1,0:T(8,128)S(1)}, f32[16,256]{1,0:T(8,128)S(1)}, u32[]{:S(2)}, u32[]{:S(2)}) %collective-permute-start.3) | collective-permute-done | bytes 16416 | tf_op jit(solution)/shard_map/ppermute | solution.py:437
  29.5 2.5 %collective-permute-start.4 = (f32[16,256]{1,0:T(8,128)S(1)}, f32[16,256]{1,0:T(8,128)S(1)}, u32[]{:S(2)}, u32[]{:S(2)}) collective-permute-start(f32[16,256]{1,0:T(8,128)S(1)} %add.3.a_ref), channel_id=1, source_target_pairs={{0,3},{1,2},{2,1},{3,0},{4,7},{5,6},{6,5},{7,4},{8,11},{9,10},{10,... | collective-permute-start | bytes 49160 | tf_op jit(solution)/shard_map/ppermute | solution.py:438
  32.0 0.0 collective-permute-done.2.h1_ref
  32.0 0.0 collective-permute-done.1.h3_ref
  32.0 0.0 collective-permute-done.h2_ref
  32.0 0.0 copy-done
  32.0 2.9 %shard_map.106 = (bf16[256,2048]{1,0:T(8,128)(2,1)S(1)}, f32[32,128]{1,0:T(8,128)S(1)}, bf16[2,1024,2,128]{3,2,1,0:T(2,128)(2,1)S(1)}, f32[128,128]{1,0:T(8,128)S(1)}) custom-call(s32[1]{0:T(128)} %bitcast.tp_ref, bf16[256,1152]{1,0:T(8,128)(2,1)S(1)} %bitcast.18, bf16[32,2048]{1,0:T(8,128)(2,1)S(1)} %copy-done, ...), custom_call_target="tpu_custom_call" | custom-call | tf_op jit(solution)/shard_map/pallas_call | solution.py:439
  34.9 0.0 collective-permute-done.4.b_ref
  34.9 1.3 %shard_map.109 = bf16[256,256]{1,0:T(8,128)(2,1)} custom-call(f32[16,256]{1,0:T(8,128)S(1)} %add.3.a_ref, f32[16,256]{1,0:T(8,128)S(1)} %collective-permute-done.4.b_ref, bf16[256,2048]{1,0:T(8,128)(2,1)S(1)} %get-tuple-element.31.m_ref, bf16[2,2048,128]{2,1,0:T(8,128)(2,1)S(1)} %bitcast.19), custom_call_target="tpu_custom_call" | custom-call | tf_op jit(solution)/shard_map/pallas_call | solution.py:462
  36.2 5.5 %all-to-all-start.1 = ((bf16[32,8,256]{2,1,0:T(8,128)(2,1)}), bf16[32,8,256]{2,1,0:T(8,128)(2,1)S(1)}, u32[]{:S(2)}, u32[]{:S(2)}) async-start(bf16[32,8,256]{2,1,0:T(8,128)(2,1)} %bitcast.14), calls=%async_computation.1 | async-start | bytes 262144 | tf_op jit(solution)/shard_map/all_to_all | solution.py:465
  41.6 0.0 copy-start.1
  41.7 0.0 copy-start.2
  41.7 0.0 copy-start.3
  41.7 3.5 %shard_map.107 = (f32[128,128]{1,0:T(8,128)S(1)}, bf16[512,64]{1,0:T(8,128)(2,1)S(1)}) custom-call(s32[1]{0:T(128)} %bitcast.tp_ref, bf16[32,2048]{1,0:T(8,128)(2,1)S(1)} %collective-permute-done.h2_ref, bf16[32,2048]{1,0:T(8,128)(2,1)S(1)} %collective-permute-done.1.h3_ref, f32[32,128]{1,0:T(8,128)S(1)} %get-tuple-element.27.inv_ref, ...), custom_call_target="tpu_custom_call" | custom-call | tf_op jit(solution)/shard_map/pallas_call | solution.py:469
  45.1 4.2 %all-to-all-done.1 = bf16[32,8,256]{2,1,0:T(8,128)(2,1)S(1)} async-done(((bf16[32,8,256]{2,1,0:T(8,128)(2,1)}), bf16[32,8,256]{2,1,0:T(8,128)(2,1)S(1)}, u32[]{:S(2)}, u32[]{:S(2)}) %all-to-all-start.1) | async-done | bytes 131104 | tf_op jit(solution)/shard_map/all_to_all | solution.py:465
  49.4 0.0 copy-done.1
  49.4 0.0 copy-done.2
  49.4 0.0 copy-done.3
  49.4 1.2 %shard_map.110 = (bf16[32,2,2,128]{3,2,1,0:T(2,128)(2,1)}, bf16[512,128]{1,0:T(8,128)(2,1)}) custom-call(bf16[64,256]{1,0:T(8,128)(2,1)S(1)} %get-tuple-element.21.hot_ref, bf16[512,64]{1,0:T(8,128)(2,1)S(1)} %get-tuple-element.29.lift_ref, bf16[256,256]{1,0:T(8,128)(2,1)S(1)} %bitcast.22, f32[128,128]{1,0:T(8,128)S(1)} %get-tuple-element.33.base_ref, ...), custom_call_target="tpu_custom_call" | custom-call | tf_op jit(solution)/shard_map/pallas_call | solution.py:480
  (1 shorter events, 0.0 us)
Async XLA Ops:
  2.6 21.9 %all-to-all-start = ((bf16[32,8,1152]{2,1,0:T(8,128)(2,1)}), bf16[32,8,1152]{2,1,0:T(8,128)(2,1)S(1)}, u32[]{:S(2)}, u32[]{:S(2)}) async-start(bf16[32,8,1152]{2,1,0:T(8,128)(2,1)} %bitcast.8), calls=%async_computation | async-start | bytes 1179648 | tf_op jit(solution)/shard_map/all_to_all | solution.py:365
  12.2 19.7 %collective-permute-start.2 = (bf16[32,2048]{1,0:T(8,128)(2,1)}, bf16[32,2048]{1,0:T(8,128)(2,1)S(1)}, u32[]{:S(2)}, u32[]{:S(2)}) collective-permute-start(bf16[32,2048]{1,0:T(8,128)(2,1)} %h0_ref.1), channel_id=1, source_target_pairs={{0,3},{1,0},{2,1},{3,2},{4,7},{5,4},{6,5},{7,6},{8,11},{9,8},{10,9... | collective-permute-start | bytes 393224 | tf_op jit(solution)/shard_map/ppermute | solution.py:370
  14.8 17.2 %collective-permute-start.1 = (bf16[32,2048]{1,0:T(8,128)(2,1)}, bf16[32,2048]{1,0:T(8,128)(2,1)S(1)}, u32[]{:S(2)}, u32[]{:S(2)}) collective-permute-start(bf16[32,2048]{1,0:T(8,128)(2,1)} %h0_ref.1), channel_id=1, source_target_pairs={{0,1},{1,2},{2,3},{3,0},{4,5},{5,6},{6,7},{7,4},{8,9},{9,10},{10,1... | collective-permute-start | bytes 393224 | tf_op jit(solution)/shard_map/ppermute | solution.py:370
  14.8 17.2 %collective-permute-start = (bf16[32,2048]{1,0:T(8,128)(2,1)}, bf16[32,2048]{1,0:T(8,128)(2,1)S(1)}, u32[]{:S(2)}, u32[]{:S(2)}) collective-permute-start(bf16[32,2048]{1,0:T(8,128)(2,1)} %h0_ref.1), channel_id=1, source_target_pairs={{0,2},{1,3},{2,0},{3,1},{4,6},{5,7},{6,4},{7,5},{8,10},{9,11},{10,... | collective-permute-start | bytes 393224 | tf_op jit(solution)/shard_map/ppermute | solution.py:370
  24.5 7.5 %copy-start = (bf16[32,2048]{1,0:T(8,128)(2,1)S(1)}, bf16[32,2048]{1,0:T(8,128)(2,1)}, u32[]{:S(2)}) copy-start(bf16[32,2048]{1,0:T(8,128)(2,1)} %h0_ref.1) | copy-start | bytes 393220
  26.8 2.7 %collective-permute-start.3 = (f32[16,256]{1,0:T(8,128)S(1)}, f32[16,256]{1,0:T(8,128)S(1)}, u32[]{:S(2)}, u32[]{:S(2)}) collective-permute-start(f32[16,256]{1,0:T(8,128)S(1)} %shard_map.108), channel_id=1, source_target_pairs={{0,1},{1,0},{2,3},{3,2},{4,5},{5,4},{6,7},{7,6},{8,9},{9,8},{10,11... | collective-permute-start | bytes 49160 | tf_op jit(solution)/shard_map/ppermute | solution.py:437
  29.5 5.4 %collective-permute-start.4 = (f32[16,256]{1,0:T(8,128)S(1)}, f32[16,256]{1,0:T(8,128)S(1)}, u32[]{:S(2)}, u32[]{:S(2)}) collective-permute-start(f32[16,256]{1,0:T(8,128)S(1)} %add.3.a_ref), channel_id=1, source_target_pairs={{0,3},{1,2},{2,1},{3,0},{4,7},{5,6},{6,5},{7,4},{8,11},{9,10},{10,... | collective-permute-start | bytes 49160 | tf_op jit(solution)/shard_map/ppermute | solution.py:438
  36.2 13.2 %all-to-all-start.1 = ((bf16[32,8,256]{2,1,0:T(8,128)(2,1)}), bf16[32,8,256]{2,1,0:T(8,128)(2,1)S(1)}, u32[]{:S(2)}, u32[]{:S(2)}) async-start(bf16[32,8,256]{2,1,0:T(8,128)(2,1)} %bitcast.14), calls=%async_computation.1 | async-start | bytes 262144 | tf_op jit(solution)/shard_map/all_to_all | solution.py:465
  41.6 7.7 %copy-start.1 = (bf16[32,16,128]{2,1,0:T(8,128)(2,1)S(1)}, bf16[32,16,128]{2,1,0:T(8,128)(2,1)}, u32[]{:S(2)}) copy-start(bf16[32,16,128]{2,1,0:T(8,128)(2,1)} %param.10) | copy-start | bytes 393220
  41.7 7.7 %copy-start.2 = (f32[512,128]{1,0:T(8,128)S(1)}, f32[512,128]{1,0:T(8,128)}, u32[]{:S(2)}) copy-start(f32[512,128]{1,0:T(8,128)} %get-tuple-element.34.mid_ref) | copy-start | bytes 786436
  41.7 7.7 %copy-start.3 = (f32[512,128]{1,0:T(8,128)S(1)}, f32[512,128]{1,0:T(8,128)}, u32[]{:S(2)}) copy-start(f32[512,128]{1,0:T(8,128)} %get-tuple-element.35.lse_ref) | copy-start | bytes 786436

commit v4 on v3

--- a/solution.py
+++ b/solution.py
@@ -434,8 +434,8 @@
             pltpu.SemaphoreType.DMA((len(PIECES),)),
         ],
     )(arrived, down, *in_hbm(adapter_down_weight.reshape(ADAPTERS * RANK, SLAB)))
-    sums = sums + lax.ppermute(sums, "tp", [(i, i ^ 1) for i in range(ring)])
-    across = lax.ppermute(sums, "tp", [(i, ring - 1 - i) for i in range(ring)])
+    sums = sums + lax.ppermute(sums, "tp", [(i, ring - 1 - i) for i in range(ring)])
+    across = lax.ppermute(sums, "tp", [(i, i ^ 1) for i in range(ring)])
     mask, inverse, up_halves, base = call(
         between_kernel,
         (

time: 50.9 us -> 50.6 us (level)
    ppermute x2, starting transfers between devices: 3.77 us -> 2.56 us  [the longest x1 2.56 us: on_device(): lax.ppermute(sums, 'tp', [(i, ring - 1 - i) for i in range(ring)])]
    all_to_all x1, starting transfers between devices: 5.46 us -> 6.51 us  [on_device(): lax.all_to_all(corrections.reshape(owners, 8, KV * HEAD), 'ad', 0, 0, til...]
where the time goes in v4:
time: 50.6 us; the launch traced here: 50.3 us
  starting transfers between devices  23 us (45%)
  Pallas kernels  17.4 us (34%)
  waiting for transfers between devices  9.14 us (18%)
  between operations  0.75 us (1%)
    all_to_all x1, starting transfers between devices, on_device(): lax.all_to_all(slots.reshape(owners, 8, HALF + 128), 'ad', 0, 0, tiled=True)  9.61 us
    all_to_all x1, starting transfers between devices, on_device(): lax.all_to_all(corrections.reshape(owners, 8, KV * HEAD), 'ad', 0, 0, til...  6.51 us
    pallas_call x1, Pallas kernels, on_device(): call(attend_kernel, (pltpu.MemorySpace.HBM((QROWS, HEAD), F32), pltpu.Mem...  4.3 us
    ppermute x3, starting transfers between devices, on_device(): lax.ppermute(rows_here, 'tp', [(i, (i - s) % ring) for i in range(ring)])  4.28 us
    all_to_all x1, waiting for transfers between devices, on_device(): lax.all_to_all(corrections.reshape(owners, 8, KV * HEAD), 'ad', 0, 0, til...  4.14 us
    all_to_all x1, waiting for transfers between devices, on_device(): lax.all_to_all(slots.reshape(owners, 8, HALF + 128), 'ad', 0, 0, tiled=True)  3.67 us
    pallas_call x1, Pallas kernels, on_device(): call(base_kernel, (shape((4 * SEQ, HEAD), F32), shape((QROWS, 2 * SEQ), B...  3.45 us
    pallas_call x1, Pallas kernels, on_device(): call(between_kernel, (shape((SLOT_ROWS, RANK * 128), BF16), shape((SEQ, 1...  2.88 us
  transfers between devices with their start and end apart: 7, of which 3 were waited for; matrix products, arithmetic and copies ran while one was open for 0% of the time, Pallas kernels for 26%

profile of v4, /device:TPU:1, one launch (start us, length us, event | category | flops | bytes accessed | tf_op | source)
XLA Modules:
  0.0 50.3 jit_solution(16606005508400151349)
XLA Ops:
  0.6 2.0 %shard_map.104 = bf16[256,1152]{1,0:T(8,128)(2,1)} custom-call(s32[32]{0:T(128)} %idx_hbm.3, bf16[32,2048]{1,0:T(8,128)(2,1)} %h0_ref.1), custom_call_target="tpu_custom_call" | custom-call | tf_op jit(solution)/shard_map/pallas_call | solution.py:351
  2.6 9.6 %all-to-all-start = ((bf16[32,8,1152]{2,1,0:T(8,128)(2,1)}), bf16[32,8,1152]{2,1,0:T(8,128)(2,1)S(1)}, u32[]{:S(2)}, u32[]{:S(2)}) async-start(bf16[32,8,1152]{2,1,0:T(8,128)(2,1)} %bitcast.8), calls=%async_computation | async-start | bytes 1179648 | tf_op jit(solution)/shard_map/all_to_all | solution.py:365
  12.2 2.5 %collective-permute-start.2 = (bf16[32,2048]{1,0:T(8,128)(2,1)}, bf16[32,2048]{1,0:T(8,128)(2,1)S(1)}, u32[]{:S(2)}, u32[]{:S(2)}) collective-permute-start(bf16[32,2048]{1,0:T(8,128)(2,1)} %h0_ref.1), channel_id=1, source_target_pairs={{0,3},{1,0},{2,1},{3,2},{4,7},{5,4},{6,5},{7,6},{8,11},{9,8},{10,9... | collective-permute-start | bytes 393224 | tf_op jit(solution)/shard_map/ppermute | solution.py:370
  14.8 0.0 collective-permute-start.1
  14.8 1.7 %collective-permute-start = (bf16[32,2048]{1,0:T(8,128)(2,1)}, bf16[32,2048]{1,0:T(8,128)(2,1)S(1)}, u32[]{:S(2)}, u32[]{:S(2)}) collective-permute-start(bf16[32,2048]{1,0:T(8,128)(2,1)} %h0_ref.1), channel_id=1, source_target_pairs={{0,2},{1,3},{2,0},{3,1},{4,6},{5,7},{6,4},{7,5},{8,10},{9,11},{10,... | collective-permute-start | bytes 393224 | tf_op jit(solution)/shard_map/ppermute | solution.py:370
  16.5 4.3 %shard_map.105 = (f32[512,128]{1,0:T(8,128)}, f32[512,128]{1,0:T(8,128)}, bf16[64,256]{1,0:T(8,128)(2,1)S(1)}, bf16[512,2048]{1,0:T(8,128)(2,1)S(1)}, f32[128,128]{1,0:T(8,128)S(1)}) custom-call(s32[1]{0:T(128)} %bitcast.tp_ref, s32[32]{0:T(128)} %len_hbm, s32[32]{0:T(128)} %idx_hbm.3, bf16[512,128]{1,0:T(8,128)(2,1)} %bitcast.20, ...), custom_call_target="tpu_custom_call" | custom-call | flops 1073741824 | bytes 12582912 | tf_op jit(solution)/shard_map/pallas_call | solution.py:386
  20.8 3.7 %all-to-all-done = bf16[32,8,1152]{2,1,0:T(8,128)(2,1)S(1)} async-done(((bf16[32,8,1152]{2,1,0:T(8,128)(2,1)}), bf16[32,8,1152]{2,1,0:T(8,128)(2,1)S(1)}, u32[]{:S(2)}, u32[]{:S(2)}) %all-to-all-start) | async-done | bytes 589856 | tf_op jit(solution)/shard_map/all_to_all | solution.py:365
  24.5 0.0 copy-start
  24.5 2.3 %shard_map.108 = f32[16,256]{1,0:T(8,128)S(1)} custom-call(bf16[256,1152]{1,0:T(8,128)(2,1)S(1)} %bitcast.17, bf16[512,2048]{1,0:T(8,128)(2,1)S(1)} %get-tuple-element.30.held_ref, bf16[1024,2048]{1,0:T(8,128)(2,1)} %bitcast.27), custom_call_target="tpu_custom_call" | custom-call | tf_op jit(solution)/shard_map/pallas_call | solution.py:428
  26.8 2.6 %collective-permute-start.3 = (f32[16,256]{1,0:T(8,128)S(1)}, f32[16,256]{1,0:T(8,128)S(1)}, u32[]{:S(2)}, u32[]{:S(2)}) collective-permute-start(f32[16,256]{1,0:T(8,128)S(1)} %shard_map.108), channel_id=1, source_target_pairs={{0,3},{1,2},{2,1},{3,0},{4,7},{5,6},{6,5},{7,4},{8,11},{9,10},{10,... | collective-permute-start | bytes 49160 | tf_op jit(solution)/shard_map/ppermute | solution.py:437
  29.4 1.3 %collective-permute-done.3 = f32[16,256]{1,0:T(8,128)S(1)} collective-permute-done((f32[16,256]{1,0:T(8,128)S(1)}, f32[16,256]{1,0:T(8,128)S(1)}, u32[]{:S(2)}, u32[]{:S(2)}) %collective-permute-start.3) | collective-permute-done | bytes 16416 | tf_op jit(solution)/shard_map/ppermute | solution.py:437
  30.7 0.0 collective-permute-start.4
  30.7 0.0 collective-permute-done.2.h1_ref
  30.7 0.0 collective-permute-done.1.h3_ref
  30.7 0.0 collective-permute-done.h2_ref
  30.7 0.0 copy-done
  30.7 2.9 %shard_map.106 = (bf16[256,2048]{1,0:T(8,128)(2,1)S(1)}, f32[32,128]{1,0:T(8,128)S(1)}, bf16[2,1024,2,128]{3,2,1,0:T(2,128)(2,1)S(1)}, f32[128,128]{1,0:T(8,128)S(1)}) custom-call(s32[1]{0:T(128)} %bitcast.tp_ref, bf16[256,1152]{1,0:T(8,128)(2,1)S(1)} %bitcast.18, bf16[32,2048]{1,0:T(8,128)(2,1)S(1)} %copy-done, ...), custom_call_target="tpu_custom_call" | custom-call | tf_op jit(solution)/shard_map/pallas_call | solution.py:439
  33.6 0.0 collective-permute-done.4.b_ref
  33.6 1.3 %shard_map.109 = bf16[256,256]{1,0:T(8,128)(2,1)} custom-call(f32[16,256]{1,0:T(8,128)S(1)} %add.3.a_ref, f32[16,256]{1,0:T(8,128)S(1)} %collective-permute-done.4.b_ref, bf16[256,2048]{1,0:T(8,128)(2,1)S(1)} %get-tuple-element.31.m_ref, bf16[2,2048,128]{2,1,0:T(8,128)(2,1)S(1)} %bitcast.19), custom_call_target="tpu_custom_call" | custom-call | tf_op jit(solution)/shard_map/pallas_call | solution.py:462
  34.9 6.5 %all-to-all-start.1 = ((bf16[32,8,256]{2,1,0:T(8,128)(2,1)}), bf16[32,8,256]{2,1,0:T(8,128)(2,1)S(1)}, u32[]{:S(2)}, u32[]{:S(2)}) async-start(bf16[32,8,256]{2,1,0:T(8,128)(2,1)} %bitcast.14), calls=%async_computation.1 | async-start | bytes 262144 | tf_op jit(solution)/shard_map/all_to_all | solution.py:465
  41.5 0.0 copy-start.1
  41.5 0.0 copy-start.2
  41.5 0.0 copy-start.3
  41.5 3.5 %shard_map.107 = (f32[128,128]{1,0:T(8,128)S(1)}, bf16[512,64]{1,0:T(8,128)(2,1)S(1)}) custom-call(s32[1]{0:T(128)} %bitcast.tp_ref, bf16[32,2048]{1,0:T(8,128)(2,1)S(1)} %collective-permute-done.h2_ref, bf16[32,2048]{1,0:T(8,128)(2,1)S(1)} %collective-permute-done.1.h3_ref, f32[32,128]{1,0:T(8,128)S(1)} %get-tuple-element.27.inv_ref, ...), custom_call_target="tpu_custom_call" | custom-call | tf_op jit(solution)/shard_map/pallas_call | solution.py:469
  44.9 4.1 %all-to-all-done.1 = bf16[32,8,256]{2,1,0:T(8,128)(2,1)S(1)} async-done(((bf16[32,8,256]{2,1,0:T(8,128)(2,1)}), bf16[32,8,256]{2,1,0:T(8,128)(2,1)S(1)}, u32[]{:S(2)}, u32[]{:S(2)}) %all-to-all-start.1) | async-done | bytes 131104 | tf_op jit(solution)/shard_map/all_to_all | solution.py:465
  49.1 0.0 copy-done.1
  49.1 0.0 copy-done.2
  49.1 0.0 copy-done.3
  49.1 1.2 %shard_map.110 = (bf16[32,2,2,128]{3,2,1,0:T(2,128)(2,1)}, bf16[512,128]{1,0:T(8,128)(2,1)}) custom-call(bf16[64,256]{1,0:T(8,128)(2,1)S(1)} %get-tuple-element.21.hot_ref, bf16[512,64]{1,0:T(8,128)(2,1)S(1)} %get-tuple-element.29.lift_ref, bf16[256,256]{1,0:T(8,128)(2,1)S(1)} %bitcast.22, f32[128,128]{1,0:T(8,128)S(1)} %get-tuple-element.33.base_ref, ...), custom_call_target="tpu_custom_call" | custom-call | tf_op jit(solution)/shard_map/pallas_call | solution.py:480
  (1 shorter events, 0.0 us)
Async XLA Ops:
  2.6 21.9 %all-to-all-start = ((bf16[32,8,1152]{2,1,0:T(8,128)(2,1)}), bf16[32,8,1152]{2,1,0:T(8,128)(2,1)S(1)}, u32[]{:S(2)}, u32[]{:S(2)}) async-start(bf16[32,8,1152]{2,1,0:T(8,128)(2,1)} %bitcast.8), calls=%async_computation | async-start | bytes 1179648 | tf_op jit(solution)/shard_map/all_to_all | solution.py:365
  12.2 18.5 %collective-permute-start.2 = (bf16[32,2048]{1,0:T(8,128)(2,1)}, bf16[32,2048]{1,0:T(8,128)(2,1)S(1)}, u32[]{:S(2)}, u32[]{:S(2)}) collective-permute-start(bf16[32,2048]{1,0:T(8,128)(2,1)} %h0_ref.1), channel_id=1, source_target_pairs={{0,3},{1,0},{2,1},{3,2},{4,7},{5,4},{6,5},{7,6},{8,11},{9,8},{10,9... | collective-permute-start | bytes 393224 | tf_op jit(solution)/shard_map/ppermute | solution.py:370
  14.8 15.9 %collective-permute-start.1 = (bf16[32,2048]{1,0:T(8,128)(2,1)}, bf16[32,2048]{1,0:T(8,128)(2,1)S(1)}, u32[]{:S(2)}, u32[]{:S(2)}) collective-permute-start(bf16[32,2048]{1,0:T(8,128)(2,1)} %h0_ref.1), channel_id=1, source_target_pairs={{0,1},{1,2},{2,3},{3,0},{4,5},{5,6},{6,7},{7,4},{8,9},{9,10},{10,1... | collective-permute-start | bytes 393224 | tf_op jit(solution)/shard_map/ppermute | solution.py:370
  14.8 16.0 %collective-permute-start = (bf16[32,2048]{1,0:T(8,128)(2,1)}, bf16[32,2048]{1,0:T(8,128)(2,1)S(1)}, u32[]{:S(2)}, u32[]{:S(2)}) collective-permute-start(bf16[32,2048]{1,0:T(8,128)(2,1)} %h0_ref.1), channel_id=1, source_target_pairs={{0,2},{1,3},{2,0},{3,1},{4,6},{5,7},{6,4},{7,5},{8,10},{9,11},{10,... | collective-permute-start | bytes 393224 | tf_op jit(solution)/shard_map/ppermute | solution.py:370
  24.5 6.3 %copy-start = (bf16[32,2048]{1,0:T(8,128)(2,1)S(1)}, bf16[32,2048]{1,0:T(8,128)(2,1)}, u32[]{:S(2)}) copy-start(bf16[32,2048]{1,0:T(8,128)(2,1)} %h0_ref.1) | copy-start | bytes 393220
  26.8 3.9 %collective-permute-start.3 = (f32[16,256]{1,0:T(8,128)S(1)}, f32[16,256]{1,0:T(8,128)S(1)}, u32[]{:S(2)}, u32[]{:S(2)}) collective-permute-start(f32[16,256]{1,0:T(8,128)S(1)} %shard_map.108), channel_id=1, source_target_pairs={{0,3},{1,2},{2,1},{3,0},{4,7},{5,6},{6,5},{7,4},{8,11},{9,10},{10,... | collective-permute-start | bytes 49160 | tf_op jit(solution)/shard_map/ppermute | solution.py:437
  30.7 2.9 %collective-permute-start.4 = (f32[16,256]{1,0:T(8,128)S(1)}, f32[16,256]{1,0:T(8,128)S(1)}, u32[]{:S(2)}, u32[]{:S(2)}) collective-permute-start(f32[16,256]{1,0:T(8,128)S(1)} %add.3.a_ref), channel_id=1, source_target_pairs={{0,1},{1,0},{2,3},{3,2},{4,5},{5,4},{6,7},{7,6},{8,9},{9,8},{10,11... | collective-permute-start | bytes 49160 | tf_op jit(solution)/shard_map/ppermute | solution.py:438
  34.9 14.1 %all-to-all-start.1 = ((bf16[32,8,256]{2,1,0:T(8,128)(2,1)}), bf16[32,8,256]{2,1,0:T(8,128)(2,1)S(1)}, u32[]{:S(2)}, u32[]{:S(2)}) async-start(bf16[32,8,256]{2,1,0:T(8,128)(2,1)} %bitcast.14), calls=%async_computation.1 | async-start | bytes 262144 | tf_op jit(solution)/shard_map/all_to_all | solution.py:465
  41.5 7.6 %copy-start.1 = (bf16[32,16,128]{2,1,0:T(8,128)(2,1)S(1)}, bf16[32,16,128]{2,1,0:T(8,128)(2,1)}, u32[]{:S(2)}) copy-start(bf16[32,16,128]{2,1,0:T(8,128)(2,1)} %param.10) | copy-start | bytes 393220
  41.5 7.6 %copy-start.2 = (f32[512,128]{1,0:T(8,128)S(1)}, f32[512,128]{1,0:T(8,128)}, u32[]{:S(2)}) copy-start(f32[512,128]{1,0:T(8,128)} %get-tuple-element.34.mid_ref) | copy-start | bytes 786436
  41.5 7.6 %copy-start.3 = (f32[512,128]{1,0:T(8,128)S(1)}, f32[512,128]{1,0:T(8,128)}, u32[]{:S(2)}) copy-start(f32[512,128]{1,0:T(8,128)} %get-tuple-element.35.lse_ref) | copy-start | bytes 786436

commit v5 on v4

--- a/solution.py
+++ b/solution.py
@@ -14,9 +14,9 @@
 OWNERS = 32
 ADAPTERS = 64
 RANK = 16
-HELD_PARTS = ((0, 256), (256, 256))
-HELD = 512
-PIECES = ((512, 256), (768, 256))
+HELD_PARTS = ((0, 256), (256, 256), (512, 96))
+HELD = 608
+PIECES = ((608, 416),)
 SLAB = 2048
 HALF = SLAB // 2
 DEPTH = 4 * SLAB
@@ -131,17 +131,24 @@
     t_ref[...] = total + jnp.where(first, ahead, behind)
 
 
-def up_kernel(a_ref, b_ref, m_ref, u_ref, z_ref):
+def up_kernel(a_ref, b_ref, m_ref, u_ref, z_hbm, z_ref, sem):
     latent = (a_ref[...] + b_ref[...]).astype(BF16).astype(F32)
     turned = jnp.transpose(latent).astype(BF16)
     repeat = ones_where(((iota((RANK, 256), 1) >> 1) & (RANK - 1)) == iota((RANK, 256), 0))
     wide = jnp.dot(turned, repeat, preferred_element_type=F32).astype(BF16)
-    total = jnp.zeros((SLOT_ROWS, KV * HEAD), F32)
-    for k in range(8):
-        part = slice(256 * k, 256 * (k + 1))
-        right = jnp.concatenate([u_ref[c, part, :] for c in range(KV)], axis=1)
-        total += jnp.dot(wide * m_ref[:, part], right, preferred_element_type=F32)
-    z_ref[...] = total.astype(BF16)
+    copies = []
+    for n in range(2):
+        rows = slice(SLOT_ROWS // 2 * n, SLOT_ROWS // 2 * (n + 1))
+        total = jnp.zeros((SLOT_ROWS // 2, KV * HEAD), F32)
+        for k in range(8):
+            part = slice(256 * k, 256 * (k + 1))
+            right = jnp.concatenate([u_ref[c, part, :] for c in range(KV)], axis=1)
+            total += jnp.dot(wide[rows] * m_ref[rows, part], right, preferred_element_type=F32)
+        z_ref[rows, :] = total.astype(BF16)
+        copies.append(pltpu.make_async_copy(z_ref.at[rows], z_hbm.at[rows], sem.at[n]))
+        copies[n].start()
+    for copy in copies:
+        copy.wait()
 
 
 def returned_rows(idx_ref, hot_ref):
@@ -213,8 +220,8 @@
 
 def attend_kernel(
     tp_ref, len_hbm, idx_hbm, q_hbm, k_hbm, v_hbm, h_hbm, d_ref, w_ref,
-    mid_hbm, lse_hbm, hot_ref, d0_ref, base_ref,
-    len_ref, idx_ref, q_ref, k_ref, v_ref, h_ref, s_ref, mid_ref, lse_ref, buf, left_ref,
+    mid_hbm, lse_hbm, hot_hbm, d0_ref, base_ref,
+    len_ref, idx_ref, q_ref, k_ref, v_ref, h_ref, s_ref, mid_ref, lse_ref, hot_ref, buf, left_ref,
     sem, in_sem, w_sem,
 ):
     inputs = [
@@ -231,6 +238,8 @@
     inputs[0].wait()
     inputs[1].wait()
     returned_rows(idx_ref, hot_ref)
+    hot_copy = pltpu.make_async_copy(hot_ref, hot_hbm, sem.at[3])
+    hot_copy.start()
     scale = HEAD**-0.5
     lane = iota((GROUP, CTX), 1)
     inputs[2].wait()
@@ -273,7 +282,7 @@
     middle_copy.start()
     inputs[5].wait()
     base_ref[...] = base_part((h_ref,), None, weights, buf, left_ref)
-    for copy in (down_copy, level_copy, middle_copy):
+    for copy in (down_copy, level_copy, middle_copy, hot_copy):
         copy.wait()
 
 
@@ -388,12 +397,12 @@
         (
             pltpu.MemorySpace.HBM((QROWS, HEAD), F32),
             pltpu.MemorySpace.HBM((QROWS, CTX), F32),
-            shape((2 * SEQ, SLOT_ROWS), BF16),
+            pltpu.MemorySpace.HBM((2 * SEQ, SLOT_ROWS), BF16),
             pltpu.VMEM((HELD, SLAB), BF16),
             shape((4 * SEQ, HEAD), F32),
         ),
         [SMEM] + [HBM] * 8,
-        out_specs=(HBM, HBM, VMEM, VMEM, VMEM),
+        out_specs=(HBM, HBM, HBM, VMEM, VMEM),
         scratch=[
             pltpu.SMEM((SEQ,), I32),
             pltpu.SMEM((SEQ,), I32),
@@ -404,8 +413,9 @@
             pltpu.VMEM((QROWS, CTX), F32),
             pltpu.VMEM((QROWS, HEAD), F32),
             pltpu.VMEM((QROWS, CTX), F32),
+            pltpu.VMEM((2 * SEQ, SLOT_ROWS), BF16),
             *weight_scratch(1),
-            pltpu.SemaphoreType.DMA((3,)),
+            pltpu.SemaphoreType.DMA((4,)),
             pltpu.SemaphoreType.DMA((6,)),
             pltpu.SemaphoreType.DMA((2,)),
         ],
@@ -459,7 +469,13 @@
         base,
         *in_hbm(adapter_up_weight.reshape(ADAPTERS * RANK, 2, KV * HEAD), weight_rows),
     )
-    corrections = call(up_kernel, shape((SLOT_ROWS, KV * HEAD), BF16), [VMEM] * 4)(
+    corrections = call(
+        up_kernel,
+        shape((SLOT_ROWS, KV * HEAD), BF16),
+        [VMEM] * 4,
+        out_specs=HBM,
+        scratch=[pltpu.VMEM((SLOT_ROWS, KV * HEAD), BF16), pltpu.SemaphoreType.DMA((2,))],
+    )(
         sums, across, mask, up_halves.reshape(KV, RANK * 128, HEAD)
     )
     returned = lax.all_to_all(

time: 50.6 us -> 50.6 us (level)
  no operation moved by 1% of the time
where the time goes in v5:
time: 50.6 us; the launch traced here: 50.2 us
  starting transfers between devices  23 us (45%)
  Pallas kernels  17.3 us (34%)
  waiting for transfers between devices  9.11 us (18%)
  between operations  0.78 us (2%)
    all_to_all x1, starting transfers between devices, on_device(): lax.all_to_all(slots.reshape(owners, 8, HALF + 128), 'ad', 0, 0, tiled=True)  9.61 us
    all_to_all x1, starting transfers between devices, on_device(): lax.all_to_all(corrections.reshape(owners, 8, KV * HEAD), 'ad', 0, 0, til...  6.53 us
    pallas_call x1, Pallas kernels, on_device(): call(attend_kernel, (pltpu.MemorySpace.HBM((QROWS, HEAD), F32), pltpu.Mem...  4.3 us
    ppermute x3, starting transfers between devices, on_device(): lax.ppermute(rows_here, 'tp', [(i, (i - s) % ring) for i in range(ring)])  4.28 us
    all_to_all x1, waiting for transfers between devices, on_device(): lax.all_to_all(corrections.reshape(owners, 8, KV * HEAD), 'ad', 0, 0, til...  4.12 us
    all_to_all x1, waiting for transfers between devices, on_device(): lax.all_to_all(slots.reshape(owners, 8, HALF + 128), 'ad', 0, 0, tiled=True)  3.66 us
    pallas_call x1, Pallas kernels, on_device(): call(base_kernel, (shape((4 * SEQ, HEAD), F32), shape((QROWS, 2 * SEQ), B...  3.45 us
    pallas_call x1, Pallas kernels, on_device(): call(between_kernel, (shape((SLOT_ROWS, RANK * 128), BF16), shape((SEQ, 1...  2.88 us
  transfers between devices with their start and end apart: 7, of which 3 were waited for; matrix products, arithmetic and copies ran while one was open for 0% of the time, Pallas kernels for 26%

profile of v5, /device:TPU:1, one launch (start us, length us, event | category | flops | bytes accessed | tf_op | source)
XLA Modules:
  0.0 50.2 jit_solution(2831968882668438131)
XLA Ops:
  0.6 2.0 %shard_map.104 = bf16[256,1152]{1,0:T(8,128)(2,1)} custom-call(s32[32]{0:T(128)} %idx_hbm.3, bf16[32,2048]{1,0:T(8,128)(2,1)} %h0_ref.1), custom_call_target="tpu_custom_call" | custom-call | tf_op jit(solution)/shard_map/pallas_call | solution.py:360
  2.6 9.6 %all-to-all-start = ((bf16[32,8,1152]{2,1,0:T(8,128)(2,1)}), bf16[32,8,1152]{2,1,0:T(8,128)(2,1)S(1)}, u32[]{:S(2)}, u32[]{:S(2)}) async-start(bf16[32,8,1152]{2,1,0:T(8,128)(2,1)} %bitcast.8), calls=%async_computation | async-start | bytes 1179648 | tf_op jit(solution)/shard_map/all_to_all | solution.py:374
  12.2 2.5 %collective-permute-start.2 = (bf16[32,2048]{1,0:T(8,128)(2,1)}, bf16[32,2048]{1,0:T(8,128)(2,1)S(1)}, u32[]{:S(2)}, u32[]{:S(2)}) collective-permute-start(bf16[32,2048]{1,0:T(8,128)(2,1)} %h0_ref.1), channel_id=1, source_target_pairs={{0,3},{1,0},{2,1},{3,2},{4,7},{5,4},{6,5},{7,6},{8,11},{9,8},{10,9... | collective-permute-start | bytes 393224 | tf_op jit(solution)/shard_map/ppermute | solution.py:379
  14.8 0.0 collective-permute-start.1
  14.8 1.7 %collective-permute-start = (bf16[32,2048]{1,0:T(8,128)(2,1)}, bf16[32,2048]{1,0:T(8,128)(2,1)S(1)}, u32[]{:S(2)}, u32[]{:S(2)}) collective-permute-start(bf16[32,2048]{1,0:T(8,128)(2,1)} %h0_ref.1), channel_id=1, source_target_pairs={{0,2},{1,3},{2,0},{3,1},{4,6},{5,7},{6,4},{7,5},{8,10},{9,11},{10,... | collective-permute-start | bytes 393224 | tf_op jit(solution)/shard_map/ppermute | solution.py:379
  16.5 4.3 %shard_map.105 = (f32[512,128]{1,0:T(8,128)}, f32[512,128]{1,0:T(8,128)}, bf16[64,256]{1,0:T(8,128)(2,1)}, bf16[608,2048]{1,0:T(8,128)(2,1)S(1)}, f32[128,128]{1,0:T(8,128)S(1)}) custom-call(s32[1]{0:T(128)} %bitcast.tp_ref, s32[32]{0:T(128)} %len_hbm, s32[32]{0:T(128)} %idx_hbm.3, bf16[512,128]{1,0:T(8,128)(2,1)} %bitcast.20, ...), custom_call_target="tpu_custom_call" | custom-call | flops 1073741824 | bytes 12582912 | tf_op jit(solution)/shard_map/pallas_call | solution.py:395
  20.8 3.7 %all-to-all-done = bf16[32,8,1152]{2,1,0:T(8,128)(2,1)S(1)} async-done(((bf16[32,8,1152]{2,1,0:T(8,128)(2,1)}), bf16[32,8,1152]{2,1,0:T(8,128)(2,1)S(1)}, u32[]{:S(2)}, u32[]{:S(2)}) %all-to-all-start) | async-done | bytes 589856 | tf_op jit(solution)/shard_map/all_to_all | solution.py:374
  24.5 0.0 copy-start
  24.5 2.3 %shard_map.108 = f32[16,256]{1,0:T(8,128)S(1)} custom-call(bf16[256,1152]{1,0:T(8,128)(2,1)S(1)} %bitcast.17, bf16[608,2048]{1,0:T(8,128)(2,1)S(1)} %get-tuple-element.30.held_ref, bf16[1024,2048]{1,0:T(8,128)(2,1)} %bitcast.27), custom_call_target="tpu_custom_call" | custom-call | tf_op jit(solution)/shard_map/pallas_call | solution.py:438
  26.7 2.6 %collective-permute-start.3 = (f32[16,256]{1,0:T(8,128)S(1)}, f32[16,256]{1,0:T(8,128)S(1)}, u32[]{:S(2)}, u32[]{:S(2)}) collective-permute-start(f32[16,256]{1,0:T(8,128)S(1)} %shard_map.108), channel_id=1, source_target_pairs={{0,3},{1,2},{2,1},{3,0},{4,7},{5,6},{6,5},{7,4},{8,11},{9,10},{10,... | collective-permute-start | bytes 49160 | tf_op jit(solution)/shard_map/ppermute | solution.py:447
  29.3 1.3 %collective-permute-done.3 = f32[16,256]{1,0:T(8,128)S(1)} collective-permute-done((f32[16,256]{1,0:T(8,128)S(1)}, f32[16,256]{1,0:T(8,128)S(1)}, u32[]{:S(2)}, u32[]{:S(2)}) %collective-permute-start.3) | collective-permute-done | bytes 16416 | tf_op jit(solution)/shard_map/ppermute | solution.py:447
  30.6 0.0 collective-permute-start.4
  30.6 0.0 collective-permute-done.2.h1_ref
  30.6 0.0 collective-permute-done.1.h3_ref
  30.7 0.0 collective-permute-done.h2_ref
  30.7 0.0 copy-done
  30.7 2.9 %shard_map.106 = (bf16[256,2048]{1,0:T(8,128)(2,1)S(1)}, f32[32,128]{1,0:T(8,128)S(1)}, bf16[2,1024,2,128]{3,2,1,0:T(2,128)(2,1)S(1)}, f32[128,128]{1,0:T(8,128)S(1)}) custom-call(s32[1]{0:T(128)} %bitcast.tp_ref, bf16[256,1152]{1,0:T(8,128)(2,1)S(1)} %bitcast.18, bf16[32,2048]{1,0:T(8,128)(2,1)S(1)} %copy-done, ...), custom_call_target="tpu_custom_call" | custom-call | tf_op jit(solution)/shard_map/pallas_call | solution.py:449
  33.6 0.0 collective-permute-done.4.b_ref
  33.6 1.3 %shard_map.109 = bf16[256,256]{1,0:T(8,128)(2,1)} custom-call(f32[16,256]{1,0:T(8,128)S(1)} %add.3.a_ref, f32[16,256]{1,0:T(8,128)S(1)} %collective-permute-done.4.b_ref, bf16[256,2048]{1,0:T(8,128)(2,1)S(1)} %get-tuple-element.31.m_ref, bf16[2,2048,128]{2,1,0:T(8,128)(2,1)S(1)} %bitcast.19), custom_call_target="tpu_custom_call" | custom-call | tf_op jit(solution)/shard_map/pallas_call | solution.py:472
  34.9 6.5 %all-to-all-start.1 = ((bf16[32,8,256]{2,1,0:T(8,128)(2,1)}), bf16[32,8,256]{2,1,0:T(8,128)(2,1)S(1)}, u32[]{:S(2)}, u32[]{:S(2)}) async-start(bf16[32,8,256]{2,1,0:T(8,128)(2,1)} %bitcast.14), calls=%async_computation.1 | async-start | bytes 262144 | tf_op jit(solution)/shard_map/all_to_all | solution.py:481
  41.4 0.0 copy-start.1
  41.4 0.0 copy-start.2
  41.4 0.0 copy-start.3
  41.4 0.0 copy-start.4
  41.4 3.5 %shard_map.107 = (f32[128,128]{1,0:T(8,128)S(1)}, bf16[512,64]{1,0:T(8,128)(2,1)S(1)}) custom-call(s32[1]{0:T(128)} %bitcast.tp_ref, bf16[32,2048]{1,0:T(8,128)(2,1)S(1)} %collective-permute-done.h2_ref, bf16[32,2048]{1,0:T(8,128)(2,1)S(1)} %collective-permute-done.1.h3_ref, f32[32,128]{1,0:T(8,128)S(1)} %get-tuple-element.27.inv_ref, ...), custom_call_target="tpu_custom_call" | custom-call | tf_op jit(solution)/shard_map/pallas_call | solution.py:485
  44.9 4.1 %all-to-all-done.1 = bf16[32,8,256]{2,1,0:T(8,128)(2,1)S(1)} async-done(((bf16[32,8,256]{2,1,0:T(8,128)(2,1)}), bf16[32,8,256]{2,1,0:T(8,128)(2,1)S(1)}, u32[]{:S(2)}, u32[]{:S(2)}) %all-to-all-start.1) | async-done | bytes 131104 | tf_op jit(solution)/shard_map/all_to_all | solution.py:481
  49.0 0.0 copy-done.1
  49.0 0.0 copy-done.2
  49.0 0.0 copy-done.3
  49.0 0.0 copy-done.4
  49.0 1.2 %shard_map.110 = (bf16[32,2,2,128]{3,2,1,0:T(2,128)(2,1)}, bf16[512,128]{1,0:T(8,128)(2,1)}) custom-call(bf16[64,256]{1,0:T(8,128)(2,1)S(1)} %copy-done.4, bf16[512,64]{1,0:T(8,128)(2,1)S(1)} %get-tuple-element.29.lift_ref, bf16[256,256]{1,0:T(8,128)(2,1)S(1)} %bitcast.22, f32[128,128]{1,0:T(8,128)S(1)} %get-tuple-element.33.base_ref, ...), custom_call_target="tpu_custom_call" | custom-call | tf_op jit(solution)/shard_map/pallas_call | solution.py:496
  (1 shorter events, 0.0 us)
Async XLA Ops:
  2.6 21.9 %all-to-all-start = ((bf16[32,8,1152]{2,1,0:T(8,128)(2,1)}), bf16[32,8,1152]{2,1,0:T(8,128)(2,1)S(1)}, u32[]{:S(2)}, u32[]{:S(2)}) async-start(bf16[32,8,1152]{2,1,0:T(8,128)(2,1)} %bitcast.8), calls=%async_computation | async-start | bytes 1179648 | tf_op jit(solution)/shard_map/all_to_all | solution.py:374
  12.2 18.4 %collective-permute-start.2 = (bf16[32,2048]{1,0:T(8,128)(2,1)}, bf16[32,2048]{1,0:T(8,128)(2,1)S(1)}, u32[]{:S(2)}, u32[]{:S(2)}) collective-permute-start(bf16[32,2048]{1,0:T(8,128)(2,1)} %h0_ref.1), channel_id=1, source_target_pairs={{0,3},{1,0},{2,1},{3,2},{4,7},{5,4},{6,5},{7,6},{8,11},{9,8},{10,9... | collective-permute-start | bytes 393224 | tf_op jit(solution)/shard_map/ppermute | solution.py:379
  14.8 15.9 %collective-permute-start.1 = (bf16[32,2048]{1,0:T(8,128)(2,1)}, bf16[32,2048]{1,0:T(8,128)(2,1)S(1)}, u32[]{:S(2)}, u32[]{:S(2)}) collective-permute-start(bf16[32,2048]{1,0:T(8,128)(2,1)} %h0_ref.1), channel_id=1, source_target_pairs={{0,1},{1,2},{2,3},{3,0},{4,5},{5,6},{6,7},{7,4},{8,9},{9,10},{10,1... | collective-permute-start | bytes 393224 | tf_op jit(solution)/shard_map/ppermute | solution.py:379
  14.8 15.9 %collective-permute-start = (bf16[32,2048]{1,0:T(8,128)(2,1)}, bf16[32,2048]{1,0:T(8,128)(2,1)S(1)}, u32[]{:S(2)}, u32[]{:S(2)}) collective-permute-start(bf16[32,2048]{1,0:T(8,128)(2,1)} %h0_ref.1), channel_id=1, source_target_pairs={{0,2},{1,3},{2,0},{3,1},{4,6},{5,7},{6,4},{7,5},{8,10},{9,11},{10,... | collective-permute-start | bytes 393224 | tf_op jit(solution)/shard_map/ppermute | solution.py:379
  24.5 6.2 %copy-start = (bf16[32,2048]{1,0:T(8,128)(2,1)S(1)}, bf16[32,2048]{1,0:T(8,128)(2,1)}, u32[]{:S(2)}) copy-start(bf16[32,2048]{1,0:T(8,128)(2,1)} %h0_ref.1) | copy-start | bytes 393220
  26.7 3.9 %collective-permute-start.3 = (f32[16,256]{1,0:T(8,128)S(1)}, f32[16,256]{1,0:T(8,128)S(1)}, u32[]{:S(2)}, u32[]{:S(2)}) collective-permute-start(f32[16,256]{1,0:T(8,128)S(1)} %shard_map.108), channel_id=1, source_target_pairs={{0,3},{1,2},{2,1},{3,0},{4,7},{5,6},{6,5},{7,4},{8,11},{9,10},{10,... | collective-permute-start | bytes 49160 | tf_op jit(solution)/shard_map/ppermute | solution.py:447
  30.6 2.9 %collective-permute-start.4 = (f32[16,256]{1,0:T(8,128)S(1)}, f32[16,256]{1,0:T(8,128)S(1)}, u32[]{:S(2)}, u32[]{:S(2)}) collective-permute-start(f32[16,256]{1,0:T(8,128)S(1)} %add.3.a_ref), channel_id=1, source_target_pairs={{0,1},{1,0},{2,3},{3,2},{4,5},{5,4},{6,7},{7,6},{8,9},{9,8},{10,11... | collective-permute-start | bytes 49160 | tf_op jit(solution)/shard_map/ppermute | solution.py:448
  34.9 14.2 %all-to-all-start.1 = ((bf16[32,8,256]{2,1,0:T(8,128)(2,1)}), bf16[32,8,256]{2,1,0:T(8,128)(2,1)S(1)}, u32[]{:S(2)}, u32[]{:S(2)}) async-start(bf16[32,8,256]{2,1,0:T(8,128)(2,1)} %bitcast.14), calls=%async_computation.1 | async-start | bytes 262144 | tf_op jit(solution)/shard_map/all_to_all | solution.py:481
  41.4 7.6 %copy-start.1 = (bf16[32,16,128]{2,1,0:T(8,128)(2,1)S(1)}, bf16[32,16,128]{2,1,0:T(8,128)(2,1)}, u32[]{:S(2)}) copy-start(bf16[32,16,128]{2,1,0:T(8,128)(2,1)} %param.10) | copy-start | bytes 393220
  41.4 7.6 %copy-start.2 = (f32[512,128]{1,0:T(8,128)S(1)}, f32[512,128]{1,0:T(8,128)}, u32[]{:S(2)}) copy-start(f32[512,128]{1,0:T(8,128)} %get-tuple-element.34.mid_ref) | copy-start | bytes 786436
  41.4 7.6 %copy-start.3 = (f32[512,128]{1,0:T(8,128)S(1)}, f32[512,128]{1,0:T(8,128)}, u32[]{:S(2)}) copy-start(f32[512,128]{1,0:T(8,128)} %get-tuple-element.35.lse_ref) | copy-start | bytes 786436
  41.4 7.6 %copy-start.4 = (bf16[64,256]{1,0:T(8,128)(2,1)S(1)}, bf16[64,256]{1,0:T(8,128)(2,1)}, u32[]{:S(2)}) copy-start(bf16[64,256]{1,0:T(8,128)(2,1)} %get-tuple-element.21.hot_ref) | copy-start | bytes 98308

commit v6 on v4

--- a/solution.py
+++ b/solution.py
@@ -277,28 +277,31 @@
         copy.wait()
 
 
-def between_kernel(
-    tp_ref, r_ref, h0_ref, h1_ref, h2_ref, h3_ref, before_ref, u_ref, w_ref,
-    mask_ref, inv_ref, u2_ref, out_ref, buf, left_ref, w_sem, sem,
-):
+def mask_kernel(r_ref, u_ref, mask_ref, u2_ref, sem):
     copies = [
         pltpu.make_async_copy(u_ref.at[:, :, pl.ds(HEAD * c, HEAD)], u2_ref.at[c], sem.at[c])
         for c in range(KV)
     ]
     for copy in copies:
         copy.start()
-    weights = start_weights(tp_ref, (1,), w_ref, buf, w_sem)
     q = iota((128, RANK * 128), 1)
     spread = ones_where(iota((128, RANK * 128), 0) == 2 * (q >> 5) + (q & 1))
     mask_ref[...] = jnp.dot(r_ref[:, HALF:], spread, preferred_element_type=F32).astype(BF16)
+    for copy in copies:
+        copy.wait()
+
+
+def base_second_kernel(
+    tp_ref, h0_ref, h1_ref, h2_ref, h3_ref, before_ref, w_ref,
+    inv_ref, out_ref, buf, left_ref, sem,
+):
+    weights = start_weights(tp_ref, (1,), w_ref, buf, sem)
     inverse = inverse_rms((h0_ref, h1_ref, h2_ref, h3_ref))
     inv_ref[...] = inverse
     total = base_part((h1_ref,), inverse, weights, buf, left_ref)
     for k in range(4):
         rows = slice(SEQ * k, SEQ * (k + 1))
         out_ref[rows, :] = total[rows] + before_ref[rows, :] * inverse
-    for copy in copies:
-        copy.wait()
 
 
 def base_kernel(
@@ -434,31 +437,29 @@
             pltpu.SemaphoreType.DMA((len(PIECES),)),
         ],
     )(arrived, down, *in_hbm(adapter_down_weight.reshape(ADAPTERS * RANK, SLAB)))
-    sums = sums + lax.ppermute(sums, "tp", [(i, ring - 1 - i) for i in range(ring)])
-    across = lax.ppermute(sums, "tp", [(i, i ^ 1) for i in range(ring)])
-    mask, inverse, up_halves, base = call(
-        between_kernel,
+    partner = lax.ppermute(sums, "tp", [(i, ring - 1 - i) for i in range(ring)])
+    rows_in, kept = lax.optimization_barrier((arrived, sums))
+    mask, up_halves = call(
+        mask_kernel,
         (
             shape((SLOT_ROWS, RANK * 128), BF16),
-            shape((SEQ, 128), F32),
             pltpu.VMEM((KV, ADAPTERS * RANK, 2, HEAD), BF16),
-            shape((4 * SEQ, HEAD), F32),
         ),
-        [SMEM] + [VMEM] * 6 + [HBM] * 2,
-        scratch=[
-            *weight_scratch(1),
-            pltpu.SemaphoreType.DMA((2,)),
-            pltpu.SemaphoreType.DMA((KV,)),
-        ],
+        [VMEM, HBM],
+        scratch=[pltpu.SemaphoreType.DMA((KV,))],
+    )(rows_in, *in_hbm(adapter_up_weight.reshape(ADAPTERS * RANK, 2, KV * HEAD)))
+    partner, mask = lax.optimization_barrier((partner, mask))
+    sums = kept + partner
+    across = lax.ppermute(sums, "tp", [(i, i ^ 1) for i in range(ring)])
+    sums, base = lax.optimization_barrier((sums, base))
+    inverse, base = call(
+        base_second_kernel,
+        (shape((SEQ, 128), F32), shape((4 * SEQ, HEAD), F32)),
+        [SMEM] + [VMEM] * 5 + [HBM],
+        scratch=[*weight_scratch(1), pltpu.SemaphoreType.DMA((2,))],
         limit=24,
-    )(
-        me,
-        arrived,
-        hidden,
-        *others,
-        base,
-        *in_hbm(adapter_up_weight.reshape(ADAPTERS * RANK, 2, KV * HEAD), weight_rows),
-    )
+    )(me, hidden, *others, base, *in_hbm(weight_rows))
+    across, base = lax.optimization_barrier((across, base))
     corrections = call(up_kernel, shape((SLOT_ROWS, KV * HEAD), BF16), [VMEM] * 4)(
         sums, across, mask, up_halves.reshape(KV, RANK * 128, HEAD)
     )

time: 50.6 us -> 50.7 us (level)
  waiting for transfers between devices: 9.14 us -> 7.97 us
  Pallas kernels: 17.4 us -> 18.3 us
    ppermute x1, waiting for transfers between devices: 1.32 us -> 0.01 us  [on_device(): partner = lax.ppermute(sums, 'tp', [(i, ring - 1 - i) for i in range(ring)])]
    pallas_call x1 -> x2, Pallas kernels: 2.88 us -> 3.82 us  [the longest x1 2.38 us: on_device(): call(base_second_kernel, (shape((SEQ, 128), F32), shape((4 * SEQ, HEAD),...]
  transfers between devices with their start and end apart: 7 -> 7, of which waited for: 3 -> 3; matrix products, arithmetic and copies ran while one was open for 0% -> 0% of each run, Pallas kernels for 26% -> 28%
where the time goes in v6:
time: 50.7 us; the launch traced here: 50.3 us
  starting transfers between devices  23.2 us (46%)
  Pallas kernels  18.3 us (36%)
  waiting for transfers between devices  7.97 us (16%)
  between operations  0.78 us (2%)
    all_to_all x1, starting transfers between devices, on_device(): lax.all_to_all(slots.reshape(owners, 8, HALF + 128), 'ad', 0, 0, tiled=True)  9.61 us
    all_to_all x1, starting transfers between devices, on_device(): lax.all_to_all(corrections.reshape(owners, 8, KV * HEAD), 'ad', 0, 0, til...  6.64 us
    pallas_call x1, Pallas kernels, on_device(): call(attend_kernel, (pltpu.MemorySpace.HBM((QROWS, HEAD), F32), pltpu.Mem...  4.29 us
    ppermute x3, starting transfers between devices, on_device(): lax.ppermute(rows_here, 'tp', [(i, (i - s) % ring) for i in range(ring)])  4.28 us
    all_to_all x1, waiting for transfers between devices, on_device(): lax.all_to_all(corrections.reshape(owners, 8, KV * HEAD), 'ad', 0, 0, til...  4.14 us
    all_to_all x1, waiting for transfers between devices, on_device(): lax.all_to_all(slots.reshape(owners, 8, HALF + 128), 'ad', 0, 0, tiled=True)  3.67 us
    pallas_call x1, Pallas kernels, on_device(): call(base_kernel, (shape((4 * SEQ, HEAD), F32), shape((QROWS, 2 * SEQ), B...  3.45 us
    ppermute x1, starting transfers between devices, on_device(): partner = lax.ppermute(sums, 'tp', [(i, ring - 1 - i) for i in range(ring)])  2.56 us
  transfers between devices with their start and end apart: 7, of which 3 were waited for; matrix products, arithmetic and copies ran while one was open for 0% of the time, Pallas kernels for 28%

profile of v6, /device:TPU:1, one launch (start us, length us, event | category | flops | bytes accessed | tf_op | source)
XLA Modules:
  0.0 50.3 jit_solution(16449814141806582524)
XLA Ops:
  0.6 2.0 %shard_map.104 = bf16[256,1152]{1,0:T(8,128)(2,1)} custom-call(s32[32]{0:T(128)} %idx_hbm.3, bf16[32,2048]{1,0:T(8,128)(2,1)} %h0_ref.1), custom_call_target="tpu_custom_call" | custom-call | tf_op jit(solution)/shard_map/pallas_call | solution.py:354
  2.6 9.6 %all-to-all-start = ((bf16[32,8,1152]{2,1,0:T(8,128)(2,1)}), bf16[32,8,1152]{2,1,0:T(8,128)(2,1)S(1)}, u32[]{:S(2)}, u32[]{:S(2)}) async-start(bf16[32,8,1152]{2,1,0:T(8,128)(2,1)} %bitcast.8), calls=%async_computation | async-start | bytes 1179648 | tf_op jit(solution)/shard_map/all_to_all | solution.py:368
  12.2 2.5 %collective-permute-start.2 = (bf16[32,2048]{1,0:T(8,128)(2,1)}, bf16[32,2048]{1,0:T(8,128)(2,1)S(1)}, u32[]{:S(2)}, u32[]{:S(2)}) collective-permute-start(bf16[32,2048]{1,0:T(8,128)(2,1)} %h0_ref.1), channel_id=1, source_target_pairs={{0,3},{1,0},{2,1},{3,2},{4,7},{5,4},{6,5},{7,6},{8,11},{9,8},{10,9... | collective-permute-start | bytes 393224 | tf_op jit(solution)/shard_map/ppermute | solution.py:373
  14.8 0.0 collective-permute-start.1
  14.8 1.7 %collective-permute-start = (bf16[32,2048]{1,0:T(8,128)(2,1)}, bf16[32,2048]{1,0:T(8,128)(2,1)S(1)}, u32[]{:S(2)}, u32[]{:S(2)}) collective-permute-start(bf16[32,2048]{1,0:T(8,128)(2,1)} %h0_ref.1), channel_id=1, source_target_pairs={{0,2},{1,3},{2,0},{3,1},{4,6},{5,7},{6,4},{7,5},{8,10},{9,11},{10,... | collective-permute-start | bytes 393224 | tf_op jit(solution)/shard_map/ppermute | solution.py:373
  16.5 4.3 %shard_map.105 = (f32[512,128]{1,0:T(8,128)}, f32[512,128]{1,0:T(8,128)}, bf16[64,256]{1,0:T(8,128)(2,1)S(1)}, bf16[512,2048]{1,0:T(8,128)(2,1)S(1)}, f32[128,128]{1,0:T(8,128)S(1)}) custom-call(s32[1]{0:T(128)} %bitcast.tp_ref, s32[32]{0:T(128)} %len_hbm, s32[32]{0:T(128)} %idx_hbm.3, bf16[512,128]{1,0:T(8,128)(2,1)} %bitcast.20, ...), custom_call_target="tpu_custom_call" | custom-call | flops 1073741824 | bytes 12582912 | tf_op jit(solution)/shard_map/pallas_call | solution.py:389
  20.8 3.7 %all-to-all-done = bf16[32,8,1152]{2,1,0:T(8,128)(2,1)S(1)} async-done(((bf16[32,8,1152]{2,1,0:T(8,128)(2,1)}), bf16[32,8,1152]{2,1,0:T(8,128)(2,1)S(1)}, u32[]{:S(2)}, u32[]{:S(2)}) %all-to-all-start) | async-done | bytes 589856 | tf_op jit(solution)/shard_map/all_to_all | solution.py:368
  24.5 0.0 copy-start
  24.5 2.3 %shard_map.106 = f32[16,256]{1,0:T(8,128)S(1)} custom-call(bf16[256,1152]{1,0:T(8,128)(2,1)S(1)} %bitcast.17, bf16[512,2048]{1,0:T(8,128)(2,1)S(1)} %get-tuple-element.34.held_ref, bf16[1024,2048]{1,0:T(8,128)(2,1)} %bitcast.27), custom_call_target="tpu_custom_call" | custom-call | tf_op jit(solution)/shard_map/pallas_call | solution.py:431
  26.8 2.6 %collective-permute-start.3 = (f32[16,256]{1,0:T(8,128)S(1)}, f32[16,256]{1,0:T(8,128)S(1)}, u32[]{:S(2)}, u32[]{:S(2)}) collective-permute-start(f32[16,256]{1,0:T(8,128)S(1)} %shard_map.106), channel_id=1, source_target_pairs={{0,3},{1,2},{2,1},{3,0},{4,7},{5,6},{6,5},{7,4},{8,11},{9,10},{10,... | collective-permute-start | bytes 49160 | tf_op jit(solution)/shard_map/ppermute | solution.py:440
  29.4 1.4 %shard_map.107 = (bf16[256,2048]{1,0:T(8,128)(2,1)S(1)}, bf16[2,1024,2,128]{3,2,1,0:T(2,128)(2,1)S(1)}) custom-call(bf16[256,1152]{1,0:T(8,128)(2,1)S(1)} %bitcast.18, bf16[1024,2,256]{2,1,0:T(2,128)(2,1)} %bitcast.30), custom_call_target="tpu_custom_call" | custom-call | tf_op jit(solution)/shard_map/pallas_call | solution.py:442
  30.8 0.0 collective-permute-done.3
  30.9 0.1 collective-permute-start.4
  30.9 0.0 collective-permute-done.2.h1_ref
  31.0 0.0 collective-permute-done.1.h3_ref
  31.0 0.0 collective-permute-done.h2_ref
  31.0 0.0 copy-done
  31.0 2.4 %shard_map.108 = (f32[32,128]{1,0:T(8,128)S(1)}, f32[128,128]{1,0:T(8,128)S(1)}) custom-call(s32[1]{0:T(128)} %bitcast.tp_ref, bf16[32,2048]{1,0:T(8,128)(2,1)S(1)} %copy-done, bf16[32,2048]{1,0:T(8,128)(2,1)S(1)} %collective-permute-done.2.h1_ref, bf16[32,2048]{1,0:T(8,128)(2,1)S(1)} %collective-permute-done.h2_ref, ...), custom_call_target="tpu_custom_call" | custom-call | tf_op jit(solution)/shard_map/pallas_call | solution.py:455
  33.4 0.1 collective-permute-done.4.b_ref
  33.5 1.3 %shard_map.110 = bf16[256,256]{1,0:T(8,128)(2,1)} custom-call(f32[16,256]{1,0:T(8,128)S(1)} %add.3.a_ref, f32[16,256]{1,0:T(8,128)S(1)} %collective-permute-done.4.b_ref, bf16[256,2048]{1,0:T(8,128)(2,1)S(1)} %get-tuple-element.47.m_ref, bf16[2,2048,128]{2,1,0:T(8,128)(2,1)S(1)} %bitcast.19), custom_call_target="tpu_custom_call" | custom-call | tf_op jit(solution)/shard_map/pallas_call | solution.py:463
  34.8 6.6 %all-to-all-start.1 = ((bf16[32,8,256]{2,1,0:T(8,128)(2,1)}), bf16[32,8,256]{2,1,0:T(8,128)(2,1)S(1)}, u32[]{:S(2)}, u32[]{:S(2)}) async-start(bf16[32,8,256]{2,1,0:T(8,128)(2,1)} %bitcast.14), calls=%async_computation.1 | async-start | bytes 262144 | tf_op jit(solution)/shard_map/all_to_all | solution.py:466
  41.5 0.0 copy-start.1
  41.5 0.0 copy-start.2
  41.5 0.0 copy-start.3
  41.5 3.5 %shard_map.109 = (f32[128,128]{1,0:T(8,128)S(1)}, bf16[512,64]{1,0:T(8,128)(2,1)S(1)}) custom-call(s32[1]{0:T(128)} %bitcast.tp_ref, bf16[32,2048]{1,0:T(8,128)(2,1)S(1)} %collective-permute-done.h2_ref, bf16[32,2048]{1,0:T(8,128)(2,1)S(1)} %collective-permute-done.1.h3_ref, f32[32,128]{1,0:T(8,128)S(1)} %get-tuple-element.41.inv_ref, ...), custom_call_target="tpu_custom_call" | custom-call | tf_op jit(solution)/shard_map/pallas_call | solution.py:470
  45.0 4.1 %all-to-all-done.1 = bf16[32,8,256]{2,1,0:T(8,128)(2,1)S(1)} async-done(((bf16[32,8,256]{2,1,0:T(8,128)(2,1)}), bf16[32,8,256]{2,1,0:T(8,128)(2,1)S(1)}, u32[]{:S(2)}, u32[]{:S(2)}) %all-to-all-start.1) | async-done | bytes 131104 | tf_op jit(solution)/shard_map/all_to_all | solution.py:466
  49.1 0.0 copy-done.1
  49.1 0.0 copy-done.2
  49.1 0.0 copy-done.3
  49.1 1.2 %shard_map.111 = (bf16[32,2,2,128]{3,2,1,0:T(2,128)(2,1)}, bf16[512,128]{1,0:T(8,128)(2,1)}) custom-call(bf16[64,256]{1,0:T(8,128)(2,1)S(1)} %get-tuple-element.29.hot_ref, bf16[512,64]{1,0:T(8,128)(2,1)S(1)} %get-tuple-element.44.lift_ref, bf16[256,256]{1,0:T(8,128)(2,1)S(1)} %bitcast.22, f32[128,128]{1,0:T(8,128)S(1)} %get-tuple-element.49.base_ref, ...), custom_call_target="tpu_custom_call" | custom-call | tf_op jit(solution)/shard_map/pallas_call | solution.py:481
  (1 shorter events, 0.0 us)
Async XLA Ops:
  2.6 21.9 %all-to-all-start = ((bf16[32,8,1152]{2,1,0:T(8,128)(2,1)}), bf16[32,8,1152]{2,1,0:T(8,128)(2,1)S(1)}, u32[]{:S(2)}, u32[]{:S(2)}) async-start(bf16[32,8,1152]{2,1,0:T(8,128)(2,1)} %bitcast.8), calls=%async_computation | async-start | bytes 1179648 | tf_op jit(solution)/shard_map/all_to_all | solution.py:368
  12.2 18.7 %collective-permute-start.2 = (bf16[32,2048]{1,0:T(8,128)(2,1)}, bf16[32,2048]{1,0:T(8,128)(2,1)S(1)}, u32[]{:S(2)}, u32[]{:S(2)}) collective-permute-start(bf16[32,2048]{1,0:T(8,128)(2,1)} %h0_ref.1), channel_id=1, source_target_pairs={{0,3},{1,0},{2,1},{3,2},{4,7},{5,4},{6,5},{7,6},{8,11},{9,8},{10,9... | collective-permute-start | bytes 393224 | tf_op jit(solution)/shard_map/ppermute | solution.py:373
  14.8 16.2 %collective-permute-start.1 = (bf16[32,2048]{1,0:T(8,128)(2,1)}, bf16[32,2048]{1,0:T(8,128)(2,1)S(1)}, u32[]{:S(2)}, u32[]{:S(2)}) collective-permute-start(bf16[32,2048]{1,0:T(8,128)(2,1)} %h0_ref.1), channel_id=1, source_target_pairs={{0,1},{1,2},{2,3},{3,0},{4,5},{5,6},{6,7},{7,4},{8,9},{9,10},{10,1... | collective-permute-start | bytes 393224 | tf_op jit(solution)/shard_map/ppermute | solution.py:373
  14.8 16.2 %collective-permute-start = (bf16[32,2048]{1,0:T(8,128)(2,1)}, bf16[32,2048]{1,0:T(8,128)(2,1)S(1)}, u32[]{:S(2)}, u32[]{:S(2)}) collective-permute-start(bf16[32,2048]{1,0:T(8,128)(2,1)} %h0_ref.1), channel_id=1, source_target_pairs={{0,2},{1,3},{2,0},{3,1},{4,6},{5,7},{6,4},{7,5},{8,10},{9,11},{10,... | collective-permute-start | bytes 393224 | tf_op jit(solution)/shard_map/ppermute | solution.py:373
  24.5 6.5 %copy-start = (bf16[32,2048]{1,0:T(8,128)(2,1)S(1)}, bf16[32,2048]{1,0:T(8,128)(2,1)}, u32[]{:S(2)}) copy-start(bf16[32,2048]{1,0:T(8,128)(2,1)} %h0_ref.1) | copy-start | bytes 393220
  26.8 4.0 %collective-permute-start.3 = (f32[16,256]{1,0:T(8,128)S(1)}, f32[16,256]{1,0:T(8,128)S(1)}, u32[]{:S(2)}, u32[]{:S(2)}) collective-permute-start(f32[16,256]{1,0:T(8,128)S(1)} %shard_map.106), channel_id=1, source_target_pairs={{0,3},{1,2},{2,1},{3,0},{4,7},{5,6},{6,5},{7,4},{8,11},{9,10},{10,... | collective-permute-start | bytes 49160 | tf_op jit(solution)/shard_map/ppermute | solution.py:440
  30.9 2.7 %collective-permute-start.4 = (f32[16,256]{1,0:T(8,128)S(1)}, f32[16,256]{1,0:T(8,128)S(1)}, u32[]{:S(2)}, u32[]{:S(2)}) collective-permute-start(f32[16,256]{1,0:T(8,128)S(1)} %add.3.a_ref), channel_id=1, source_target_pairs={{0,1},{1,0},{2,3},{3,2},{4,5},{5,4},{6,7},{7,6},{8,9},{9,8},{10,11... | collective-permute-start | bytes 49160 | tf_op jit(solution)/shard_map/ppermute | solution.py:453
  34.8 14.3 %all-to-all-start.1 = ((bf16[32,8,256]{2,1,0:T(8,128)(2,1)}), bf16[32,8,256]{2,1,0:T(8,128)(2,1)S(1)}, u32[]{:S(2)}, u32[]{:S(2)}) async-start(bf16[32,8,256]{2,1,0:T(8,128)(2,1)} %bitcast.14), calls=%async_computation.1 | async-start | bytes 262144 | tf_op jit(solution)/shard_map/all_to_all | solution.py:466
  41.5 7.6 %copy-start.1 = (bf16[32,16,128]{2,1,0:T(8,128)(2,1)S(1)}, bf16[32,16,128]{2,1,0:T(8,128)(2,1)}, u32[]{:S(2)}) copy-start(bf16[32,16,128]{2,1,0:T(8,128)(2,1)} %param.10) | copy-start | bytes 393220
  41.5 7.6 %copy-start.2 = (f32[512,128]{1,0:T(8,128)S(1)}, f32[512,128]{1,0:T(8,128)}, u32[]{:S(2)}) copy-start(f32[512,128]{1,0:T(8,128)} %get-tuple-element.50.mid_ref) | copy-start | bytes 786436
  41.5 7.6 %copy-start.3 = (f32[512,128]{1,0:T(8,128)S(1)}, f32[512,128]{1,0:T(8,128)}, u32[]{:S(2)}) copy-start(f32[512,128]{1,0:T(8,128)} %get-tuple-element.51.lse_ref) | copy-start | bytes 786436
